TPU v7x, 512 devices: a whole 4x4x16 slice. The times are simulated.
512 devices in a mesh: region: 16 (over z), slab: 32 (over x, y, core).
Axes of the slice: x: 4, y: 4, z: 16, core: 2. Of those that a mesh axis runs over, the one named last changes fastest.
Arguments:
- records: bfloat16 [16384, 4096], P('region', 'slab'), may hold values from -6 to 6
- first_station: int32 [65536], P(('region', 'slab')), may hold values from 0 to 1023
- second_region: int32 [65536, 1], P(('region', 'slab')), may hold values from 0 to 15; in each aligned block of 128 rows (0 to 127, 128 to 255, ...) at most 16 rows name the same one
- second_station: int32 [65536], P(('region', 'slab')), may hold values from 0 to 1023
Outputs:
- stacks: bfloat16 [65536, 2048], P(('region', 'slab'))
Inputs may be any that keep to these rules, and one draw needn't show every extreme that they name: `second_region`: no region is named by more than 16 pairs of one device.
All inputs are finite; a program needn't handle non-finite values.
Results may differ from a plain program's by a relative error of at most 0.0077.
Values may be sent and summed in bfloat16 or wider, within the bound.
A program may use at most 64 MiB of HBM per device.

v0:
```python
import math

import jax
import jax.numpy as jnp
from jax import lax
from jax.sharding import PartitionSpec as P

NFFT = 2048
BINS = 1024
SEG = 2
HALF = 4


def dft_table():
    sample = jnp.arange(NFFT, dtype=jnp.int32)[:, None]
    frequency = jnp.arange(BINS, dtype=jnp.int32)[None, :]
    phase = (sample * frequency % NFFT).astype(jnp.float32) * (2.0 * math.pi / NFFT)
    return jnp.concatenate([jnp.cos(phase), -jnp.sin(phase)], axis=1).astype(jnp.bfloat16)


def whitened(traces):
    count = traces.shape[0]
    signal = traces.astype(jnp.float32).reshape(count * SEG, NFFT)
    signal = signal - jnp.mean(signal, axis=1, keepdims=True)
    position = jnp.arange(NFFT, dtype=jnp.int32).astype(jnp.float32)
    taper = 0.5 - 0.5 * jnp.cos(position * (2.0 * math.pi / NFFT))
    tapered = (signal * taper[None, :]).astype(jnp.bfloat16)
    spectrum = jnp.dot(tapered, dft_table(), preferred_element_type=jnp.float32)
    real_part = spectrum[:, :BINS]
    imag_part = spectrum[:, BINS:]
    amplitude = jnp.sqrt(real_part * real_part + imag_part * imag_part + 1e-06)
    padded = jnp.pad(amplitude, ((0, 0), (HALF, HALF)))
    smooth = jnp.zeros_like(amplitude)
    for offset in range(2 * HALF + 1):
        smooth = smooth + padded[:, offset : offset + BINS]
    smooth = smooth / (2 * HALF + 1)
    level = jnp.mean(amplitude, axis=1, keepdims=True)
    divisor = smooth + level + 1e-06
    white = spectrum / jnp.concatenate([divisor, divisor], axis=1)
    return white.astype(jnp.bfloat16).reshape(count, SEG * NFFT)


def cross(first_rows, second_rows):
    left = first_rows.astype(jnp.float32).reshape(first_rows.shape[:-1] + (SEG, 2, BINS))
    right = second_rows.astype(jnp.float32).reshape(second_rows.shape[:-1] + (SEG, 2, BINS))
    real_sum = jnp.mean(
        left[..., 0, :] * right[..., 0, :] + left[..., 1, :] * right[..., 1, :], axis=-2
    )
    imag_sum = jnp.mean(
        left[..., 0, :] * right[..., 1, :] - left[..., 1, :] * right[..., 0, :], axis=-2
    )
    return jnp.concatenate([real_sum, imag_sum], axis=-1).astype(jnp.bfloat16)


def local(records, first_station, second_region, second_station):
    regions = lax.axis_size("region")
    pair_count = first_station.shape[0]
    capacity = max(2, pair_count // regions + pair_count // 16)
    arrived = lax.all_to_all(records, "slab", split_axis=0, concat_axis=1, tiled=True)
    spectra = whitened(arrived)
    width = spectra.shape[1]
    target = second_region[:, 0]
    onehot = (target[:, None] == jnp.arange(regions, dtype=jnp.int32)[None, :]).astype(jnp.int32)
    ranking = jnp.sum((jnp.cumsum(onehot, axis=0) - onehot) * onehot, axis=1)
    slot_index = target * capacity + ranking
    requests = (
        jnp.zeros((regions * capacity,), jnp.int32)
        .at[slot_index]
        .set(second_station)
        .reshape(regions, capacity)
    )
    incoming = lax.all_to_all(requests, "region", split_axis=0, concat_axis=0, tiled=True)
    wanted = jnp.concatenate([first_station, incoming.reshape(-1)])
    initial = jnp.zeros((wanted.shape[0], width), jnp.bfloat16)
    piece = lax.all_gather(spectra, "slab", axis=0, tiled=True)
    inside = (wanted >= 0) & (wanted < piece.shape[0])
    chosen = jnp.take(piece, jnp.clip(wanted, 0, piece.shape[0] - 1), axis=0)
    picked = jnp.where(inside[:, None], chosen, initial)
    first_rows = picked[:pair_count]
    served = picked[pair_count:]
    returned = lax.all_to_all(
        served.reshape(regions, capacity, width), "region", split_axis=0, concat_axis=0, tiled=True
    )
    second_rows = jnp.take(returned.reshape(regions * capacity, width), slot_index, axis=0)
    stacks = cross(first_rows, second_rows)
    return stacks


def solution(mesh):
    placed = (
        P("region", "slab"),
        P(("region", "slab")),
        P(("region", "slab"), None),
        P(("region", "slab")),
    )
    return jax.shard_map(
        local, mesh=mesh, in_specs=placed, out_specs=P(("region", "slab"), None), check_vma=False
    )
```

profile of v0, /device:TPU:1, one launch (start us, length us, event | category | flops | bytes accessed | tf_op | source)
XLA Modules:
  0.0 268.4 jit_solution(3383094113395302440)
XLA Ops:
  6.5 10.4 %all-to-all-start.1 = ((bf16[32,32,128]{2,1,0:T(8,128)(2,1)}), bf16[32,32,128]{2,1,0:T(8,128)(2,1)S(1)}, u32[]{:S(2)}, u32[]{:S(2)}) async-start(bf16[32,32,128]{2,1,0:T(8,128)(2,1)} %bitcast.20), calls=%async_computation.1 | async-start | bytes 524288 | tf_op jit(solution)/shard_map/all_to_all | solution.py:59
  16.9 0.0 all-gather.2.cloned.1.call-start
  17.0 34.9 %negate_convert_fusion = (bf16[2048,1024]{1,0:T(8,128)(2,1)}, bf16[2048,1024]{1,0:T(8,128)(2,1)}) fusion(), kind=kLoop, calls=%fused_computation.13 | loop fusion | flops 35651584 | bytes 8388608 | tf_op jit(solution)/shard_map/convert.6
  51.9 0.1 multiply_subtract_fusion
  52.0 0.0 all-to-all-done.1
  52.0 0.2 convert_reduce_fusion
  52.2 0.1 copy.8
  52.3 0.1 reduce_sum.60
  52.4 0.1 reduce_sum.61
  52.5 0.1 convert_bitcast_fusion
  52.6 0.3 copy.7
  52.9 0.1 reshape.149
  53.0 0.0 copy-start.2
  53.0 0.0 copy-start.3
  53.0 4.4 %fusion.3 = f32[64,2048]{1,0:T(8,128)S(1)} fusion(bf16[2048,1024]{1,0:T(8,128)(2,1)} %get-tuple-element.13, bf16[2048,1024]{1,0:T(8,128)(2,1)} %get-tuple-element.14, f32[64,2048]{1,0:T(8,128)S(1)} %reshape.149, f32[2048]{0:T(1024)S(1)} %multiply_subtract_fusion, f32[64]{0:T(128)S(1)} %broadcast_multiply_fusion.1), kind=kOutput, calls=%fused_computation.9 | convolution fusion | flops 554041344 | bytes 9445632 | tf_op jit(solution)/shard_map/dot_general | solution.py:28
  57.4 0.2 fusion.33
  57.6 0.6 fusion.22
  58.2 0.1 fusion.11
  58.3 0.8 reshape.144
  59.1 0.0 all-gather.2.cloned.1.call-update
  59.1 0.0 copy-done.2
  59.1 0.1 fusion.28
  59.2 0.2 reduce_window_sum.11
  59.4 0.2 select_reduce_fusion
  59.6 1.1 scatter_custom_fusion
  60.7 0.7 all_to_all.19
  61.4 13.1 %all-to-all-start = ((s32[16,1,16]{2,1,0:T(1,128)}), s32[16,1,16]{2,1,0:T(1,128)S(1)}, u32[]{:S(2)}, u32[]{:S(2)}) async-start(s32[16,1,16]{2,1,0:T(1,128)} %all_to_all.19), calls=%async_computation | async-start | bytes 16384 | tf_op jit(solution)/shard_map/all_to_all | solution.py:72
  74.5 0.0 copy-done.3
  74.5 11.2 %all-to-all-done = s32[16,1,16]{2,1,0:T(1,128)S(1)} async-done(((s32[16,1,16]{2,1,0:T(1,128)}), s32[16,1,16]{2,1,0:T(1,128)S(1)}, u32[]{:S(2)}, u32[]{:S(2)}) %all-to-all-start) | async-done | bytes 1056 | tf_op jit(solution)/shard_map/all_to_all | solution.py:72
  85.7 0.1 concatenate.43
  85.8 0.5 broadcast.142
  86.3 0.6 reduce.12
  86.9 0.1 concatenate.38
  87.0 43.1 %all-gather.2.cloned.1.call-done = bf16[1024,4096]{1,0:T(8,128)(2,1)} async-done(((bf16[32,4096]{1,0:T(8,128)(2,1)}), bf16[1024,4096]{1,0:T(8,128)(2,1)}) %all-gather.2.cloned.1.call-update) | async-done | bytes 8388624 | tf_op jit(solution)/shard_map/all_gather | solution.py:75
  130.2 12.0 %gather_fusion = bf16[384,4096]{1,0:T(8,128)(2,1)S(1)} fusion(bf16[1024,4096]{1,0:T(8,128)(2,1)} %all-gather.2.cloned.1.call-done, s32[1024]{0:T(1024)S(1)} %pad_clamp_fusion.1), kind=kCustom, calls=%fused_computation | custom fusion | bytes 6292992 | tf_op jit(solution)/shard_map/jit(_take)/gather | solution.py:77
  142.2 0.5 select_select_fusion
  142.6 0.0 copy-start
  142.6 1.7 copy-done
  144.3 1.5 slice.77
  145.8 12.0 %all-to-all-start.2 = ((bf16[16,16,4096]{2,1,0:T(8,128)(2,1)}), bf16[16,16,4096]{2,1,0:T(8,128)(2,1)S(1)}, u32[]{:S(2)}, u32[]{:S(2)}) async-start(bf16[16,16,4096]{2,1,0:T(8,128)(2,1)} %bitcast.19), calls=%async_computation.2 | async-start | bytes 4194304 | tf_op jit(solution)/shard_map/all_to_all | solution.py:81
  157.8 2.8 %slice_convert_fusion = f32[128,4096]{1,0:T(8,128)} fusion(bf16[384,4096]{1,0:T(8,128)(2,1)} %copy-done), kind=kLoop, calls=%fused_computation.21 | loop fusion | flops 524288 | bytes 3145728 | tf_op jit(solution)/shard_map/reshape | solution.py:44
  160.6 4.0 %reshape.151 = f32[128,2,2,1024]{3,2,1,0:T(2,128)} reshape(f32[128,4096]{1,0:T(8,128)} %slice_convert_fusion) | data formatting | bytes 4194304 | tf_op jit(solution)/shard_map/reshape | solution.py:44
  164.7 85.1 %all-to-all-done.2 = bf16[16,16,4096]{2,1,0:T(8,128)(2,1)S(1)} async-done(((bf16[16,16,4096]{2,1,0:T(8,128)(2,1)}), bf16[16,16,4096]{2,1,0:T(8,128)(2,1)S(1)}, u32[]{:S(2)}, u32[]{:S(2)}) %all-to-all-start.2) | async-done | bytes 2097184 | tf_op jit(solution)/shard_map/all_to_all | solution.py:81
  249.8 1.2 gather_fusion.1
  251.0 0.0 copy-start.1
  251.0 1.6 gather.12
  252.6 2.2 fusion.10
  254.8 0.0 copy-done.1
  254.8 5.8 %add_reduce_fusion = (f32[128,1024]{1,0:T(8,128)S(1)}, f32[128,1024]{1,0:T(8,128)S(1)}) fusion(f32[128,2,2,1024]{3,2,1,0:T(2,128)S(1)} %fusion.10, f32[128,2,2,1024]{3,2,1,0:T(2,128)S(1)} %copy-done.1), kind=kLoop, calls=%fused_computation.23 | loop fusion | flops 1835008 | bytes 5242880 | tf_op jit(solution)/shard_map/reduce_sum | solution.py:46
  260.7 0.8 pad_maximum_fusion
  (12 shorter events, 0.2 us)
Async XLA Ops:
  6.5 45.5 %all-to-all-start.1 = ((bf16[32,32,128]{2,1,0:T(8,128)(2,1)}), bf16[32,32,128]{2,1,0:T(8,128)(2,1)S(1)}, u32[]{:S(2)}, u32[]{:S(2)}) async-start(bf16[32,32,128]{2,1,0:T(8,128)(2,1)} %bitcast.20), calls=%async_computation.1 | async-start | bytes 524288 | tf_op jit(solution)/shard_map/all_to_all | solution.py:59
  16.9 113.2 %all-gather.2.cloned.1.call-start = ((), (), s32[]{:S(2)}) async-start(), calls=%async_computation.3 | async-start | bytes 8650752 | tf_op jit(solution)/shard_map/all_gather | solution.py:75
  53.0 6.2 %copy-start.2 = (s32[128,1]{0,1:T(1,128)S(1)}, s32[128,1]{0,1:T(1,128)}, u32[]{:S(2)}) copy-start(s32[128,1]{0,1:T(1,128)} %param.6) | copy-start | bytes 1540
  53.0 21.5 %copy-start.3 = (s32[128]{0:T(128)S(1)}, s32[128]{0:T(128)}, u32[]{:S(2)}) copy-start(s32[128]{0:T(128)} %param.5) | copy-start | bytes 1540
  61.4 24.4 %all-to-all-start = ((s32[16,1,16]{2,1,0:T(1,128)}), s32[16,1,16]{2,1,0:T(1,128)S(1)}, u32[]{:S(2)}, u32[]{:S(2)}) async-start(s32[16,1,16]{2,1,0:T(1,128)} %all_to_all.19), calls=%async_computation | async-start | bytes 16384 | tf_op jit(solution)/shard_map/all_to_all | solution.py:72
  142.6 1.7 copy-start
  145.8 104.0 %all-to-all-start.2 = ((bf16[16,16,4096]{2,1,0:T(8,128)(2,1)}), bf16[16,16,4096]{2,1,0:T(8,128)(2,1)S(1)}, u32[]{:S(2)}, u32[]{:S(2)}) async-start(bf16[16,16,4096]{2,1,0:T(8,128)(2,1)} %bitcast.19), calls=%async_computation.2 | async-start | bytes 4194304 | tf_op jit(solution)/shard_map/all_to_all | solution.py:81
  251.0 3.8 %copy-start.1 = (f32[128,2,2,1024]{3,2,1,0:T(2,128)S(1)}, f32[128,2,2,1024]{3,2,1,0:T(2,128)}, u32[]{:S(2)}) copy-start(f32[128,2,2,1024]{3,2,1,0:T(2,128)} %reshape.151) | copy-start | bytes 6291460
Sparse Core Ops, SparseCore 0:
  59.2 70.8 all-gather.1
where the time goes:
time: 270 us; the launch traced here: 268 us
  waiting for transfers between devices  139 us (51%)
  other arithmetic  49.5 us (18%)
  starting transfers between devices  35.6 us (13%)
  local copies, waits for them, and re-layouts  25.8 us (10%)
  between operations  13.7 us (5%)
  matrix products  4.41 us (2%)
    all_to_all x1, waiting for transfers between devices, local(): lax.all_to_all(served.reshape(regions, capacity, width), 'region', split_...  85.1 us
    all_gather x1, waiting for transfers between devices, local(): piece = lax.all_gather(spectra, 'slab', axis=0, tiled=True)  43.1 us
    another operation x3, other arithmetic  35 us
    all_to_all x1, starting transfers between devices, local(): lax.all_to_all(requests, 'region', split_axis=0, concat_axis=0, tiled=True)  13.1 us
    all_to_all x1, starting transfers between devices, local(): lax.all_to_all(served.reshape(regions, capacity, width), 'region', split_...  12 us
    gather x1, local copies, waits for them, and re-layouts, local(): chosen = jnp.take(piece, jnp.clip(wanted, 0, piece.shape[0] - 1), axis=0)  12 us
    all_to_all x1, waiting for transfers between devices, local(): lax.all_to_all(requests, 'region', split_axis=0, concat_axis=0, tiled=True)  11.2 us
    all_to_all x1, starting transfers between devices, local(): lax.all_to_all(records, 'slab', split_axis=0, concat_axis=1, tiled=True)  10.4 us
  transfers between devices with their start and end apart: 4, of which 3 were waited for; matrix products, arithmetic and copies ran while one was open for 17% of the time, Pallas kernels for 0%

commit v1 on v0

--- a/solution.py
+++ b/solution.py
@@ -12,10 +12,18 @@
 
 
 def dft_table():
-    sample = jnp.arange(NFFT, dtype=jnp.int32)[:, None]
+    low = 64
+    high = NFFT // low
     frequency = jnp.arange(BINS, dtype=jnp.int32)[None, :]
-    phase = (sample * frequency % NFFT).astype(jnp.float32) * (2.0 * math.pi / NFFT)
-    return jnp.concatenate([jnp.cos(phase), -jnp.sin(phase)], axis=1).astype(jnp.bfloat16)
+    coarse = jnp.arange(high, dtype=jnp.int32)[:, None]
+    fine = jnp.arange(low, dtype=jnp.int32)[:, None]
+    angle_a = ((coarse * frequency) % high).astype(jnp.float32) * (2.0 * math.pi / high)
+    angle_b = ((fine * frequency) % NFFT).astype(jnp.float32) * (2.0 * math.pi / NFFT)
+    ca, sa = jnp.cos(angle_a)[:, None, :], jnp.sin(angle_a)[:, None, :]
+    cb, sb = jnp.cos(angle_b)[None, :, :], jnp.sin(angle_b)[None, :, :]
+    cos_part = (ca * cb - sa * sb).reshape(NFFT, BINS)
+    sin_part = (sa * cb + ca * sb).reshape(NFFT, BINS)
+    return jnp.concatenate([cos_part, -sin_part], axis=1).astype(jnp.bfloat16)
 
 
 def whitened(traces):
@@ -52,13 +60,23 @@
     return jnp.concatenate([real_sum, imag_sum], axis=-1).astype(jnp.bfloat16)
 
 
+def to_rows(parts):
+    slabs, rows, width = parts.shape
+    return jnp.transpose(parts, (1, 0, 2)).reshape(rows, slabs * width)
+
+
 def local(records, first_station, second_region, second_station):
     regions = lax.axis_size("region")
+    slabs = lax.axis_size("slab")
     pair_count = first_station.shape[0]
+    width = records.shape[1]
     capacity = max(2, pair_count // regions + pair_count // 16)
-    arrived = lax.all_to_all(records, "slab", split_axis=0, concat_axis=1, tiled=True)
-    spectra = whitened(arrived)
-    width = spectra.shape[1]
+
+    firsts = lax.all_gather(first_station, "slab", axis=0, tiled=False)
+    first_parts = jnp.take(records, firsts.reshape(-1), axis=0).reshape(slabs, pair_count, width)
+    first_arrived = lax.all_to_all(first_parts, "slab", split_axis=0, concat_axis=0, tiled=True)
+    first_rows = whitened(to_rows(first_arrived))
+
     target = second_region[:, 0]
     onehot = (target[:, None] == jnp.arange(regions, dtype=jnp.int32)[None, :]).astype(jnp.int32)
     ranking = jnp.sum((jnp.cumsum(onehot, axis=0) - onehot) * onehot, axis=1)
@@ -69,21 +87,18 @@
         .set(second_station)
         .reshape(regions, capacity)
     )
-    incoming = lax.all_to_all(requests, "region", split_axis=0, concat_axis=0, tiled=True)
-    wanted = jnp.concatenate([first_station, incoming.reshape(-1)])
-    initial = jnp.zeros((wanted.shape[0], width), jnp.bfloat16)
-    piece = lax.all_gather(spectra, "slab", axis=0, tiled=True)
-    inside = (wanted >= 0) & (wanted < piece.shape[0])
-    chosen = jnp.take(piece, jnp.clip(wanted, 0, piece.shape[0] - 1), axis=0)
-    picked = jnp.where(inside[:, None], chosen, initial)
-    first_rows = picked[:pair_count]
-    served = picked[pair_count:]
-    returned = lax.all_to_all(
-        served.reshape(regions, capacity, width), "region", split_axis=0, concat_axis=0, tiled=True
-    )
-    second_rows = jnp.take(returned.reshape(regions * capacity, width), slot_index, axis=0)
-    stacks = cross(first_rows, second_rows)
-    return stacks
+    plane_requests = lax.all_gather(requests, "slab", axis=0, tiled=False)
+    asked = lax.all_to_all(plane_requests, "region", split_axis=1, concat_axis=1, tiled=True)
+    served = jnp.take(records, jnp.transpose(asked, (1, 0, 2)).reshape(-1), axis=0)
+    served = served.reshape(regions, slabs * capacity, width)
+    arrived = lax.all_to_all(served, "region", split_axis=0, concat_axis=0, tiled=True)
+    slots = lax.all_gather(slot_index, "slab", axis=0, tiled=False)
+    flat = (slots // capacity) * (slabs * capacity) + jnp.arange(slabs, dtype=jnp.int32)[:, None] * capacity + slots % capacity
+    second_parts = jnp.take(arrived.reshape(regions * slabs * capacity, width), flat.reshape(-1), axis=0)
+    second_parts = second_parts.reshape(slabs, pair_count, width)
+    second_arrived = lax.all_to_all(second_parts, "slab", split_axis=0, concat_axis=0, tiled=True)
+    second_rows = whitened(to_rows(second_arrived))
+    return cross(first_rows, second_rows)
 
 
 def solution(mesh):

time: 270 us -> 295 us (1.093)
  waiting for transfers between devices: 139 us -> 49.6 us
  blocking collectives: 0 us -> 71.6 us
  local copies, waits for them, and re-layouts: 25.8 us -> 73.6 us
  between operations: 13.7 us -> 0.37 us
  matrix products: 4.41 us -> 12.8 us
  starting transfers between devices: 35.6 us -> 41.4 us
  other arithmetic: 49.5 us -> 44.9 us
    all_gather x0 -> x3, blocking collectives: none -> 71.6 us  [the longest x1 28.5 us: local(): plane_requests = lax.all_gather(requests, 'slab', axis=0, tiled=False)]
    all_to_all x3 -> x4, waiting for transfers between devices: 96.3 us -> 49.6 us  [the longest x1 45 us: local(): lax.all_to_all(served, 'region', split_axis=0, concat_axis=0, tiled=True)]
    all_gather x1 -> x0, waiting for transfers between devices: 43.1 us -> none  [local(): piece = lax.all_gather(spectra, 'slab', axis=0, tiled=True)]
    gather x3, local copies, waits for them, and re-layouts: 14.8 us -> 48.3 us  [the longest x1 24 us: local(): jnp.take(records, jnp.transpose(asked, (1, 0, 2)).reshape(-1), axis=0)]
    another operation x3, other arithmetic: 35 us -> 5.12 us
    convert_element_type x2 -> x4, local copies, waits for them, and re-layouts: 0.39 us -> 10.6 us  [whitened(): signal = traces.astype(jnp.float32).reshape(count * SEG, NFFT)]
    add x1 -> x2, other arithmetic: 0.62 us -> 9.78 us  [whitened(): divisor = smooth + level + 1e-06]
    dot_general x1 -> x2, matrix products: 4.41 us -> 12.8 us  [whitened(): spectrum = jnp.dot(tapered, dft_table(), preferred_element_type=jnp.float32)]
  transfers between devices with their start and end apart: 4 -> 4, of which waited for: 3 -> 2; matrix products, arithmetic and copies ran while one was open for 17% -> 26% of each run, Pallas kernels for 0% -> 0%
where the time goes in v1:
time: 295 us; the launch traced here: 294 us
  local copies, waits for them, and re-layouts  73.6 us (25%)
  blocking collectives  71.6 us (24%)
  waiting for transfers between devices  49.6 us (17%)
  other arithmetic  44.9 us (15%)
  starting transfers between devices  41.4 us (14%)
  matrix products  12.8 us (4%)
    all_to_all x1, waiting for transfers between devices, local(): lax.all_to_all(served, 'region', split_axis=0, concat_axis=0, tiled=True)  45 us
    all_gather x1, blocking collectives, local(): plane_requests = lax.all_gather(requests, 'slab', axis=0, tiled=False)  28.5 us
    gather x1, local copies, waits for them, and re-layouts, local(): jnp.take(records, jnp.transpose(asked, (1, 0, 2)).reshape(-1), axis=0)  24 us
    all_gather x1, blocking collectives, local(): slots = lax.all_gather(slot_index, 'slab', axis=0, tiled=False)  22.3 us
    all_gather x1, blocking collectives, local(): firsts = lax.all_gather(first_station, 'slab', axis=0, tiled=False)  20.8 us
    dot_general x2, matrix products, whitened(): spectrum = jnp.dot(tapered, dft_table(), preferred_element_type=jnp.float32)  12.8 us
    all_to_all x1, starting transfers between devices, local(): lax.all_to_all(plane_requests, 'region', split_axis=1, concat_axis=1, til...  12.8 us
    gather x1, local copies, waits for them, and re-layouts, local(): jnp.take(records, firsts.reshape(-1), axis=0)  12.1 us
  transfers between devices with their start and end apart: 4, of which 2 were waited for; matrix products, arithmetic and copies ran while one was open for 26% of the time, Pallas kernels for 0%

profile of v1, /device:TPU:1, one launch (start us, length us, event | category | flops | bytes accessed | tf_op | source)
XLA Modules:
  0.0 294.2 jit_solution(7287885748230803281)
XLA Ops:
  0.0 0.8 fusion.52
  0.8 0.2 reduce_window_sum.11
  1.0 0.8 select_reduce_fusion
  1.8 0.7 fusion.62
  2.5 1.1 scatter_custom_fusion
  3.6 0.1 all_gather_reshape.3
  3.7 28.5 %all_gather.16 = s32[32,16,16]{2,1,0:T(8,128)S(1)} all-gather(s32[1,16,16]{2,1,0:T(8,128)S(1)} %all_gather_reshape.3), channel_id=1, replica_groups=mesh['region'=16,'slab'=32] {'slab'}, dimensions={0}, use_global_device_ids=true | all-gather | bytes 33792 | tf_op jit(solution)/shard_map/all_gather | solution.py:90
  32.2 0.2 copy.18
  32.3 0.7 reshape.354
  33.1 12.8 %all-to-all-start.1 = ((s32[16,1,512]{2,1,0:T(1,128)}), s32[16,1,512]{2,1,0:T(1,128)S(1)}, u32[]{:S(2)}, u32[]{:S(2)}) async-start(s32[16,1,512]{2,1,0:T(1,128)} %reshape.354), calls=%async_computation.1 | async-start | bytes 65536 | tf_op jit(solution)/shard_map/all_to_all | solution.py:91
  45.9 20.8 %all-gather.1 = s32[32,1,128]{2,1,0:T(1,128)S(1)} all-gather(s32[1,1,128]{2,1,0:T(1,128)} %bitcast.61), channel_id=2, replica_groups=mesh['region'=16,'slab'=32] {'slab'}, dimensions={0}, use_global_device_ids=true | all-gather | bytes 16896 | tf_op jit(solution)/shard_map/all_gather | solution.py:75
  66.7 0.0 copy-done
  66.7 12.1 %gather_fusion = bf16[4096,128]{1,0:T(8,128)(2,1)S(1)} fusion(bf16[1024,128]{1,0:T(8,128)(2,1)S(1)} %copy-done, s32[4096]{0:T(1024)S(1)} %broadcast_clamp_fusion.2), kind=kCustom, calls=%fused_computation | custom fusion | bytes 2113536 | tf_op jit(solution)/shard_map/jit(_take)/gather | solution.py:76
  78.9 1.5 broadcast_select_fusion.2
  80.4 0.0 all-to-all-done.1
  80.4 5.7 %all-to-all-start = ((bf16[32,128,128]{2,1,0:T(8,128)(2,1)}), bf16[32,128,128]{2,1,0:T(8,128)(2,1)S(1)}, u32[]{:S(2)}, u32[]{:S(2)}) async-start(bf16[32,128,128]{2,1,0:T(8,128)(2,1)} %broadcast_select_fusion.2), calls=%async_computation | async-start | bytes 2097152 | tf_op jit(solution)/shard_map/all_to_all | solution.py:77
  86.1 0.5 broadcast.374
  86.7 0.7 reduce.8
  87.4 0.1 reshape.355
  87.5 0.1 copy.19
  87.6 0.2 reshape.305
  87.8 0.2 reshape.304
  88.0 24.0 %gather_fusion.1 = bf16[8192,128]{1,0:T(8,128)(2,1)S(1)} fusion(bf16[1024,128]{1,0:T(8,128)(2,1)S(1)} %copy-done, s32[8192]{0:T(1024)S(1)} %broadcast_clamp_fusion), kind=kCustom, calls=%fused_computation.1 | custom fusion | bytes 4227072 | tf_op jit(solution)/shard_map/jit(_take)/gather | solution.py:92
  112.1 2.7 broadcast_select_fusion
  114.7 0.0 all-to-all-done
  114.7 11.8 %all-to-all-start.2 = ((bf16[16,512,128]{2,1,0:T(8,128)(2,1)}), bf16[16,512,128]{2,1,0:T(8,128)(2,1)S(1)}, u32[]{:S(2)}, u32[]{:S(2)}) async-start(bf16[16,512,128]{2,1,0:T(8,128)(2,1)} %broadcast_select_fusion), calls=%async_computation.2 | async-start | bytes 4194304 | tf_op jit(solution)/shard_map/all_to_all | solution.py:94
  126.6 22.3 %all-gather.2 = s32[32,1,128]{2,1,0:T(1,128)S(1)} all-gather(s32[1,1,128]{2,1,0:T(1,128)S(1)} %fusion.63), channel_id=1, replica_groups=mesh['region'=16,'slab'=32] {'slab'}, dimensions={0}, use_global_device_ids=true | all-gather | bytes 16896 | tf_op jit(solution)/shard_map/all_gather | solution.py:95
  148.9 0.6 multiply_subtract_fusion
  149.5 0.5 fusion.53
  150.1 1.0 fusion.47
  151.1 0.7 compare_and_fusion.1
  151.8 5.0 %subtract_convert_fusion = (bf16[32,64,1024]{2,1,0:T(8,128)(2,1)}, bf16[32,64,1024]{2,1,0:T(8,128)(2,1)}) fusion(f32[64,1024]{1,0:T(8,128)S(1)} %get-tuple-element.15, f32[32,1024]{1,0:T(8,128)S(1)} %get-tuple-element.17, f32[64,1024]{1,0:T(8,128)S(1)} %get-tuple-element.16, f32[32,1024]{1,0:T(8,128)S(1)} %get-tuple-element.18), kind=kLoop, calls=%fused_computation.6 | loop fusion | flops 18874368 | bytes 9175040 | tf_op jit(solution)/shard_map/convert.11
  156.9 0.3 convert_reduce_fusion.1
  157.2 0.7 copy.17
  157.9 0.9 reduce_sum.87
  158.9 0.2 convert_bitcast_fusion.1
  159.1 2.5 copy.16
  161.6 2.8 reshape.308
  164.4 0.1 reduce_sum.88
  164.5 6.4 %fusion.1 = f32[256,2048]{1,0:T(8,128)S(1)} fusion(bf16[2048,1024]{1,0:T(8,128)(2,1)} %bitcast.48, bf16[2048,1024]{1,0:T(8,128)(2,1)} %bitcast.46, f32[256,2048]{1,0:T(8,128)} %reshape.308, f32[2048]{0:T(1024)S(1)} %copy-done.4, f32[256]{0:T(256)S(1)} %broadcast_multiply_fusion.3), kind=kOutput, calls=%fused_computation.8 | convolution fusion | flops 2165833728 | bytes 12592128 | tf_op jit(solution)/shard_map/dot_general | solution.py:36
  170.9 1.3 copy-done.1
  172.2 1.4 fusion.68
  173.6 45.0 %all-to-all-done.2 = bf16[16,512,128]{2,1,0:T(8,128)(2,1)S(1)} async-done(((bf16[16,512,128]{2,1,0:T(8,128)(2,1)}), bf16[16,512,128]{2,1,0:T(8,128)(2,1)S(1)}, u32[]{:S(2)}, u32[]{:S(2)}) %all-to-all-start.2) | async-done | bytes 2097184 | tf_op jit(solution)/shard_map/all_to_all | solution.py:94
  218.6 12.1 %gather_fusion.2 = bf16[4096,128]{1,0:T(8,128)(2,1)S(1)} fusion(bf16[8192,128]{1,0:T(8,128)(2,1)S(1)} %bitcast.42, s32[4096]{0:T(1024)S(1)} %broadcast_clamp_fusion.1), kind=kCustom, calls=%fused_computation.2 | custom fusion | bytes 2113536 | tf_op jit(solution)/shard_map/jit(_take)/gather | solution.py:97
  230.7 1.6 broadcast_select_fusion.1
  232.3 11.0 %all-to-all-start.3 = ((bf16[32,128,128]{2,1,0:T(8,128)(2,1)}), bf16[32,128,128]{2,1,0:T(8,128)(2,1)S(1)}, u32[]{:S(2)}, u32[]{:S(2)}) async-start(bf16[32,128,128]{2,1,0:T(8,128)(2,1)} %broadcast_select_fusion.1), calls=%async_computation.3 | async-start | bytes 2097152 | tf_op jit(solution)/shard_map/all_to_all | solution.py:99
  243.3 7.5 %fusion.14 = f32[256,1024]{1,0:T(8,128)S(1)} fusion(f32[256,1024]{1,0:T(8,128)} %get-tuple-element.8, f32[256]{0:T(256)S(1)} %broadcast_multiply_fusion.1), kind=kLoop, calls=%fused_computation.46 | loop fusion | flops 2883584 | bytes 2098176 | tf_op jit(solution)/shard_map/add | solution.py:46
  250.9 1.7 fusion.37
  252.6 3.0 %reshape.309 = f32[128,2,2,1024]{3,2,1,0:T(2,128)S(1)} reshape(f32[256,2048]{1,0:T(8,128)} %fusion.37) | data formatting | bytes 4194304 | tf_op jit(solution)/shard_map/convert_element_type | solution.py:52
  255.6 4.6 %all-to-all-done.3 = bf16[32,128,128]{2,1,0:T(8,128)(2,1)S(1)} async-done(((bf16[32,128,128]{2,1,0:T(8,128)(2,1)}), bf16[32,128,128]{2,1,0:T(8,128)(2,1)S(1)}, u32[]{:S(2)}, u32[]{:S(2)}) %all-to-all-start.3) | async-done | bytes 1048608 | tf_op jit(solution)/shard_map/all_to_all | solution.py:99
  260.2 0.3 convert_reduce_fusion
  260.6 0.7 copy.22
  261.3 0.9 reduce_sum.95
  262.2 0.1 reduce_sum.96
  262.3 0.2 convert_bitcast_fusion
  262.6 2.5 copy.21
  265.1 2.8 reshape.310
  267.9 6.4 %fusion = f32[256,2048]{1,0:T(8,128)S(1)} fusion(bf16[2048,1024]{1,0:T(8,128)(2,1)} %bitcast.49, bf16[2048,1024]{1,0:T(8,128)(2,1)} %bitcast.47, f32[256,2048]{1,0:T(8,128)} %reshape.310, f32[256]{0:T(256)S(1)} %broadcast_multiply_fusion.2, f32[2048]{0:T(1024)S(1)} %copy-done.5), kind=kOutput, calls=%fused_computation.7 | convolution fusion | flops 2165833728 | bytes 12592128 | tf_op jit(solution)/shard_map/dot_general | solution.py:36
  274.3 0.5 fusion.70
  274.8 2.3 fusion.25
  277.1 1.7 fusion.36
  278.8 4.0 %reshape.311 = f32[128,2,2,1024]{3,2,1,0:T(2,128)} reshape(f32[256,2048]{1,0:T(8,128)} %fusion.36) | data formatting | bytes 4194304 | tf_op jit(solution)/shard_map/convert_element_type | solution.py:53
  282.8 10.5 %add_reduce_fusion = (f32[128,1024]{1,0:T(8,128)S(1)}, f32[128,1024]{1,0:T(8,128)S(1)}) fusion(f32[128,2,2,1024]{3,2,1,0:T(2,128)} %reshape.311, f32[128,2,2,1024]{3,2,1,0:T(2,128)S(1)} %reshape.309), kind=kLoop, calls=%fused_computation.69 | loop fusion | flops 1835008 | bytes 5242880 | tf_op jit(solution)/shard_map/reduce_sum | solution.py:54
  293.4 0.8 pad_maximum_fusion.3
  (29 shorter events, 0.2 us)
Async XLA Ops:
  0.0 66.7 %copy-start = (bf16[1024,128]{1,0:T(8,128)(2,1)S(1)}, bf16[1024,128]{1,0:T(8,128)(2,1)}, u32[]{:S(2)}) copy-start(bf16[1024,128]{1,0:T(8,128)(2,1)} %param.4) | copy-start | bytes 786436
  33.1 47.3 %all-to-all-start.1 = ((s32[16,1,512]{2,1,0:T(1,128)}), s32[16,1,512]{2,1,0:T(1,128)S(1)}, u32[]{:S(2)}, u32[]{:S(2)}) async-start(s32[16,1,512]{2,1,0:T(1,128)} %reshape.354), calls=%async_computation.1 | async-start | bytes 65536 | tf_op jit(solution)/shard_map/all_to_all | solution.py:91
  80.4 34.4 %all-to-all-start = ((bf16[32,128,128]{2,1,0:T(8,128)(2,1)}), bf16[32,128,128]{2,1,0:T(8,128)(2,1)S(1)}, u32[]{:S(2)}, u32[]{:S(2)}) async-start(bf16[32,128,128]{2,1,0:T(8,128)(2,1)} %broadcast_select_fusion.2), calls=%async_computation | async-start | bytes 2097152 | tf_op jit(solution)/shard_map/all_to_all | solution.py:77
  114.7 11.9 %copy-start.6 = (s32[128,1]{0,1:T(1,128)S(1)}, s32[128,1]{0,1:T(1,128)}, u32[]{:S(2)}) copy-start(s32[128,1]{0,1:T(1,128)} %param.6) | copy-start | bytes 1540
  114.7 103.8 %all-to-all-start.2 = ((bf16[16,512,128]{2,1,0:T(8,128)(2,1)}), bf16[16,512,128]{2,1,0:T(8,128)(2,1)S(1)}, u32[]{:S(2)}, u32[]{:S(2)}) async-start(bf16[16,512,128]{2,1,0:T(8,128)(2,1)} %broadcast_select_fusion), calls=%async_computation.2 | async-start | bytes 4194304 | tf_op jit(solution)/shard_map/all_to_all | solution.py:94
  161.6 2.9 copy-start.4
  170.9 1.3 copy-start.1
  218.6 12.1 %copy-start.3 = (pred[32,128]{1,0:T(8,128)(4,1)S(1)}, pred[32,128]{1,0:T(8,128)(4,1)}, u32[]{:S(2)}) copy-start(pred[32,128]{1,0:T(8,128)(4,1)} %get-tuple-element.11) | copy-start | bytes 12292
  232.3 18.6 %copy-start.2 = (f32[256,2048]{1,0:T(8,128)S(1)}, f32[256,2048]{1,0:T(8,128)}, u32[]{:S(2)}) copy-start(f32[256,2048]{1,0:T(8,128)} %copy-done.1) | copy-start | bytes 6291460
  232.3 27.9 %all-to-all-start.3 = ((bf16[32,128,128]{2,1,0:T(8,128)(2,1)}), bf16[32,128,128]{2,1,0:T(8,128)(2,1)S(1)}, u32[]{:S(2)}, u32[]{:S(2)}) async-start(bf16[32,128,128]{2,1,0:T(8,128)(2,1)} %broadcast_select_fusion.1), calls=%async_computation.3 | async-start | bytes 2097152 | tf_op jit(solution)/shard_map/all_to_all | solution.py:99
  265.1 2.8 copy-start.5

commit v2 on v1

--- a/solution.py
+++ b/solution.py
@@ -3,6 +3,8 @@
 import jax
 import jax.numpy as jnp
 from jax import lax
+from jax.experimental import pallas as pl
+from jax.experimental.pallas import tpu as pltpu
 from jax.sharding import PartitionSpec as P
 
 NFFT = 2048
@@ -60,6 +62,60 @@
     return jnp.concatenate([real_sum, imag_sum], axis=-1).astype(jnp.bfloat16)
 
 
+def _pick_kernel(ids_ref, table_ref, out_ref):
+    ids = ids_ref[...]
+    rows = table_ref.shape[0]
+    onehot = (lax.broadcasted_iota(jnp.int32, (ids.shape[0], rows), 1) == ids).astype(table_ref.dtype)
+    out_ref[...] = jnp.dot(onehot, table_ref[...], preferred_element_type=jnp.float32).astype(out_ref.dtype)
+
+
+def pick_rows(table, ids, block=512):
+    rows, width = table.shape
+    count = ids.shape[0]
+    block = min(block, count)
+    return pl.pallas_call(
+        _pick_kernel,
+        out_shape=jax.ShapeDtypeStruct((count, width), table.dtype),
+        grid=(count // block,),
+        in_specs=[
+            pl.BlockSpec((block, 1), lambda i: (i, 0)),
+            pl.BlockSpec((rows, width), lambda i: (0, 0)),
+        ],
+        out_specs=pl.BlockSpec((block, width), lambda i: (i, 0)),
+        cost_estimate=pl.CostEstimate(
+            flops=2 * count * rows * width, transcendentals=0, bytes_accessed=2 * (rows + count) * width
+        ),
+    )(ids.reshape(count, 1), table)
+
+
+def _compact_kernel(ids_ref, table_ref, out_ref):
+    ids = ids_ref[0]
+    buckets, capacity, width = table_ref.shape
+    table = table_ref[...].reshape(buckets * capacity, width)
+    onehot = (lax.broadcasted_iota(jnp.int32, (ids.shape[0], buckets * capacity), 1) == ids).astype(table.dtype)
+    out_ref[0] = jnp.dot(onehot, table, preferred_element_type=jnp.float32).astype(out_ref.dtype)
+
+
+def compact_rows(arrived, slots):
+    buckets, slabs, capacity, width = arrived.shape
+    pairs = slots.shape[1]
+    return pl.pallas_call(
+        _compact_kernel,
+        out_shape=jax.ShapeDtypeStruct((slabs, pairs, width), arrived.dtype),
+        grid=(slabs,),
+        in_specs=[
+            pl.BlockSpec((1, pairs, 1), lambda s: (s, 0, 0)),
+            pl.BlockSpec((buckets, None, capacity, width), lambda s: (0, s, 0, 0)),
+        ],
+        out_specs=pl.BlockSpec((1, pairs, width), lambda s: (s, 0, 0)),
+        cost_estimate=pl.CostEstimate(
+            flops=2 * slabs * pairs * buckets * capacity * width,
+            transcendentals=0,
+            bytes_accessed=2 * (buckets * capacity + pairs) * slabs * width,
+        ),
+    )(slots.reshape(slabs, pairs, 1), arrived)
+
+
 def to_rows(parts):
     slabs, rows, width = parts.shape
     return jnp.transpose(parts, (1, 0, 2)).reshape(rows, slabs * width)
@@ -72,11 +128,6 @@
     width = records.shape[1]
     capacity = max(2, pair_count // regions + pair_count // 16)
 
-    firsts = lax.all_gather(first_station, "slab", axis=0, tiled=False)
-    first_parts = jnp.take(records, firsts.reshape(-1), axis=0).reshape(slabs, pair_count, width)
-    first_arrived = lax.all_to_all(first_parts, "slab", split_axis=0, concat_axis=0, tiled=True)
-    first_rows = whitened(to_rows(first_arrived))
-
     target = second_region[:, 0]
     onehot = (target[:, None] == jnp.arange(regions, dtype=jnp.int32)[None, :]).astype(jnp.int32)
     ranking = jnp.sum((jnp.cumsum(onehot, axis=0) - onehot) * onehot, axis=1)
@@ -85,17 +136,22 @@
         jnp.zeros((regions * capacity,), jnp.int32)
         .at[slot_index]
         .set(second_station)
-        .reshape(regions, capacity)
     )
-    plane_requests = lax.all_gather(requests, "slab", axis=0, tiled=False)
+    packed = jnp.concatenate([first_station, slot_index, requests])
+    plane = lax.all_gather(packed, "slab", axis=0, tiled=False)
+    firsts = plane[:, :pair_count]
+    slots = plane[:, pair_count : 2 * pair_count]
+    plane_requests = plane[:, 2 * pair_count :].reshape(slabs, regions, capacity)
+
+    first_parts = pick_rows(records, firsts.reshape(-1)).reshape(slabs, pair_count, width)
+    first_arrived = lax.all_to_all(first_parts, "slab", split_axis=0, concat_axis=0, tiled=True)
+    first_rows = whitened(to_rows(first_arrived))
+
     asked = lax.all_to_all(plane_requests, "region", split_axis=1, concat_axis=1, tiled=True)
-    served = jnp.take(records, jnp.transpose(asked, (1, 0, 2)).reshape(-1), axis=0)
+    served = pick_rows(records, jnp.transpose(asked, (1, 0, 2)).reshape(-1))
     served = served.reshape(regions, slabs * capacity, width)
     arrived = lax.all_to_all(served, "region", split_axis=0, concat_axis=0, tiled=True)
-    slots = lax.all_gather(slot_index, "slab", axis=0, tiled=False)
-    flat = (slots // capacity) * (slabs * capacity) + jnp.arange(slabs, dtype=jnp.int32)[:, None] * capacity + slots % capacity
-    second_parts = jnp.take(arrived.reshape(regions * slabs * capacity, width), flat.reshape(-1), axis=0)
-    second_parts = second_parts.reshape(slabs, pair_count, width)
+    second_parts = compact_rows(arrived.reshape(regions, slabs, capacity, width), slots)
     second_arrived = lax.all_to_all(second_parts, "slab", split_axis=0, concat_axis=0, tiled=True)
     second_rows = whitened(to_rows(second_arrived))
     return cross(first_rows, second_rows)

time: 295 us -> 268 us (0.908)
  blocking collectives: 71.6 us -> 27.9 us
  local copies, waits for them, and re-layouts: 73.6 us -> 31 us
  Pallas kernels: 0 us -> 41.5 us
  waiting for transfers between devices: 49.6 us -> 74.2 us
  other arithmetic: 44.9 us -> 39.1 us
    gather x3 -> x0, local copies, waits for them, and re-layouts: 48.3 us -> none  [the longest x1 24 us: local(): jnp.take(records, jnp.transpose(asked, (1, 0, 2)).reshape(-1), axis=0)]
    all_gather x3 -> x1, blocking collectives: 71.6 us -> 27.9 us  [local(): plane = lax.all_gather(packed, 'slab', axis=0, tiled=False)]
    pallas_call x0 -> x3, Pallas kernels: none -> 41.5 us  [the longest x2 22.2 us: pick_rows(): pl.pallas_call(_pick_kernel, out_shape=jax.ShapeDtypeStruct((count, width...]
    all_to_all x1, waiting for transfers between devices: 45 us -> 67.8 us  [local(): lax.all_to_all(served, 'region', split_axis=0, concat_axis=0, tiled=True)]
    select_n x6 -> x0, other arithmetic: 5.83 us -> none  [the longest x2 2.72 us: local(): jnp.take(records, jnp.transpose(asked, (1, 0, 2)).reshape(-1), axis=0)]
    another operation x1 -> x2, local copies, waits for them, and re-layouts: 0.08 us -> 5.6 us  [pick_rows(): ids.reshape(count, 1)]
  transfers between devices with their start and end apart: 4 -> 4, of which waited for: 2 -> 3; matrix products, arithmetic and copies ran while one was open for 26% -> 16% of each run, Pallas kernels for 0% -> 8%
where the time goes in v2:
time: 268 us; the launch traced here: 266 us
  waiting for transfers between devices  74.2 us (28%)
  Pallas kernels  41.5 us (15%)
  starting transfers between devices  39.3 us (15%)
  other arithmetic  39.1 us (15%)
  local copies, waits for them, and re-layouts  31 us (12%)
  blocking collectives  27.9 us (10%)
  matrix products  12.8 us (5%)
    all_to_all x1, waiting for transfers between devices, local(): lax.all_to_all(served, 'region', split_axis=0, concat_axis=0, tiled=True)  67.8 us
    all_gather x1, blocking collectives, local(): plane = lax.all_gather(packed, 'slab', axis=0, tiled=False)  27.9 us
    pallas_call x2, Pallas kernels, pick_rows(): pl.pallas_call(_pick_kernel, out_shape=jax.ShapeDtypeStruct((count, width...  22.2 us
    pallas_call x1, Pallas kernels, compact_rows(): pl.pallas_call(_compact_kernel, out_shape=jax.ShapeDtypeStruct((slabs, pa...  19.2 us
    all_to_all x1, starting transfers between devices, local(): lax.all_to_all(plane_requests, 'region', split_axis=1, concat_axis=1, til...  12.8 us
    dot_general x2, matrix products, whitened(): spectrum = jnp.dot(tapered, dft_table(), preferred_element_type=jnp.float32)  12.8 us
    all_to_all x1, starting transfers between devices, local(): lax.all_to_all(second_parts, 'slab', split_axis=0, concat_axis=0, tiled=T...  11 us
    convert_element_type x4, local copies, waits for them, and re-layouts, whitened(): signal = traces.astype(jnp.float32).reshape(count * SEG, NFFT)  10.6 us
  transfers between devices with their start and end apart: 4, of which 3 were waited for; matrix products, arithmetic and copies ran while one was open for 16% of the time, Pallas kernels for 8%

profile of v2, /device:TPU:1, one launch (start us, length us, event | category | flops | bytes accessed | tf_op | source)
XLA Modules:
  0.0 266.0 jit_solution(8302617701293182405)
XLA Ops:
  0.0 0.7 fusion.54
  0.7 0.2 reduce_window_sum.11
  0.9 0.8 select_reduce_fusion
  1.7 0.7 fusion.55
  2.4 0.7 multiply_add_fusion
  3.1 1.1 scatter_custom_fusion
  4.2 0.7 pad_add_fusion
  4.9 27.9 %all-gather.1 = s32[32,1,512]{2,1,0:T(1,128)S(1)} all-gather(s32[1,1,512]{2,1,0:T(1,128)S(1)} %bitcast.46), channel_id=2, replica_groups=mesh['region'=16,'slab'=32] {'slab'}, dimensions={0}, use_global_device_ids=true | all-gather | bytes 67584 | tf_op jit(solution)/shard_map/all_gather | solution.py:141
  32.7 0.1 copy.31
  32.8 0.7 reshape.182
  33.6 12.8 %all-to-all-start.1 = ((s32[16,1,512]{2,1,0:T(1,128)}), s32[16,1,512]{2,1,0:T(1,128)S(1)}, u32[]{:S(2)}, u32[]{:S(2)}) async-start(s32[16,1,512]{2,1,0:T(1,128)} %reshape.182), calls=%async_computation.1 | async-start | bytes 65536 | tf_op jit(solution)/shard_map/all_to_all | solution.py:150
  46.4 2.0 copy.28.ids_ref
  48.4 7.8 %shard_map.46 = bf16[4096,128]{1,0:T(8,128)(2,1)} custom-call(s32[4096,1]{1,0:T(8,128)} %copy.28.ids_ref, bf16[1024,128]{1,0:T(8,128)(2,1)} %table_ref.3), custom_call_target="tpu_custom_call" | custom-call | flops 1073741824 | bytes 1310720 | tf_op jit(solution)/shard_map/pallas_call | solution.py:76
  56.3 1.7 all-to-all-done.1
  58.0 6.4 %all-to-all-start = ((bf16[32,128,128]{2,1,0:T(8,128)(2,1)}), bf16[32,128,128]{2,1,0:T(8,128)(2,1)S(1)}, u32[]{:S(2)}, u32[]{:S(2)}) async-start(bf16[32,128,128]{2,1,0:T(8,128)(2,1)} %bitcast.39), calls=%async_computation | async-start | bytes 2097152 | tf_op jit(solution)/shard_map/all_to_all | solution.py:147
  64.4 0.5 broadcast.246
  64.9 0.7 reduce.8
  65.7 0.1 reshape.183
  65.8 0.1 copy.32
  65.9 3.6 %reshape_reshape.8.ids_ref = s32[8192,1]{1,0:T(8,128)} reshape(s32[16,32,16]{2,1,0:T(8,128)S(1)} %copy.32) | data formatting | bytes 65536 | tf_op jit(solution)/shard_map/reshape;reshape | solution.py:88
  69.5 14.4 %shard_map.47 = bf16[8192,128]{1,0:T(8,128)(2,1)} custom-call(s32[8192,1]{1,0:T(8,128)} %reshape_reshape.8.ids_ref, bf16[1024,128]{1,0:T(8,128)(2,1)} %table_ref.3), custom_call_target="tpu_custom_call" | custom-call | flops 2147483648 | bytes 2359296 | tf_op jit(solution)/shard_map/pallas_call | solution.py:76
  83.9 0.0 all-to-all-done
  83.9 9.0 %all-to-all-start.2 = ((bf16[16,512,128]{2,1,0:T(8,128)(2,1)}), bf16[16,512,128]{2,1,0:T(8,128)(2,1)S(1)}, u32[]{:S(2)}, u32[]{:S(2)}) async-start(bf16[16,512,128]{2,1,0:T(8,128)(2,1)} %bitcast.38), calls=%async_computation.2 | async-start | bytes 4194304 | tf_op jit(solution)/shard_map/all_to_all | solution.py:153
  93.0 2.0 copy.34.ids_ref
  95.0 0.1 multiply_subtract_fusion
  95.1 0.5 fusion.52
  95.6 1.0 fusion.47
  96.6 5.0 %subtract_convert_fusion = (bf16[32,64,1024]{2,1,0:T(8,128)(2,1)}, bf16[32,64,1024]{2,1,0:T(8,128)(2,1)}) fusion(f32[64,1024]{1,0:T(8,128)S(1)} %get-tuple-element.15, f32[32,1024]{1,0:T(8,128)S(1)} %get-tuple-element.17, f32[64,1024]{1,0:T(8,128)S(1)} %get-tuple-element.16, f32[32,1024]{1,0:T(8,128)S(1)} %get-tuple-element.18), kind=kLoop, calls=%fused_computation.3 | loop fusion | flops 18874368 | bytes 9175040 | tf_op jit(solution)/shard_map/convert.11
  101.7 0.3 convert_reduce_fusion.1
  102.0 0.1 copy.30
  102.1 0.1 reduce_sum.87
  102.2 0.2 convert_bitcast_fusion.1
  102.4 2.6 copy.29
  105.0 2.7 %reshape.164 = f32[256,2048]{1,0:T(8,128)} reshape(f32[128,32,128]{2,1,0:T(8,128)} %copy.29) | data formatting | bytes 4194304 | tf_op jit(solution)/shard_map/convert_element_type | solution.py:33
  107.7 0.1 reduce_sum.88
  107.9 6.4 %fusion.1 = f32[256,2048]{1,0:T(8,128)S(1)} fusion(bf16[2048,1024]{1,0:T(8,128)(2,1)} %bitcast.36, bf16[2048,1024]{1,0:T(8,128)(2,1)} %bitcast.34, f32[256,2048]{1,0:T(8,128)} %reshape.164, f32[2048]{0:T(1024)S(1)} %multiply_subtract_fusion, f32[256]{0:T(256)S(1)} %broadcast_multiply_fusion.3), kind=kOutput, calls=%fused_computation.5 | convolution fusion | flops 2165833728 | bytes 12592128 | tf_op jit(solution)/shard_map/dot_general | solution.py:38
  114.3 0.0 copy-start.1
  114.3 1.4 copy-done.1
  115.7 1.4 fusion.60
  117.1 67.8 %all-to-all-done.2 = bf16[16,512,128]{2,1,0:T(8,128)(2,1)S(1)} async-done(((bf16[16,512,128]{2,1,0:T(8,128)(2,1)}), bf16[16,512,128]{2,1,0:T(8,128)(2,1)S(1)}, u32[]{:S(2)}, u32[]{:S(2)}) %all-to-all-start.2) | async-done | bytes 2097184 | tf_op jit(solution)/shard_map/all_to_all | solution.py:153
  184.9 0.0 copy-start
  184.9 1.3 copy-done
  186.2 19.2 %shard_map.48 = bf16[32,128,128]{2,1,0:T(8,128)(2,1)} custom-call(s32[32,128,1]{2,1,0:T(8,128)} %copy.34.ids_ref, bf16[16,32,16,128]{3,2,1,0:T(8,128)(2,1)} %bitcast.33), custom_call_target="tpu_custom_call" | custom-call | flops 268435456 | bytes 3145728 | tf_op jit(solution)/shard_map/pallas_call | solution.py:102
  205.5 0.0 copy-start.2
  205.5 11.0 %all-to-all-start.3 = ((bf16[32,128,128]{2,1,0:T(8,128)(2,1)}), bf16[32,128,128]{2,1,0:T(8,128)(2,1)S(1)}, u32[]{:S(2)}, u32[]{:S(2)}) async-start(bf16[32,128,128]{2,1,0:T(8,128)(2,1)} %shard_map.48), calls=%async_computation.3 | async-start | bytes 2097152 | tf_op jit(solution)/shard_map/all_to_all | solution.py:155
  216.5 7.5 %fusion.14 = f32[256,1024]{1,0:T(8,128)S(1)} fusion(f32[256,1024]{1,0:T(8,128)} %get-tuple-element.8, f32[256]{0:T(256)S(1)} %broadcast_multiply_fusion.1), kind=kLoop, calls=%fused_computation.42 | loop fusion | flops 2883584 | bytes 2098176 | tf_op jit(solution)/shard_map/add | solution.py:48
  224.0 0.0 copy-done.2
  224.0 1.8 fusion.37
  225.8 3.0 %reshape.165 = f32[128,2,2,1024]{3,2,1,0:T(2,128)S(1)} reshape(f32[256,2048]{1,0:T(8,128)} %fusion.37) | data formatting | bytes 4194304 | tf_op jit(solution)/shard_map/convert_element_type | solution.py:54
  228.8 4.6 %all-to-all-done.3 = bf16[32,128,128]{2,1,0:T(8,128)(2,1)S(1)} async-done(((bf16[32,128,128]{2,1,0:T(8,128)(2,1)}), bf16[32,128,128]{2,1,0:T(8,128)(2,1)S(1)}, u32[]{:S(2)}, u32[]{:S(2)}) %all-to-all-start.3) | async-done | bytes 1048608 | tf_op jit(solution)/shard_map/all_to_all | solution.py:155
  233.4 0.3 convert_reduce_fusion
  233.7 0.1 copy.36
  233.8 0.1 reduce_sum.92
  233.9 0.1 reduce_sum.93
  234.1 0.2 convert_bitcast_fusion
  234.3 2.5 copy.35
  236.8 2.8 %reshape.166 = f32[256,2048]{1,0:T(8,128)} reshape(f32[128,32,128]{2,1,0:T(8,128)} %copy.35) | data formatting | bytes 4194304 | tf_op jit(solution)/shard_map/convert_element_type | solution.py:33
  239.6 6.4 %fusion = f32[256,2048]{1,0:T(8,128)S(1)} fusion(bf16[2048,1024]{1,0:T(8,128)(2,1)} %bitcast.37, bf16[2048,1024]{1,0:T(8,128)(2,1)} %bitcast.35, f32[256,2048]{1,0:T(8,128)} %reshape.166, f32[256]{0:T(256)S(1)} %broadcast_multiply_fusion.2, f32[2048]{0:T(1024)S(1)} %multiply_subtract_fusion), kind=kOutput, calls=%fused_computation.4 | convolution fusion | flops 2165833728 | bytes 12592128 | tf_op jit(solution)/shard_map/dot_general | solution.py:38
  246.0 0.5 fusion.62
  246.5 2.3 fusion.25
  248.8 1.8 fusion.36
  250.6 4.0 %reshape.167 = f32[128,2,2,1024]{3,2,1,0:T(2,128)} reshape(f32[256,2048]{1,0:T(8,128)} %fusion.36) | data formatting | bytes 4194304 | tf_op jit(solution)/shard_map/convert_element_type | solution.py:55
  254.6 10.5 %add_reduce_fusion = (f32[128,1024]{1,0:T(8,128)S(1)}, f32[128,1024]{1,0:T(8,128)S(1)}) fusion(f32[128,2,2,1024]{3,2,1,0:T(2,128)} %reshape.167, f32[128,2,2,1024]{3,2,1,0:T(2,128)S(1)} %reshape.165), kind=kLoop, calls=%fused_computation.65 | loop fusion | flops 1835008 | bytes 5242880 | tf_op jit(solution)/shard_map/reduce_sum | solution.py:56
  265.2 0.8 pad_maximum_fusion.3
  (10 shorter events, 0.1 us)
Async XLA Ops:
  33.6 24.4 %all-to-all-start.1 = ((s32[16,1,512]{2,1,0:T(1,128)}), s32[16,1,512]{2,1,0:T(1,128)S(1)}, u32[]{:S(2)}, u32[]{:S(2)}) async-start(s32[16,1,512]{2,1,0:T(1,128)} %reshape.182), calls=%async_computation.1 | async-start | bytes 65536 | tf_op jit(solution)/shard_map/all_to_all | solution.py:150
  58.0 25.9 %all-to-all-start = ((bf16[32,128,128]{2,1,0:T(8,128)(2,1)}), bf16[32,128,128]{2,1,0:T(8,128)(2,1)S(1)}, u32[]{:S(2)}, u32[]{:S(2)}) async-start(bf16[32,128,128]{2,1,0:T(8,128)(2,1)} %bitcast.39), calls=%async_computation | async-start | bytes 2097152 | tf_op jit(solution)/shard_map/all_to_all | solution.py:147
  83.9 101.0 %all-to-all-start.2 = ((bf16[16,512,128]{2,1,0:T(8,128)(2,1)}), bf16[16,512,128]{2,1,0:T(8,128)(2,1)S(1)}, u32[]{:S(2)}, u32[]{:S(2)}) async-start(bf16[16,512,128]{2,1,0:T(8,128)(2,1)} %bitcast.38), calls=%async_computation.2 | async-start | bytes 4194304 | tf_op jit(solution)/shard_map/all_to_all | solution.py:153
  114.3 1.4 copy-start.1
  184.9 1.3 copy-start
  205.5 18.5 %copy-start.2 = (f32[256,2048]{1,0:T(8,128)S(1)}, f32[256,2048]{1,0:T(8,128)}, u32[]{:S(2)}) copy-start(f32[256,2048]{1,0:T(8,128)} %copy-done.1) | copy-start | bytes 6291460
  205.5 27.9 %all-to-all-start.3 = ((bf16[32,128,128]{2,1,0:T(8,128)(2,1)}), bf16[32,128,128]{2,1,0:T(8,128)(2,1)S(1)}, u32[]{:S(2)}, u32[]{:S(2)}) async-start(bf16[32,128,128]{2,1,0:T(8,128)(2,1)} %shard_map.48), calls=%async_computation.3 | async-start | bytes 2097152 | tf_op jit(solution)/shard_map/all_to_all | solution.py:155

commit v3 on v2

--- a/solution.py
+++ b/solution.py
@@ -89,11 +89,12 @@
 
 
 def _compact_kernel(ids_ref, table_ref, out_ref):
-    ids = ids_ref[0]
-    buckets, capacity, width = table_ref.shape
-    table = table_ref[...].reshape(buckets * capacity, width)
-    onehot = (lax.broadcasted_iota(jnp.int32, (ids.shape[0], buckets * capacity), 1) == ids).astype(table.dtype)
-    out_ref[0] = jnp.dot(onehot, table, preferred_element_type=jnp.float32).astype(out_ref.dtype)
+    buckets, slabs, capacity, width = table_ref.shape
+    for s in range(slabs):
+        ids = ids_ref[s]
+        table = table_ref[:, s].reshape(buckets * capacity, width)
+        onehot = (lax.broadcasted_iota(jnp.int32, (ids.shape[0], buckets * capacity), 1) == ids).astype(table.dtype)
+        out_ref[s] = jnp.dot(onehot, table, preferred_element_type=jnp.float32).astype(out_ref.dtype)
 
 
 def compact_rows(arrived, slots):
@@ -102,18 +103,115 @@
     return pl.pallas_call(
         _compact_kernel,
         out_shape=jax.ShapeDtypeStruct((slabs, pairs, width), arrived.dtype),
-        grid=(slabs,),
-        in_specs=[
-            pl.BlockSpec((1, pairs, 1), lambda s: (s, 0, 0)),
-            pl.BlockSpec((buckets, None, capacity, width), lambda s: (0, s, 0, 0)),
-        ],
-        out_specs=pl.BlockSpec((1, pairs, width), lambda s: (s, 0, 0)),
         cost_estimate=pl.CostEstimate(
             flops=2 * slabs * pairs * buckets * capacity * width,
             transcendentals=0,
             bytes_accessed=2 * (buckets * capacity + pairs) * slabs * width,
         ),
     )(slots.reshape(slabs, pairs, 1), arrived)
+
+
+def _white_block(x, table, taper):
+    slabs, rows, width = x.shape
+    per_segment = slabs // SEG
+    signal = x.astype(jnp.float32)
+    tapered = []
+    for segment in range(SEG):
+        part = signal[segment * per_segment : (segment + 1) * per_segment]
+        mean = jnp.sum(jnp.sum(part, axis=2, keepdims=True), axis=0) / NFFT
+        pieces = [((part[i] - mean) * taper[i : i + 1, :]).astype(jnp.bfloat16) for i in range(per_segment)]
+        tapered.append(jnp.concatenate(pieces, axis=1))
+    spectrum = jnp.dot(jnp.concatenate(tapered, axis=0), table, preferred_element_type=jnp.float32)
+    real_part = spectrum[:, :BINS]
+    imag_part = spectrum[:, BINS:]
+    amplitude = jnp.sqrt(real_part * real_part + imag_part * imag_part + 1e-06)
+    lane = lax.broadcasted_iota(jnp.int32, amplitude.shape, 1)
+    smooth = jnp.zeros_like(amplitude)
+    for offset in range(-HALF, HALF + 1):
+        moved = amplitude if offset == 0 else pltpu.roll(amplitude, (-offset) % BINS, 1)
+        inside = (lane + offset >= 0) & (lane + offset < BINS)
+        smooth = smooth + jnp.where(inside, moved, 0.0)
+    smooth = smooth / (2 * HALF + 1)
+    level = jnp.sum(amplitude, axis=1, keepdims=True) / BINS
+    divisor = smooth + level + 1e-06
+    white_real = (real_part / divisor).astype(jnp.bfloat16)
+    white_imag = (imag_part / divisor).astype(jnp.bfloat16)
+    return white_real, white_imag
+
+
+def _white_kernel(x_ref, table_ref, taper_ref, out_ref):
+    rows = x_ref.shape[1]
+    white_real, white_imag = _white_block(x_ref[...], table_ref[...], taper_ref[...])
+    for segment in range(SEG):
+        out_ref[2 * segment] = white_real[segment * rows : (segment + 1) * rows]
+        out_ref[2 * segment + 1] = white_imag[segment * rows : (segment + 1) * rows]
+
+
+def _cross_kernel(x_ref, first_ref, table_ref, taper_ref, out_ref):
+    rows = x_ref.shape[1]
+    white_real, white_imag = _white_block(x_ref[...], table_ref[...], taper_ref[...])
+    real_sum = None
+    imag_sum = None
+    for segment in range(SEG):
+        left_real = first_ref[2 * segment].astype(jnp.float32)
+        left_imag = first_ref[2 * segment + 1].astype(jnp.float32)
+        right_real = white_real[segment * rows : (segment + 1) * rows].astype(jnp.float32)
+        right_imag = white_imag[segment * rows : (segment + 1) * rows].astype(jnp.float32)
+        real_term = left_real * right_real + left_imag * right_imag
+        imag_term = left_real * right_imag - left_imag * right_real
+        real_sum = real_term if real_sum is None else real_sum + real_term
+        imag_sum = imag_term if imag_sum is None else imag_sum + imag_term
+    out_ref[:, :BINS] = (real_sum / SEG).astype(out_ref.dtype)
+    out_ref[:, BINS:] = (imag_sum / SEG).astype(out_ref.dtype)
+
+
+def taper_table(slabs_per_segment, width):
+    position = jnp.arange(NFFT, dtype=jnp.int32).astype(jnp.float32)
+    taper = 0.5 - 0.5 * jnp.cos(position * (2.0 * math.pi / NFFT))
+    return taper.reshape(slabs_per_segment, width)
+
+
+def _white_specs(slabs, block, width, per_segment):
+    return [
+        pl.BlockSpec((slabs, block, width), lambda i: (0, i, 0)),
+        pl.BlockSpec((NFFT, 2 * BINS), lambda i: (0, 0), pipeline_mode=pl.Buffered(1)),
+        pl.BlockSpec((per_segment, width), lambda i: (0, 0)),
+    ]
+
+
+def white_rows(parts, table, taper, block=32):
+    slabs, rows, width = parts.shape
+    specs = _white_specs(slabs, block, width, slabs // SEG)
+    return pl.pallas_call(
+        _white_kernel,
+        out_shape=jax.ShapeDtypeStruct((2 * SEG, rows, BINS), jnp.bfloat16),
+        grid=(rows // block,),
+        in_specs=specs,
+        out_specs=pl.BlockSpec((2 * SEG, block, BINS), lambda i: (0, i, 0)),
+        compiler_params=pltpu.CompilerParams(vmem_limit_bytes=48 * 1024 * 1024),
+        cost_estimate=pl.CostEstimate(
+            flops=2 * SEG * rows * NFFT * 2 * BINS, transcendentals=SEG * rows * BINS,
+            bytes_accessed=NFFT * 2 * BINS * 2 + 4 * slabs * rows * width,
+        ),
+    )(parts, table, taper)
+
+
+def cross_rows(parts, first_white, table, taper, block=32):
+    slabs, rows, width = parts.shape
+    specs = _white_specs(slabs, block, width, slabs // SEG)
+    specs.insert(1, pl.BlockSpec((2 * SEG, block, BINS), lambda i: (0, i, 0)))
+    return pl.pallas_call(
+        _cross_kernel,
+        out_shape=jax.ShapeDtypeStruct((rows, 2 * BINS), jnp.bfloat16),
+        grid=(rows // block,),
+        in_specs=specs,
+        out_specs=pl.BlockSpec((block, 2 * BINS), lambda i: (i, 0)),
+        compiler_params=pltpu.CompilerParams(vmem_limit_bytes=48 * 1024 * 1024),
+        cost_estimate=pl.CostEstimate(
+            flops=2 * SEG * rows * NFFT * 2 * BINS, transcendentals=SEG * rows * BINS,
+            bytes_accessed=NFFT * 2 * BINS * 2 + 8 * slabs * rows * width,
+        ),
+    )(parts, first_white, table, taper)
 
 
 def to_rows(parts):
@@ -145,7 +243,9 @@
 
     first_parts = pick_rows(records, firsts.reshape(-1)).reshape(slabs, pair_count, width)
     first_arrived = lax.all_to_all(first_parts, "slab", split_axis=0, concat_axis=0, tiled=True)
-    first_rows = whitened(to_rows(first_arrived))
+    table = dft_table()
+    taper = taper_table(slabs // SEG, width)
+    first_white = white_rows(first_arrived, table, taper)
 
     asked = lax.all_to_all(plane_requests, "region", split_axis=1, concat_axis=1, tiled=True)
     served = pick_rows(records, jnp.transpose(asked, (1, 0, 2)).reshape(-1))
@@ -153,8 +253,7 @@
     arrived = lax.all_to_all(served, "region", split_axis=0, concat_axis=0, tiled=True)
     second_parts = compact_rows(arrived.reshape(regions, slabs, capacity, width), slots)
     second_arrived = lax.all_to_all(second_parts, "slab", split_axis=0, concat_axis=0, tiled=True)
-    second_rows = whitened(to_rows(second_arrived))
-    return cross(first_rows, second_rows)
+    return cross_rows(second_arrived, first_white, table, taper)
 
 
 def solution(mesh):

time: 268 us -> 244 us (0.910)
  blocking collectives: 27.9 us -> 52.1 us
  local copies, waits for them, and re-layouts: 31 us -> 9.68 us
  starting transfers between devices: 39.3 us -> 18.1 us
  other arithmetic: 39.1 us -> 21.3 us
  waiting for transfers between devices: 74.2 us -> 89.9 us
  matrix products: 12.8 us -> 0 us
  Pallas kernels: 41.5 us -> 52.3 us
    pallas_call x0 -> x2, Pallas kernels: none -> 26 us  [the longest x1 13.5 us: cross_rows(): pl.pallas_call(_cross_kernel, out_shape=jax.ShapeDtypeStruct((rows, 2 * B...]
    all_to_all x0 -> x1, blocking collectives: none -> 24.2 us  [local(): lax.all_to_all(plane_requests, 'region', split_axis=1, concat_axis=1, til...]
    convert_element_type x6 -> x0, local copies, waits for them, and re-layouts: 17.6 us -> none  [the longest x4 10.6 us: whitened(): signal = traces.astype(jnp.float32).reshape(count * SEG, NFFT)]
    pallas_call x1, Pallas kernels: 19.2 us -> 3.98 us  [compact_rows(): pl.pallas_call(_compact_kernel, out_shape=jax.ShapeDtypeStruct((slabs, pa...]
    all_to_all x1, waiting for transfers between devices: 67.8 us -> 81.9 us  [local(): lax.all_to_all(served, 'region', split_axis=0, concat_axis=0, tiled=True)]
    reduce_sum x7 -> x0, other arithmetic: 13.3 us -> none  [the longest x1 10.5 us: cross(): jnp.mean(left[..., 0, :] * right[..., 0, :] + left[..., 1, :] * right[......]
    all_to_all x1 -> x0, starting transfers between devices: 12.8 us -> none  [local(): lax.all_to_all(plane_requests, 'region', split_axis=1, concat_axis=1, til...]
    dot_general x2 -> x0, matrix products: 12.8 us -> none  [whitened(): spectrum = jnp.dot(tapered, dft_table(), preferred_element_type=jnp.float32)]
  transfers between devices with their start and end apart: 4 -> 3, of which waited for: 3 -> 2; matrix products, arithmetic and copies ran while one was open for 16% -> 9% of each run, Pallas kernels for 8% -> 10%
where the time goes in v3:
time: 244 us; the launch traced here: 243 us
  waiting for transfers between devices  89.9 us (37%)
  Pallas kernels  52.3 us (21%)
  blocking collectives  52.1 us (21%)
  other arithmetic  21.3 us (9%)
  starting transfers between devices  18.1 us (7%)
  local copies, waits for them, and re-layouts  9.68 us (4%)
    all_to_all x1, waiting for transfers between devices, local(): lax.all_to_all(served, 'region', split_axis=0, concat_axis=0, tiled=True)  81.9 us
    all_gather x1, blocking collectives, local(): plane = lax.all_gather(packed, 'slab', axis=0, tiled=False)  27.9 us
    all_to_all x1, blocking collectives, local(): lax.all_to_all(plane_requests, 'region', split_axis=1, concat_axis=1, til...  24.2 us
    pallas_call x2, Pallas kernels, pick_rows(): pl.pallas_call(_pick_kernel, out_shape=jax.ShapeDtypeStruct((count, width...  22.2 us
    pallas_call x1, Pallas kernels, cross_rows(): pl.pallas_call(_cross_kernel, out_shape=jax.ShapeDtypeStruct((rows, 2 * B...  13.5 us
    pallas_call x1, Pallas kernels, white_rows(): pl.pallas_call(_white_kernel, out_shape=jax.ShapeDtypeStruct((2 * SEG, ro...  12.5 us
    all_to_all x1, starting transfers between devices, local(): lax.all_to_all(first_parts, 'slab', split_axis=0, concat_axis=0, tiled=True)  10.4 us
    concatenate x1, other arithmetic, dft_table(): return jnp.concatenate([cos_part, -sin_part], axis=1).astype(jnp.bfloat16)  8.15 us
  transfers between devices with their start and end apart: 3, of which 2 were waited for; matrix products, arithmetic and copies ran while one was open for 9% of the time, Pallas kernels for 10%

profile of v3, /device:TPU:1, one launch (start us, length us, event | category | flops | bytes accessed | tf_op | source)
XLA Modules:
  0.0 243.4 jit_solution(17100510057074578765)
XLA Ops:
  0.0 0.7 fusion.16
  0.7 0.2 reduce_window_sum.11
  0.9 0.8 select_reduce_fusion
  1.7 0.7 fusion.17
  2.4 0.7 multiply_add_fusion
  3.1 1.1 scatter_custom_fusion
  4.2 0.7 pad_add_fusion
  4.9 27.9 %all-gather.1 = s32[32,1,512]{2,1,0:T(1,128)S(1)} all-gather(s32[1,1,512]{2,1,0:T(1,128)S(1)} %bitcast.35), channel_id=2, replica_groups=mesh['region'=16,'slab'=32] {'slab'}, dimensions={0}, use_global_device_ids=true | all-gather | bytes 67584 | tf_op jit(solution)/shard_map/all_gather | solution.py:239
  32.7 0.1 copy.11
  32.8 0.1 reshape.126
  33.0 24.2 %all_to_all.20 = s32[16,1,512]{2,1,0:T(1,128)S(1)} all-to-all(s32[16,1,512]{2,1,0:T(1,128)S(1)} %reshape.126), channel_id=1, replica_groups=mesh['region'=16,'slab'=32] {'region'}, dimensions={0} | all-to-all | bytes 65536 | tf_op jit(solution)/shard_map/all_to_all | solution.py:250
  57.2 0.5 broadcast.148
  57.7 0.7 reduce
  58.4 0.1 reshape.127
  58.5 0.1 copy.12
  58.7 3.6 %reshape_reshape.8.ids_ref = s32[8192,1]{1,0:T(8,128)} reshape(s32[16,32,16]{2,1,0:T(8,128)S(1)} %copy.12) | data formatting | bytes 65536 | tf_op jit(solution)/shard_map/reshape;reshape | solution.py:88
  62.3 14.4 %shard_map.46 = bf16[8192,128]{1,0:T(8,128)(2,1)} custom-call(s32[8192,1]{1,0:T(8,128)} %reshape_reshape.8.ids_ref, bf16[1024,128]{1,0:T(8,128)(2,1)} %table_ref.3), custom_call_target="tpu_custom_call" | custom-call | flops 2147483648 | bytes 2359296 | tf_op jit(solution)/shard_map/pallas_call | solution.py:76
  76.7 3.7 %all-to-all-start.1 = ((bf16[16,512,128]{2,1,0:T(8,128)(2,1)}), bf16[16,512,128]{2,1,0:T(8,128)(2,1)S(1)}, u32[]{:S(2)}, u32[]{:S(2)}) async-start(bf16[16,512,128]{2,1,0:T(8,128)(2,1)} %bitcast.29), calls=%async_computation.1 | async-start | bytes 4194304 | tf_op jit(solution)/shard_map/all_to_all | solution.py:253
  80.4 2.0 copy.15.ids_ref
  82.4 7.8 %shard_map.48 = bf16[4096,128]{1,0:T(8,128)(2,1)} custom-call(s32[4096,1]{1,0:T(8,128)} %copy.15.ids_ref, bf16[1024,128]{1,0:T(8,128)(2,1)} %table_ref.3), custom_call_target="tpu_custom_call" | custom-call | flops 1073741824 | bytes 1310720 | tf_op jit(solution)/shard_map/pallas_call | solution.py:76
  90.2 81.9 %all-to-all-done.1 = bf16[16,512,128]{2,1,0:T(8,128)(2,1)S(1)} async-done(((bf16[16,512,128]{2,1,0:T(8,128)(2,1)}), bf16[16,512,128]{2,1,0:T(8,128)(2,1)S(1)}, u32[]{:S(2)}, u32[]{:S(2)}) %all-to-all-start.1) | async-done | bytes 2097184 | tf_op jit(solution)/shard_map/all_to_all | solution.py:253
  172.1 0.0 copy-start
  172.1 10.4 %all-to-all-start.3 = ((bf16[32,128,128]{2,1,0:T(8,128)(2,1)}), bf16[32,128,128]{2,1,0:T(8,128)(2,1)S(1)}, u32[]{:S(2)}, u32[]{:S(2)}) async-start(bf16[32,128,128]{2,1,0:T(8,128)(2,1)} %bitcast.30), calls=%async_computation.3 | async-start | bytes 2097152 | tf_op jit(solution)/shard_map/all_to_all | solution.py:245
  182.5 2.0 copy.14.ids_ref
  184.5 1.2 fusion.14
  185.7 1.7 fusion.9
  187.4 0.0 copy-done
  187.4 4.0 %shard_map.47 = bf16[32,128,128]{2,1,0:T(8,128)(2,1)} custom-call(s32[32,128,1]{2,1,0:T(8,128)} %copy.14.ids_ref, bf16[16,32,16,128]{3,2,1,0:T(8,128)(2,1)} %bitcast.28), custom_call_target="tpu_custom_call" | custom-call | flops 268435456 | bytes 3145728 | tf_op jit(solution)/shard_map/pallas_call | solution.py:103
  191.4 8.0 %all-to-all-done.3.x_ref = bf16[32,128,128]{2,1,0:T(8,128)(2,1)S(1)} async-done(((bf16[32,128,128]{2,1,0:T(8,128)(2,1)}), bf16[32,128,128]{2,1,0:T(8,128)(2,1)S(1)}, u32[]{:S(2)}, u32[]{:S(2)}) %all-to-all-start.3) | async-done | bytes 1048608 | tf_op jit(solution)/shard_map/all_to_all | solution.py:245
  199.4 4.0 %all-to-all-start.2 = ((bf16[32,128,128]{2,1,0:T(8,128)(2,1)}), bf16[32,128,128]{2,1,0:T(8,128)(2,1)S(1)}, u32[]{:S(2)}, u32[]{:S(2)}) async-start(bf16[32,128,128]{2,1,0:T(8,128)(2,1)} %shard_map.47), calls=%async_computation.2 | async-start | bytes 2097152 | tf_op jit(solution)/shard_map/all_to_all | solution.py:255
  203.4 5.8 %subtract_convert_fusion = (bf16[32,64,1024]{2,1,0:T(8,128)(2,1)}, bf16[32,64,1024]{2,1,0:T(8,128)(2,1)}) fusion(f32[64,1024]{1,0:T(8,128)S(1)} %get-tuple-element.9, f32[32,1024]{1,0:T(8,128)S(1)} %get-tuple-element.11, f32[64,1024]{1,0:T(8,128)} %get-tuple-element.10, f32[32,1024]{1,0:T(8,128)} %get-tuple-element.12), kind=kLoop, calls=%fused_computation.3 | loop fusion | flops 18874368 | bytes 9175040 | tf_op jit(solution)/shard_map/convert.3
  209.2 0.1 multiply_subtract_fusion.taper_ref
  209.2 8.1 %pad_maximum_fusion.table_ref = bf16[2048,2048]{1,0:T(8,128)(2,1)} fusion(bf16[2048,1024]{1,0:T(8,128)(2,1)} %bitcast.27, bf16[2048,1024]{1,0:T(8,128)(2,1)} %bitcast.26), kind=kLoop, calls=%fused_computation.1 | loop fusion | flops 16777216 | bytes 16777216 | tf_op jit(solution)/shard_map/concatenate | solution.py:28
  217.4 12.5 %shard_map.49.first_ref = bf16[4,128,1024]{2,1,0:T(8,128)(2,1)S(1)} custom-call(bf16[32,128,128]{2,1,0:T(8,128)(2,1)S(1)} %all-to-all-done.3.x_ref, bf16[2048,2048]{1,0:T(8,128)(2,1)} %pad_maximum_fusion.table_ref, f32[16,128]{1,0:T(8,128)S(1)} %multiply_subtract_fusion.taper_ref), custom_call_target="tpu_custom_call" | custom-call | flops 2147483648 | bytes 10485760 | tf_op jit(solution)/shard_map/pallas_call | solution.py:185
  229.9 0.0 all-to-all-done.2.x_ref
  229.9 13.5 %shard_map.50 = bf16[128,2048]{1,0:T(8,128)(2,1)} custom-call(bf16[32,128,128]{2,1,0:T(8,128)(2,1)S(1)} %all-to-all-done.2.x_ref, bf16[4,128,1024]{2,1,0:T(8,128)(2,1)S(1)} %shard_map.49.first_ref, bf16[2048,2048]{1,0:T(8,128)(2,1)} %pad_maximum_fusion.table_ref, f32[16,128]{1,0:T(8,128)S(1)} %multiply_subtract_fusion.taper_ref), custom_call_target="tpu_custom_call" | custom-call | flops 2147483648 | bytes 12582912 | tf_op jit(solution)/shard_map/pallas_call | solution.py:203
  (4 shorter events, 0.0 us)
Async XLA Ops:
  76.7 95.4 %all-to-all-start.1 = ((bf16[16,512,128]{2,1,0:T(8,128)(2,1)}), bf16[16,512,128]{2,1,0:T(8,128)(2,1)S(1)}, u32[]{:S(2)}, u32[]{:S(2)}) async-start(bf16[16,512,128]{2,1,0:T(8,128)(2,1)} %bitcast.29), calls=%async_computation.1 | async-start | bytes 4194304 | tf_op jit(solution)/shard_map/all_to_all | solution.py:253
  172.1 15.3 %copy-start = (bf16[16,512,128]{2,1,0:T(8,128)(2,1)}, bf16[16,512,128]{2,1,0:T(8,128)(2,1)S(1)}, u32[]{:S(2)}) copy-start(bf16[16,512,128]{2,1,0:T(8,128)(2,1)S(1)} %all-to-all-done.1) | copy-start | bytes 6291460
  172.1 27.3 %all-to-all-start.3 = ((bf16[32,128,128]{2,1,0:T(8,128)(2,1)}), bf16[32,128,128]{2,1,0:T(8,128)(2,1)S(1)}, u32[]{:S(2)}, u32[]{:S(2)}) async-start(bf16[32,128,128]{2,1,0:T(8,128)(2,1)} %bitcast.30), calls=%async_computation.3 | async-start | bytes 2097152 | tf_op jit(solution)/shard_map/all_to_all | solution.py:245
  199.4 30.5 %all-to-all-start.2 = ((bf16[32,128,128]{2,1,0:T(8,128)(2,1)}), bf16[32,128,128]{2,1,0:T(8,128)(2,1)S(1)}, u32[]{:S(2)}, u32[]{:S(2)}) async-start(bf16[32,128,128]{2,1,0:T(8,128)(2,1)} %shard_map.47), calls=%async_computation.2 | async-start | bytes 2097152 | tf_op jit(solution)/shard_map/all_to_all | solution.py:255

commit v4 on v3

--- a/solution.py
+++ b/solution.py
@@ -214,6 +214,51 @@
     )(parts, first_white, table, taper)
 
 
+def _slab_exchange_kernel(x_ref, out_ref, landed, send_sems, recv_sems):
+    slabs = x_ref.shape[0]
+    region = lax.axis_index("region")
+    me = lax.axis_index("slab")
+    barrier = pltpu.get_barrier_semaphore()
+    for step in range(1, slabs):
+        pl.semaphore_signal(
+            barrier, inc=1, device_id=(region, lax.rem(me + step, slabs)), device_id_type=pl.DeviceIdType.MESH
+        )
+    pl.semaphore_wait(barrier, slabs - 1)
+    copies = []
+    for step in range(1, slabs):
+        peer = lax.rem(me + step, slabs)
+        copy = pltpu.make_async_remote_copy(
+            src_ref=x_ref.at[peer],
+            dst_ref=landed.at[me],
+            send_sem=send_sems.at[step],
+            recv_sem=recv_sems.at[step],
+            device_id=(region, peer),
+            device_id_type=pl.DeviceIdType.MESH,
+        )
+        copy.start()
+        copies.append(copy)
+    landed[me] = x_ref[me]
+    for copy in copies:
+        copy.wait_send()
+        copy.wait_recv()
+    out_ref[...] = landed[...]
+
+
+def slab_exchange(parts, collective):
+    slabs = parts.shape[0]
+    return pl.pallas_call(
+        _slab_exchange_kernel,
+        out_shape=jax.ShapeDtypeStruct(parts.shape, parts.dtype),
+        scratch_shapes=[
+            pltpu.VMEM(parts.shape, parts.dtype),
+            pltpu.SemaphoreType.DMA((slabs,)),
+            pltpu.SemaphoreType.DMA((slabs,)),
+        ],
+        compiler_params=pltpu.CompilerParams(collective_id=collective, has_side_effects=True),
+        cost_estimate=pl.CostEstimate(flops=0, transcendentals=0, bytes_accessed=4 * parts.size),
+    )(parts)
+
+
 def to_rows(parts):
     slabs, rows, width = parts.shape
     return jnp.transpose(parts, (1, 0, 2)).reshape(rows, slabs * width)
@@ -242,7 +287,7 @@
     plane_requests = plane[:, 2 * pair_count :].reshape(slabs, regions, capacity)
 
     first_parts = pick_rows(records, firsts.reshape(-1)).reshape(slabs, pair_count, width)
-    first_arrived = lax.all_to_all(first_parts, "slab", split_axis=0, concat_axis=0, tiled=True)
+    first_arrived = slab_exchange(first_parts, 0)
     table = dft_table()
     taper = taper_table(slabs // SEG, width)
     first_white = white_rows(first_arrived, table, taper)
@@ -252,7 +297,7 @@
     served = served.reshape(regions, slabs * capacity, width)
     arrived = lax.all_to_all(served, "region", split_axis=0, concat_axis=0, tiled=True)
     second_parts = compact_rows(arrived.reshape(regions, slabs, capacity, width), slots)
-    second_arrived = lax.all_to_all(second_parts, "slab", split_axis=0, concat_axis=0, tiled=True)
+    second_arrived = slab_exchange(second_parts, 1)
     return cross_rows(second_arrived, first_white, table, taper)
 
 

time: 244 us -> 223 us (0.914); the launches traced: 243 us -> 218 us
  waiting for transfers between devices: 89.9 us -> 30 us
  Pallas kernels: 52.3 us -> 101 us
  starting transfers between devices: 18.1 us -> 4.6 us
    all_to_all x1, waiting for transfers between devices: 81.9 us -> 30 us  [local(): lax.all_to_all(served, 'region', split_axis=0, concat_axis=0, tiled=True)]
    pallas_call x0 -> x2, Pallas kernels: none -> 49.3 us  [slab_exchange(): pl.pallas_call(_slab_exchange_kernel, out_shape=jax.ShapeDtypeStruct(part...]
    all_to_all x2 -> x0, starting transfers between devices: 14.3 us -> none  [the longest x1 10.4 us: local(): lax.all_to_all(first_parts, 'slab', split_axis=0, concat_axis=0, tiled=True)]
    all_to_all x2 -> x0, waiting for transfers between devices: 8.02 us -> none  [the longest x1 8.02 us: local(): lax.all_to_all(first_parts, 'slab', split_axis=0, concat_axis=0, tiled=True)]
  transfers between devices with their start and end apart: 3 -> 1, of which waited for: 2 -> 1; matrix products, arithmetic and copies ran while one was open for 9% -> 9% of each run, Pallas kernels for 10% -> 20%
where the time goes in v4:
time: 223 us; the launch traced here: 218 us
  Pallas kernels  101 us (45%)
  blocking collectives  52.1 us (23%)
  waiting for transfers between devices  30 us (13%)
  other arithmetic  19.3 us (9%)
  local copies, waits for them, and re-layouts  10.9 us (5%)
  starting transfers between devices  4.6 us (2%)
    pallas_call x2, Pallas kernels, slab_exchange(): pl.pallas_call(_slab_exchange_kernel, out_shape=jax.ShapeDtypeStruct(part...  49.3 us
    all_to_all x1, waiting for transfers between devices, local(): lax.all_to_all(served, 'region', split_axis=0, concat_axis=0, tiled=True)  30 us
    all_gather x1, blocking collectives, local(): plane = lax.all_gather(packed, 'slab', axis=0, tiled=False)  27.9 us
    all_to_all x1, blocking collectives, local(): lax.all_to_all(plane_requests, 'region', split_axis=1, concat_axis=1, til...  24.2 us
    pallas_call x2, Pallas kernels, pick_rows(): pl.pallas_call(_pick_kernel, out_shape=jax.ShapeDtypeStruct((count, width...  22.2 us
    pallas_call x1, Pallas kernels, cross_rows(): pl.pallas_call(_cross_kernel, out_shape=jax.ShapeDtypeStruct((rows, 2 * B...  13.5 us
    pallas_call x1, Pallas kernels, white_rows(): pl.pallas_call(_white_kernel, out_shape=jax.ShapeDtypeStruct((2 * SEG, ro...  12.5 us
    concatenate x1, other arithmetic, dft_table(): return jnp.concatenate([cos_part, -sin_part], axis=1).astype(jnp.bfloat16)  8.22 us
  transfers between devices with their start and end apart: 1, of which 1 were waited for; matrix products, arithmetic and copies ran while one was open for 9% of the time, Pallas kernels for 20%

profile of v4, /device:TPU:1, one launch (start us, length us, event | category | flops | bytes accessed | tf_op | source)
XLA Modules:
  0.0 218.4 jit_solution(1237817687900774159)
XLA Ops:
  0.0 0.7 fusion.16
  0.7 0.2 reduce_window_sum.11
  0.9 0.8 select_reduce_fusion
  1.7 0.7 fusion.17
  2.4 0.7 multiply_add_fusion
  3.1 1.1 scatter_custom_fusion
  4.2 0.7 pad_add_fusion
  4.9 27.9 %all-gather.1 = s32[32,1,512]{2,1,0:T(1,128)S(1)} all-gather(s32[1,1,512]{2,1,0:T(1,128)S(1)} %bitcast.34), channel_id=2, replica_groups=mesh['region'=16,'slab'=32] {'slab'}, dimensions={0}, use_global_device_ids=true | all-gather | bytes 67584 | tf_op jit(solution)/shard_map/all_gather | solution.py:284
  32.7 0.1 copy.11
  32.8 0.1 reshape.126
  33.0 24.2 %all_to_all.10 = s32[16,1,512]{2,1,0:T(1,128)S(1)} all-to-all(s32[16,1,512]{2,1,0:T(1,128)S(1)} %reshape.126), channel_id=1, replica_groups=mesh['region'=16,'slab'=32] {'region'}, dimensions={0} | all-to-all | bytes 65536 | tf_op jit(solution)/shard_map/all_to_all | solution.py:295
  57.2 0.5 broadcast.148
  57.7 0.7 reduce
  58.4 0.1 reshape.127
  58.5 0.1 copy.12
  58.7 3.6 %reshape_reshape.8.ids_ref = s32[8192,1]{1,0:T(8,128)} reshape(s32[16,32,16]{2,1,0:T(8,128)S(1)} %copy.12) | data formatting | bytes 65536 | tf_op jit(solution)/shard_map/reshape;reshape | solution.py:88
  62.3 14.4 %shard_map.46 = bf16[8192,128]{1,0:T(8,128)(2,1)} custom-call(s32[8192,1]{1,0:T(8,128)} %reshape_reshape.8.ids_ref, bf16[1024,128]{1,0:T(8,128)(2,1)} %table_ref.3), custom_call_target="tpu_custom_call" | custom-call | flops 2147483648 | bytes 2359296 | tf_op jit(solution)/shard_map/pallas_call | solution.py:76
  76.6 4.6 %all-to-all-start.1 = ((bf16[16,512,128]{2,1,0:T(8,128)(2,1)}), bf16[16,512,128]{2,1,0:T(8,128)(2,1)}, u32[]{:S(2)}, u32[]{:S(2)}) async-start(bf16[16,512,128]{2,1,0:T(8,128)(2,1)} %bitcast.28), calls=%async_computation.1 | async-start | bytes 4194304 | tf_op jit(solution)/shard_map/all_to_all | solution.py:298
  81.3 2.0 copy.15.ids_ref
  83.3 7.8 %shard_map.49 = bf16[4096,128]{1,0:T(8,128)(2,1)} custom-call(s32[4096,1]{1,0:T(8,128)} %copy.15.ids_ref, bf16[1024,128]{1,0:T(8,128)(2,1)} %table_ref.3), custom_call_target="tpu_custom_call" | custom-call | flops 1073741824 | bytes 1310720 | tf_op jit(solution)/shard_map/pallas_call | solution.py:76
  91.1 22.3 %shard_map.50.x_ref = bf16[32,128,128]{2,1,0:T(8,128)(2,1)} custom-call(bf16[32,128,128]{2,1,0:T(8,128)(2,1)} %bitcast.29), custom_call_target="tpu_custom_call" | custom-call | bytes 2097152 | tf_op jit(solution)/shard_map/pallas_call | solution.py:249
  113.4 2.0 copy.14.ids_ref
  115.4 0.1 multiply_subtract_fusion.taper_ref
  115.5 0.5 fusion.14
  116.0 1.0 fusion.9
  117.0 5.0 %subtract_convert_fusion = (bf16[32,64,1024]{2,1,0:T(8,128)(2,1)}, bf16[32,64,1024]{2,1,0:T(8,128)(2,1)}) fusion(f32[64,1024]{1,0:T(8,128)S(1)} %get-tuple-element.9, f32[32,1024]{1,0:T(8,128)S(1)} %get-tuple-element.11, f32[64,1024]{1,0:T(8,128)S(1)} %get-tuple-element.10, f32[32,1024]{1,0:T(8,128)S(1)} %get-tuple-element.12), kind=kLoop, calls=%fused_computation.3 | loop fusion | flops 18874368 | bytes 9175040 | tf_op jit(solution)/shard_map/convert.3
  122.0 0.0 copy-start
  122.0 8.2 %pad_maximum_fusion.table_ref = bf16[2048,2048]{1,0:T(8,128)(2,1)} fusion(bf16[2048,1024]{1,0:T(8,128)(2,1)} %bitcast.27, bf16[2048,1024]{1,0:T(8,128)(2,1)} %bitcast.26), kind=kLoop, calls=%fused_computation.1 | loop fusion | flops 16777216 | bytes 16777216 | tf_op jit(solution)/shard_map/concatenate | solution.py:28
  130.2 0.0 copy-done
  130.2 12.5 %shard_map.51.first_ref = bf16[4,128,1024]{2,1,0:T(8,128)(2,1)S(1)} custom-call(bf16[32,128,128]{2,1,0:T(8,128)(2,1)S(1)} %copy-done, bf16[2048,2048]{1,0:T(8,128)(2,1)} %pad_maximum_fusion.table_ref, f32[16,128]{1,0:T(8,128)S(1)} %multiply_subtract_fusion.taper_ref), custom_call_target="tpu_custom_call" | custom-call | flops 2147483648 | bytes 10485760 | tf_op jit(solution)/shard_map/pallas_call | solution.py:185
  142.8 30.0 %all-to-all-done.1 = bf16[16,512,128]{2,1,0:T(8,128)(2,1)} async-done(((bf16[16,512,128]{2,1,0:T(8,128)(2,1)}), bf16[16,512,128]{2,1,0:T(8,128)(2,1)}, u32[]{:S(2)}, u32[]{:S(2)}) %all-to-all-start.1) | async-done | bytes 2097184 | tf_op jit(solution)/shard_map/all_to_all | solution.py:298
  172.8 4.0 %shard_map.47.x_ref = bf16[32,128,128]{2,1,0:T(8,128)(2,1)} custom-call(s32[32,128,1]{2,1,0:T(8,128)} %copy.14.ids_ref, bf16[16,32,16,128]{3,2,1,0:T(8,128)(2,1)} %bitcast.8.table_ref), custom_call_target="tpu_custom_call" | custom-call | flops 268435456 | bytes 3145728 | tf_op jit(solution)/shard_map/pallas_call | solution.py:103
  176.8 26.9 %shard_map.48.x_ref = bf16[32,128,128]{2,1,0:T(8,128)(2,1)} custom-call(bf16[32,128,128]{2,1,0:T(8,128)(2,1)} %shard_map.47.x_ref), custom_call_target="tpu_custom_call" | custom-call | bytes 2097152 | tf_op jit(solution)/shard_map/pallas_call | solution.py:249
  203.7 0.0 copy-start.1
  203.8 1.2 copy-done.1
  205.0 13.5 %shard_map.52 = bf16[128,2048]{1,0:T(8,128)(2,1)} custom-call(bf16[32,128,128]{2,1,0:T(8,128)(2,1)S(1)} %copy-done.1, bf16[4,128,1024]{2,1,0:T(8,128)(2,1)S(1)} %shard_map.51.first_ref, bf16[2048,2048]{1,0:T(8,128)(2,1)} %pad_maximum_fusion.table_ref, f32[16,128]{1,0:T(8,128)S(1)} %multiply_subtract_fusion.taper_ref), custom_call_target="tpu_custom_call" | custom-call | flops 2147483648 | bytes 12582912 | tf_op jit(solution)/shard_map/pallas_call | solution.py:203
  (4 shorter events, 0.0 us)
Async XLA Ops:
  76.6 96.2 %all-to-all-start.1 = ((bf16[16,512,128]{2,1,0:T(8,128)(2,1)}), bf16[16,512,128]{2,1,0:T(8,128)(2,1)}, u32[]{:S(2)}, u32[]{:S(2)}) async-start(bf16[16,512,128]{2,1,0:T(8,128)(2,1)} %bitcast.28), calls=%async_computation.1 | async-start | bytes 4194304 | tf_op jit(solution)/shard_map/all_to_all | solution.py:298
  122.0 8.2 %copy-start = (bf16[32,128,128]{2,1,0:T(8,128)(2,1)S(1)}, bf16[32,128,128]{2,1,0:T(8,128)(2,1)}, u32[]{:S(2)}) copy-start(bf16[32,128,128]{2,1,0:T(8,128)(2,1)} %shard_map.50.x_ref) | copy-start | bytes 3145732
  203.7 1.2 copy-start.1

commit v5 on v4

--- a/solution.py
+++ b/solution.py
@@ -1,3 +1,4 @@
+import functools
 import math
 
 import jax
@@ -214,25 +215,28 @@
     )(parts, first_white, table, taper)
 
 
-def _slab_exchange_kernel(x_ref, out_ref, landed, send_sems, recv_sems):
-    slabs = x_ref.shape[0]
-    region = lax.axis_index("region")
-    me = lax.axis_index("slab")
+def _exchange_kernel(axis, x_ref, out_ref, landed, send_sems, recv_sems):
+    count = x_ref.shape[0]
+    me = lax.axis_index(axis)
+
+    def peer_id(peer):
+        return {axis: peer}
+
     barrier = pltpu.get_barrier_semaphore()
-    for step in range(1, slabs):
+    for step in range(1, count):
         pl.semaphore_signal(
-            barrier, inc=1, device_id=(region, lax.rem(me + step, slabs)), device_id_type=pl.DeviceIdType.MESH
+            barrier, inc=1, device_id=peer_id(lax.rem(me + step, count)), device_id_type=pl.DeviceIdType.MESH
         )
-    pl.semaphore_wait(barrier, slabs - 1)
+    pl.semaphore_wait(barrier, count - 1)
     copies = []
-    for step in range(1, slabs):
-        peer = lax.rem(me + step, slabs)
+    for step in range(1, count):
+        peer = lax.rem(me + step, count)
         copy = pltpu.make_async_remote_copy(
             src_ref=x_ref.at[peer],
             dst_ref=landed.at[me],
             send_sem=send_sems.at[step],
             recv_sem=recv_sems.at[step],
-            device_id=(region, peer),
+            device_id=peer_id(peer),
             device_id_type=pl.DeviceIdType.MESH,
         )
         copy.start()
@@ -244,15 +248,15 @@
     out_ref[...] = landed[...]
 
 
-def slab_exchange(parts, collective):
-    slabs = parts.shape[0]
-    return pl.pallas_call(
-        _slab_exchange_kernel,
+def exchange(parts, axis, collective):
+    count = parts.shape[0]
+    return pl.pallas_call(
+        functools.partial(_exchange_kernel, axis),
         out_shape=jax.ShapeDtypeStruct(parts.shape, parts.dtype),
         scratch_shapes=[
             pltpu.VMEM(parts.shape, parts.dtype),
-            pltpu.SemaphoreType.DMA((slabs,)),
-            pltpu.SemaphoreType.DMA((slabs,)),
+            pltpu.SemaphoreType.DMA((count,)),
+            pltpu.SemaphoreType.DMA((count,)),
         ],
         compiler_params=pltpu.CompilerParams(collective_id=collective, has_side_effects=True),
         cost_estimate=pl.CostEstimate(flops=0, transcendentals=0, bytes_accessed=4 * parts.size),
@@ -287,17 +291,19 @@
     plane_requests = plane[:, 2 * pair_count :].reshape(slabs, regions, capacity)
 
     first_parts = pick_rows(records, firsts.reshape(-1)).reshape(slabs, pair_count, width)
-    first_arrived = slab_exchange(first_parts, 0)
+    first_arrived = exchange(first_parts, "slab", 0)
     table = dft_table()
     taper = taper_table(slabs // SEG, width)
     first_white = white_rows(first_arrived, table, taper)
 
-    asked = lax.all_to_all(plane_requests, "region", split_axis=1, concat_axis=1, tiled=True)
-    served = pick_rows(records, jnp.transpose(asked, (1, 0, 2)).reshape(-1))
+    outgoing = jnp.transpose(plane_requests, (1, 0, 2)).reshape(regions, -1, 128)
+    outgoing = jnp.pad(outgoing, ((0, 0), (0, (-outgoing.shape[1]) % 8), (0, 0)))
+    asked = exchange(outgoing, "region", 1)[:, : slabs * capacity // 128].reshape(-1)
+    served = pick_rows(records, asked)
     served = served.reshape(regions, slabs * capacity, width)
     arrived = lax.all_to_all(served, "region", split_axis=0, concat_axis=0, tiled=True)
     second_parts = compact_rows(arrived.reshape(regions, slabs, capacity, width), slots)
-    second_arrived = slab_exchange(second_parts, 1)
+    second_arrived = lax.all_to_all(second_parts, "slab", split_axis=0, concat_axis=0, tiled=True)
     return cross_rows(second_arrived, first_white, table, taper)
 
 

time: 223 us -> 256 us (1.15)
  waiting for transfers between devices: 30 us -> 81.3 us
  blocking collectives: 52.1 us -> 27.9 us
  starting transfers between devices: 4.6 us -> 20.2 us
  Pallas kernels: 101 us -> 94.2 us
    all_to_all x1, waiting for transfers between devices: 30 us -> 81.3 us  [local(): lax.all_to_all(served, 'region', split_axis=0, concat_axis=0, tiled=True)]
    all_to_all x1 -> x0, blocking collectives: 24.2 us -> none  [local(): lax.all_to_all(plane_requests, 'region', split_axis=1, concat_axis=1, til...]
    all_to_all x0 -> x1, starting transfers between devices: none -> 10.3 us  [local(): lax.all_to_all(second_parts, 'slab', split_axis=0, concat_axis=0, tiled=T...]
    pallas_call x2, Pallas kernels: 49.3 us -> 42 us  [exchange(): pl.pallas_call(functools.partial(_exchange_kernel, axis), out_shape=jax.S...]
    all_to_all x1, starting transfers between devices: 4.6 us -> 9.98 us  [local(): lax.all_to_all(served, 'region', split_axis=0, concat_axis=0, tiled=True)]
  transfers between devices with their start and end apart: 1 -> 2, of which waited for: 1 -> 1; matrix products, arithmetic and copies ran while one was open for 9% -> 7% of each run, Pallas kernels for 20% -> 17%
where the time goes in v5:
time: 256 us; the launch traced here: 253 us
  Pallas kernels  94.2 us (37%)
  waiting for transfers between devices  81.3 us (32%)
  blocking collectives  27.9 us (11%)
  starting transfers between devices  20.2 us (8%)
  other arithmetic  18.6 us (7%)
  local copies, waits for them, and re-layouts  10.8 us (4%)
    all_to_all x1, waiting for transfers between devices, local(): lax.all_to_all(served, 'region', split_axis=0, concat_axis=0, tiled=True)  81.3 us
    pallas_call x2, Pallas kernels, exchange(): pl.pallas_call(functools.partial(_exchange_kernel, axis), out_shape=jax.S...  42 us
    all_gather x1, blocking collectives, local(): plane = lax.all_gather(packed, 'slab', axis=0, tiled=False)  27.9 us
    pallas_call x2, Pallas kernels, pick_rows(): pl.pallas_call(_pick_kernel, out_shape=jax.ShapeDtypeStruct((count, width...  22.2 us
    pallas_call x1, Pallas kernels, cross_rows(): pl.pallas_call(_cross_kernel, out_shape=jax.ShapeDtypeStruct((rows, 2 * B...  13.5 us
    pallas_call x1, Pallas kernels, white_rows(): pl.pallas_call(_white_kernel, out_shape=jax.ShapeDtypeStruct((2 * SEG, ro...  12.5 us
    all_to_all x1, starting transfers between devices, local(): lax.all_to_all(second_parts, 'slab', split_axis=0, concat_axis=0, tiled=T...  10.3 us
    all_to_all x1, starting transfers between devices, local(): lax.all_to_all(served, 'region', split_axis=0, concat_axis=0, tiled=True)  9.98 us
  transfers between devices with their start and end apart: 2, of which 1 were waited for; matrix products, arithmetic and copies ran while one was open for 7% of the time, Pallas kernels for 17%

profile of v5, /device:TPU:1, one launch (start us, length us, event | category | flops | bytes accessed | tf_op | source)
XLA Modules:
  0.0 253.2 jit_solution(833476742331515238)
XLA Ops:
  0.0 0.7 fusion.16
  0.7 0.2 reduce_window_sum.11
  0.9 0.8 select_reduce_fusion
  1.7 0.7 fusion.17
  2.4 0.7 multiply_add_fusion
  3.1 1.1 scatter_custom_fusion
  4.2 0.7 pad_add_fusion
  4.9 27.9 %all-gather.1 = s32[32,1,512]{2,1,0:T(1,128)S(1)} all-gather(s32[1,1,512]{2,1,0:T(1,128)S(1)} %bitcast.34), channel_id=2, replica_groups=mesh['region'=16,'slab'=32] {'slab'}, dimensions={0}, use_global_device_ids=true | all-gather | bytes 67584 | tf_op jit(solution)/shard_map/all_gather | solution.py:288
  32.7 0.1 copy.11
  32.8 0.1 copy.12
  33.0 0.1 reshape.112
  33.1 0.6 pad.4.x_ref
  33.7 18.7 %shard_map.46 = s32[16,8,128]{2,1,0:T(8,128)} custom-call(s32[16,8,128]{2,1,0:T(8,128)} %pad.4.x_ref), custom_call_target="tpu_custom_call" | custom-call | bytes 65536 | tf_op jit(solution)/shard_map/pallas_call | solution.py:253
  52.5 0.8 slice.14
  53.3 2.6 %copy.13.ids_ref = s32[8192,1]{1,0:T(8,128)} copy(s32[8192,1]{0,1:T(1,128)S(1)} %bitcast.32) | data formatting | bytes 65536 | tf_op jit(solution)/shard_map/reshape;reshape | solution.py:89
  55.9 14.4 %shard_map.47 = bf16[8192,128]{1,0:T(8,128)(2,1)} custom-call(s32[8192,1]{1,0:T(8,128)} %copy.13.ids_ref, bf16[1024,128]{1,0:T(8,128)(2,1)} %table_ref.3), custom_call_target="tpu_custom_call" | custom-call | flops 2147483648 | bytes 2359296 | tf_op jit(solution)/shard_map/pallas_call | solution.py:77
  70.3 10.0 %all-to-all-start = ((bf16[16,512,128]{2,1,0:T(8,128)(2,1)}), bf16[16,512,128]{2,1,0:T(8,128)(2,1)S(1)}, u32[]{:S(2)}, u32[]{:S(2)}) async-start(bf16[16,512,128]{2,1,0:T(8,128)(2,1)} %bitcast.27), calls=%async_computation | async-start | bytes 4194304 | tf_op jit(solution)/shard_map/all_to_all | solution.py:304
  80.3 2.0 copy.15.ids_ref
  82.3 2.0 copy.14.ids_ref
  84.2 0.5 fusion.14
  84.8 1.0 fusion.9
  85.8 5.0 %subtract_convert_fusion = (bf16[32,64,1024]{2,1,0:T(8,128)(2,1)}, bf16[32,64,1024]{2,1,0:T(8,128)(2,1)}) fusion(f32[64,1024]{1,0:T(8,128)S(1)} %get-tuple-element.9, f32[32,1024]{1,0:T(8,128)S(1)} %get-tuple-element.11, f32[64,1024]{1,0:T(8,128)S(1)} %get-tuple-element.10, f32[32,1024]{1,0:T(8,128)S(1)} %get-tuple-element.12), kind=kLoop, calls=%fused_computation.3 | loop fusion | flops 18874368 | bytes 9175040 | tf_op jit(solution)/shard_map/convert.3
  90.8 81.3 %all-to-all-done = bf16[16,512,128]{2,1,0:T(8,128)(2,1)S(1)} async-done(((bf16[16,512,128]{2,1,0:T(8,128)(2,1)}), bf16[16,512,128]{2,1,0:T(8,128)(2,1)S(1)}, u32[]{:S(2)}, u32[]{:S(2)}) %all-to-all-start) | async-done | bytes 2097184 | tf_op jit(solution)/shard_map/all_to_all | solution.py:304
  172.1 0.0 copy-start.1
  172.1 1.3 copy-done.1
  173.4 4.0 %shard_map.48 = bf16[32,128,128]{2,1,0:T(8,128)(2,1)} custom-call(s32[32,128,1]{2,1,0:T(8,128)} %copy.14.ids_ref, bf16[16,32,16,128]{3,2,1,0:T(8,128)(2,1)} %bitcast.26), custom_call_target="tpu_custom_call" | custom-call | flops 268435456 | bytes 3145728 | tf_op jit(solution)/shard_map/pallas_call | solution.py:104
  177.4 10.3 %all-to-all-start.1 = ((bf16[32,128,128]{2,1,0:T(8,128)(2,1)}), bf16[32,128,128]{2,1,0:T(8,128)(2,1)S(1)}, u32[]{:S(2)}, u32[]{:S(2)}) async-start(bf16[32,128,128]{2,1,0:T(8,128)(2,1)} %shard_map.48), calls=%async_computation.1 | async-start | bytes 2097152 | tf_op jit(solution)/shard_map/all_to_all | solution.py:306
  187.7 7.9 %shard_map.49 = bf16[4096,128]{1,0:T(8,128)(2,1)} custom-call(s32[4096,1]{1,0:T(8,128)} %copy.15.ids_ref, bf16[1024,128]{1,0:T(8,128)(2,1)} %table_ref.3), custom_call_target="tpu_custom_call" | custom-call | flops 1073741824 | bytes 1310720 | tf_op jit(solution)/shard_map/pallas_call | solution.py:77
  195.5 23.3 %shard_map.50.x_ref = bf16[32,128,128]{2,1,0:T(8,128)(2,1)} custom-call(bf16[32,128,128]{2,1,0:T(8,128)(2,1)} %bitcast.28), custom_call_target="tpu_custom_call" | custom-call | bytes 2097152 | tf_op jit(solution)/shard_map/pallas_call | solution.py:253
  218.8 0.1 multiply_subtract_fusion.taper_ref
  218.9 0.0 copy-start
  218.9 8.2 %pad_maximum_fusion.table_ref = bf16[2048,2048]{1,0:T(8,128)(2,1)} fusion(bf16[2048,1024]{1,0:T(8,128)(2,1)} %bitcast.25, bf16[2048,1024]{1,0:T(8,128)(2,1)} %bitcast.24), kind=kLoop, calls=%fused_computation.1 | loop fusion | flops 16777216 | bytes 16777216 | tf_op jit(solution)/shard_map/concatenate | solution.py:29
  227.1 0.0 copy-done
  227.1 12.5 %shard_map.51.first_ref = bf16[4,128,1024]{2,1,0:T(8,128)(2,1)S(1)} custom-call(bf16[32,128,128]{2,1,0:T(8,128)(2,1)S(1)} %copy-done, bf16[2048,2048]{1,0:T(8,128)(2,1)} %pad_maximum_fusion.table_ref, f32[16,128]{1,0:T(8,128)S(1)} %multiply_subtract_fusion.taper_ref), custom_call_target="tpu_custom_call" | custom-call | flops 2147483648 | bytes 10485760 | tf_op jit(solution)/shard_map/pallas_call | solution.py:186
  239.7 0.0 all-to-all-done.1.x_ref
  239.7 13.5 %shard_map.52 = bf16[128,2048]{1,0:T(8,128)(2,1)} custom-call(bf16[32,128,128]{2,1,0:T(8,128)(2,1)S(1)} %all-to-all-done.1.x_ref, bf16[4,128,1024]{2,1,0:T(8,128)(2,1)S(1)} %shard_map.51.first_ref, bf16[2048,2048]{1,0:T(8,128)(2,1)} %pad_maximum_fusion.table_ref, f32[16,128]{1,0:T(8,128)S(1)} %multiply_subtract_fusion.taper_ref), custom_call_target="tpu_custom_call" | custom-call | flops 2147483648 | bytes 12582912 | tf_op jit(solution)/shard_map/pallas_call | solution.py:204
  (3 shorter events, 0.0 us)
Async XLA Ops:
  70.3 101.8 %all-to-all-start = ((bf16[16,512,128]{2,1,0:T(8,128)(2,1)}), bf16[16,512,128]{2,1,0:T(8,128)(2,1)S(1)}, u32[]{:S(2)}, u32[]{:S(2)}) async-start(bf16[16,512,128]{2,1,0:T(8,128)(2,1)} %bitcast.27), calls=%async_computation | async-start | bytes 4194304 | tf_op jit(solution)/shard_map/all_to_all | solution.py:304
  172.1 1.3 copy-start.1
  177.4 62.3 %all-to-all-start.1 = ((bf16[32,128,128]{2,1,0:T(8,128)(2,1)}), bf16[32,128,128]{2,1,0:T(8,128)(2,1)S(1)}, u32[]{:S(2)}, u32[]{:S(2)}) async-start(bf16[32,128,128]{2,1,0:T(8,128)(2,1)} %shard_map.48), calls=%async_computation.1 | async-start | bytes 2097152 | tf_op jit(solution)/shard_map/all_to_all | solution.py:306
  218.9 8.2 %copy-start = (bf16[32,128,128]{2,1,0:T(8,128)(2,1)S(1)}, bf16[32,128,128]{2,1,0:T(8,128)(2,1)}, u32[]{:S(2)}) copy-start(bf16[32,128,128]{2,1,0:T(8,128)(2,1)} %shard_map.50.x_ref) | copy-start | bytes 3145732

commit v6 on v5

--- a/solution.py
+++ b/solution.py
@@ -302,6 +302,7 @@
     served = pick_rows(records, asked)
     served = served.reshape(regions, slabs * capacity, width)
     arrived = lax.all_to_all(served, "region", split_axis=0, concat_axis=0, tiled=True)
+    arrived, first_white = lax.optimization_barrier((arrived, first_white))
     second_parts = compact_rows(arrived.reshape(regions, slabs, capacity, width), slots)
     second_arrived = lax.all_to_all(second_parts, "slab", split_axis=0, concat_axis=0, tiled=True)
     return cross_rows(second_arrived, first_white, table, taper)

time: 256 us -> 218 us (0.85)
  waiting for transfers between devices: 81.3 us -> 30.3 us
  blocking collectives: 27.9 us -> 55 us
  starting transfers between devices: 20.2 us -> 10 us
    all_to_all x1, waiting for transfers between devices: 81.3 us -> 30.3 us  [local(): lax.all_to_all(served, 'region', split_axis=0, concat_axis=0, tiled=True)]
    all_to_all x0 -> x1, blocking collectives: none -> 27.2 us  [local(): lax.all_to_all(second_parts, 'slab', split_axis=0, concat_axis=0, tiled=T...]
    all_to_all x1 -> x0, starting transfers between devices: 10.3 us -> none  [local(): lax.all_to_all(second_parts, 'slab', split_axis=0, concat_axis=0, tiled=T...]
  transfers between devices with their start and end apart: 2 -> 1, of which waited for: 1 -> 1; matrix products, arithmetic and copies ran while one was open for 7% -> 9% of each run, Pallas kernels for 17% -> 20%
where the time goes in v6:
time: 218 us; the launch traced here: 217 us
  Pallas kernels  93.3 us (43%)
  blocking collectives  55 us (25%)
  waiting for transfers between devices  30.3 us (14%)
  other arithmetic  18.5 us (8%)
  starting transfers between devices  10 us (5%)
  local copies, waits for them, and re-layouts  9.55 us (4%)
    pallas_call x2, Pallas kernels, exchange(): pl.pallas_call(functools.partial(_exchange_kernel, axis), out_shape=jax.S...  41.1 us
    all_to_all x1, waiting for transfers between devices, local(): lax.all_to_all(served, 'region', split_axis=0, concat_axis=0, tiled=True)  30.3 us
    all_gather x1, blocking collectives, local(): plane = lax.all_gather(packed, 'slab', axis=0, tiled=False)  27.9 us
    all_to_all x1, blocking collectives, local(): lax.all_to_all(second_parts, 'slab', split_axis=0, concat_axis=0, tiled=T...  27.2 us
    pallas_call x2, Pallas kernels, pick_rows(): pl.pallas_call(_pick_kernel, out_shape=jax.ShapeDtypeStruct((count, width...  22.2 us
    pallas_call x1, Pallas kernels, cross_rows(): pl.pallas_call(_cross_kernel, out_shape=jax.ShapeDtypeStruct((rows, 2 * B...  13.5 us
    pallas_call x1, Pallas kernels, white_rows(): pl.pallas_call(_white_kernel, out_shape=jax.ShapeDtypeStruct((2 * SEG, ro...  12.6 us
    all_to_all x1, starting transfers between devices, local(): lax.all_to_all(served, 'region', split_axis=0, concat_axis=0, tiled=True)  10 us
  transfers between devices with their start and end apart: 1, of which 1 were waited for; matrix products, arithmetic and copies ran while one was open for 9% of the time, Pallas kernels for 20%

profile of v6, /device:TPU:1, one launch (start us, length us, event | category | flops | bytes accessed | tf_op | source)
XLA Modules:
  0.0 216.8 jit_solution(9672150384253567184)
XLA Ops:
  0.0 0.7 fusion.16
  0.7 0.2 reduce_window_sum.11
  0.9 0.8 select_reduce_fusion
  1.7 0.7 fusion.17
  2.4 0.7 multiply_add_fusion
  3.1 1.1 scatter_custom_fusion
  4.2 0.7 pad_add_fusion
  4.9 27.9 %all-gather.1 = s32[32,1,512]{2,1,0:T(1,128)S(1)} all-gather(s32[1,1,512]{2,1,0:T(1,128)S(1)} %bitcast.33), channel_id=2, replica_groups=mesh['region'=16,'slab'=32] {'slab'}, dimensions={0}, use_global_device_ids=true | all-gather | bytes 67584 | tf_op jit(solution)/shard_map/all_gather | solution.py:288
  32.7 0.1 copy.16
  32.8 0.1 copy.17
  33.0 0.1 reshape.112
  33.1 0.6 pad.4.x_ref
  33.7 18.7 %shard_map.46 = s32[16,8,128]{2,1,0:T(8,128)} custom-call(s32[16,8,128]{2,1,0:T(8,128)} %pad.4.x_ref), custom_call_target="tpu_custom_call" | custom-call | bytes 65536 | tf_op jit(solution)/shard_map/pallas_call | solution.py:253
  52.5 0.8 slice.14
  53.3 2.6 %copy.18.ids_ref = s32[8192,1]{1,0:T(8,128)} copy(s32[8192,1]{0,1:T(1,128)S(1)} %bitcast.31) | data formatting | bytes 65536 | tf_op jit(solution)/shard_map/reshape;reshape | solution.py:89
  55.9 14.4 %shard_map.47 = bf16[8192,128]{1,0:T(8,128)(2,1)} custom-call(s32[8192,1]{1,0:T(8,128)} %copy.18.ids_ref, bf16[1024,128]{1,0:T(8,128)(2,1)} %table_ref.3), custom_call_target="tpu_custom_call" | custom-call | flops 2147483648 | bytes 2359296 | tf_op jit(solution)/shard_map/pallas_call | solution.py:77
  70.3 10.0 %all-to-all-start = ((bf16[16,512,128]{2,1,0:T(8,128)(2,1)}), bf16[16,512,128]{2,1,0:T(8,128)(2,1)}, u32[]{:S(2)}, u32[]{:S(2)}) async-start(bf16[16,512,128]{2,1,0:T(8,128)(2,1)} %bitcast.26), calls=%async_computation | async-start | bytes 4194304 | tf_op jit(solution)/shard_map/all_to_all | solution.py:304
  80.3 2.0 copy.19.ids_ref
  82.3 7.8 %shard_map.48 = bf16[4096,128]{1,0:T(8,128)(2,1)} custom-call(s32[4096,1]{1,0:T(8,128)} %copy.19.ids_ref, bf16[1024,128]{1,0:T(8,128)(2,1)} %table_ref.3), custom_call_target="tpu_custom_call" | custom-call | flops 1073741824 | bytes 1310720 | tf_op jit(solution)/shard_map/pallas_call | solution.py:77
  90.2 22.4 %shard_map.49.x_ref = bf16[32,128,128]{2,1,0:T(8,128)(2,1)} custom-call(bf16[32,128,128]{2,1,0:T(8,128)(2,1)} %bitcast.27), custom_call_target="tpu_custom_call" | custom-call | bytes 2097152 | tf_op jit(solution)/shard_map/pallas_call | solution.py:253
  112.6 2.0 copy.20.ids_ref
  114.6 0.1 multiply_subtract_fusion.taper_ref
  114.6 0.5 fusion.14
  115.2 1.0 fusion.9
  116.2 5.0 %subtract_convert_fusion = (bf16[32,64,1024]{2,1,0:T(8,128)(2,1)}, bf16[32,64,1024]{2,1,0:T(8,128)(2,1)}) fusion(f32[64,1024]{1,0:T(8,128)S(1)} %get-tuple-element.13, f32[32,1024]{1,0:T(8,128)S(1)} %get-tuple-element.15, f32[64,1024]{1,0:T(8,128)S(1)} %get-tuple-element.14, f32[32,1024]{1,0:T(8,128)S(1)} %get-tuple-element.16), kind=kLoop, calls=%fused_computation.3 | loop fusion | flops 18874368 | bytes 9175040 | tf_op jit(solution)/shard_map/convert.3
  121.2 0.0 copy-start
  121.2 8.2 %pad_maximum_fusion.table_ref = bf16[2048,2048]{1,0:T(8,128)(2,1)} fusion(bf16[2048,1024]{1,0:T(8,128)(2,1)} %bitcast.25, bf16[2048,1024]{1,0:T(8,128)(2,1)} %bitcast.24), kind=kLoop, calls=%fused_computation.1 | loop fusion | flops 16777216 | bytes 16777216 | tf_op jit(solution)/shard_map/concatenate | solution.py:29
  129.4 0.0 copy-done
  129.4 12.6 %shard_map.50.first_ref = bf16[4,128,1024]{2,1,0:T(8,128)(2,1)S(1)} custom-call(bf16[32,128,128]{2,1,0:T(8,128)(2,1)S(1)} %copy-done, bf16[2048,2048]{1,0:T(8,128)(2,1)} %pad_maximum_fusion.table_ref, f32[16,128]{1,0:T(8,128)S(1)} %multiply_subtract_fusion.taper_ref), custom_call_target="tpu_custom_call" | custom-call | flops 2147483648 | bytes 10485760 | tf_op jit(solution)/shard_map/pallas_call | solution.py:186
  142.0 30.3 %all-to-all-done = bf16[16,512,128]{2,1,0:T(8,128)(2,1)} async-done(((bf16[16,512,128]{2,1,0:T(8,128)(2,1)}), bf16[16,512,128]{2,1,0:T(8,128)(2,1)}, u32[]{:S(2)}, u32[]{:S(2)}) %all-to-all-start) | async-done | bytes 2097184 | tf_op jit(solution)/shard_map/all_to_all | solution.py:304
  172.2 4.0 %shard_map.51 = bf16[32,128,128]{2,1,0:T(8,128)(2,1)} custom-call(s32[32,128,1]{2,1,0:T(8,128)} %copy.20.ids_ref, bf16[16,32,16,128]{3,2,1,0:T(8,128)(2,1)} %bitcast.13.table_ref), custom_call_target="tpu_custom_call" | custom-call | flops 268435456 | bytes 3145728 | tf_op jit(solution)/shard_map/pallas_call | solution.py:104
  176.2 27.2 %all_to_all.10.x_ref = bf16[32,128,128]{2,1,0:T(8,128)(2,1)S(1)} all-to-all(bf16[32,128,128]{2,1,0:T(8,128)(2,1)} %shard_map.51), channel_id=1, replica_groups=mesh['region'=16,'slab'=32] {'slab'}, dimensions={0} | all-to-all | bytes 2097152 | tf_op jit(solution)/shard_map/all_to_all | solution.py:307
  203.4 13.5 %shard_map.52 = bf16[128,2048]{1,0:T(8,128)(2,1)} custom-call(bf16[32,128,128]{2,1,0:T(8,128)(2,1)S(1)} %all_to_all.10.x_ref, bf16[4,128,1024]{2,1,0:T(8,128)(2,1)S(1)} %shard_map.50.first_ref, bf16[2048,2048]{1,0:T(8,128)(2,1)} %pad_maximum_fusion.table_ref, f32[16,128]{1,0:T(8,128)S(1)} %multiply_subtract_fusion.taper_ref), custom_call_target="tpu_custom_call" | custom-call | flops 2147483648 | bytes 12582912 | tf_op jit(solution)/shard_map/pallas_call | solution.py:204
  (3 shorter events, 0.0 us)
Async XLA Ops:
  70.3 101.9 %all-to-all-start = ((bf16[16,512,128]{2,1,0:T(8,128)(2,1)}), bf16[16,512,128]{2,1,0:T(8,128)(2,1)}, u32[]{:S(2)}, u32[]{:S(2)}) async-start(bf16[16,512,128]{2,1,0:T(8,128)(2,1)} %bitcast.26), calls=%async_computation | async-start | bytes 4194304 | tf_op jit(solution)/shard_map/all_to_all | solution.py:304
  121.2 8.2 %copy-start = (bf16[32,128,128]{2,1,0:T(8,128)(2,1)S(1)}, bf16[32,128,128]{2,1,0:T(8,128)(2,1)}, u32[]{:S(2)}) copy-start(bf16[32,128,128]{2,1,0:T(8,128)(2,1)} %shard_map.49.x_ref) | copy-start | bytes 3145732

commit v7 on v6

--- a/solution.py
+++ b/solution.py
@@ -300,11 +300,11 @@
     outgoing = jnp.pad(outgoing, ((0, 0), (0, (-outgoing.shape[1]) % 8), (0, 0)))
     asked = exchange(outgoing, "region", 1)[:, : slabs * capacity // 128].reshape(-1)
     served = pick_rows(records, asked)
-    served = served.reshape(regions, slabs * capacity, width)
-    arrived = lax.all_to_all(served, "region", split_axis=0, concat_axis=0, tiled=True)
+    served = served.reshape(regions * slabs, capacity, width)
+    arrived = lax.all_to_all(served, ("region", "slab"), split_axis=0, concat_axis=0, tiled=True)
     arrived, first_white = lax.optimization_barrier((arrived, first_white))
-    second_parts = compact_rows(arrived.reshape(regions, slabs, capacity, width), slots)
-    second_arrived = lax.all_to_all(second_parts, "slab", split_axis=0, concat_axis=0, tiled=True)
+    own_slots = jnp.broadcast_to(slot_index[None, :], (slabs, pair_count))
+    second_arrived = compact_rows(arrived.reshape(regions, slabs, capacity, width), own_slots)
     return cross_rows(second_arrived, first_white, table, taper)
 
 

time: 218 us -> 209 us (0.959)
  blocking collectives: 55 us -> 27.9 us
  starting transfers between devices: 10 us -> 19.1 us
  Pallas kernels: 93.3 us -> 99.5 us
    all_to_all x1 -> x0, blocking collectives: 27.2 us -> none  [local(): lax.all_to_all(second_parts, 'slab', split_axis=0, concat_axis=0, tiled=T...]
    all_to_all x1, starting transfers between devices: 10 us -> 19.1 us  [local(): lax.all_to_all(served, ('region', 'slab'), split_axis=0, concat_axis=0, t...]
    pallas_call x2, Pallas kernels: 41.1 us -> 47.3 us  [exchange(): pl.pallas_call(functools.partial(_exchange_kernel, axis), out_shape=jax.S...]
  transfers between devices with their start and end apart: 1 -> 1, of which waited for: 1 -> 1; matrix products, arithmetic and copies ran while one was open for 9% -> 8% of each run, Pallas kernels for 20% -> 24%
where the time goes in v7:
time: 209 us; the launch traced here: 208 us
  Pallas kernels  99.5 us (48%)
  waiting for transfers between devices  31.9 us (15%)
  blocking collectives  27.9 us (13%)
  starting transfers between devices  19.1 us (9%)
  other arithmetic  18.5 us (9%)
  local copies, waits for them, and re-layouts  10.6 us (5%)
    pallas_call x2, Pallas kernels, exchange(): pl.pallas_call(functools.partial(_exchange_kernel, axis), out_shape=jax.S...  47.3 us
    all_to_all x1, waiting for transfers between devices, local(): lax.all_to_all(served, ('region', 'slab'), split_axis=0, concat_axis=0, t...  31.9 us
    all_gather x1, blocking collectives, local(): plane = lax.all_gather(packed, 'slab', axis=0, tiled=False)  27.9 us
    pallas_call x2, Pallas kernels, pick_rows(): pl.pallas_call(_pick_kernel, out_shape=jax.ShapeDtypeStruct((count, width...  22.2 us
    all_to_all x1, starting transfers between devices, local(): lax.all_to_all(served, ('region', 'slab'), split_axis=0, concat_axis=0, t...  19.1 us
    pallas_call x1, Pallas kernels, cross_rows(): pl.pallas_call(_cross_kernel, out_shape=jax.ShapeDtypeStruct((rows, 2 * B...  13.5 us
    pallas_call x1, Pallas kernels, white_rows(): pl.pallas_call(_white_kernel, out_shape=jax.ShapeDtypeStruct((2 * SEG, ro...  12.6 us
    concatenate x1, other arithmetic, dft_table(): return jnp.concatenate([cos_part, -sin_part], axis=1).astype(jnp.bfloat16)  8.22 us
  transfers between devices with their start and end apart: 1, of which 1 were waited for; matrix products, arithmetic and copies ran while one was open for 8% of the time, Pallas kernels for 24%

profile of v7, /device:TPU:1, one launch (start us, length us, event | category | flops | bytes accessed | tf_op | source)
XLA Modules:
  0.0 207.6 jit_solution(14064627526129706259)
XLA Ops:
  0.0 0.7 fusion.16
  0.7 0.2 reduce_window_sum.11
  0.9 0.8 select_reduce_fusion
  1.7 0.7 multiply_add_fusion
  2.4 0.7 fusion.17
  3.1 1.1 scatter_custom_fusion
  4.2 0.7 pad_add_fusion
  4.9 27.9 %all-gather.1 = s32[32,1,512]{2,1,0:T(1,128)S(1)} all-gather(s32[1,1,512]{2,1,0:T(1,128)S(1)} %bitcast.29), channel_id=2, replica_groups=mesh['region'=16,'slab'=32] {'slab'}, dimensions={0}, use_global_device_ids=true | all-gather | bytes 67584 | tf_op jit(solution)/shard_map/all_gather | solution.py:288
  32.7 0.1 copy.14
  32.9 0.1 copy.15
  33.0 0.1 reshape.120
  33.1 0.6 pad.4.x_ref
  33.8 18.7 %shard_map.46 = s32[16,8,128]{2,1,0:T(8,128)} custom-call(s32[16,8,128]{2,1,0:T(8,128)} %pad.4.x_ref), custom_call_target="tpu_custom_call" | custom-call | bytes 65536 | tf_op jit(solution)/shard_map/pallas_call | solution.py:253
  52.5 0.8 slice.10
  53.4 2.6 %copy.16.ids_ref = s32[8192,1]{1,0:T(8,128)} copy(s32[8192,1]{0,1:T(1,128)S(1)} %bitcast.27) | data formatting | bytes 65536 | tf_op jit(solution)/shard_map/reshape;reshape | solution.py:89
  55.9 14.4 %shard_map.47 = bf16[8192,128]{1,0:T(8,128)(2,1)} custom-call(s32[8192,1]{1,0:T(8,128)} %copy.16.ids_ref, bf16[1024,128]{1,0:T(8,128)(2,1)} %table_ref.3), custom_call_target="tpu_custom_call" | custom-call | flops 2147483648 | bytes 2359296 | tf_op jit(solution)/shard_map/pallas_call | solution.py:77
  70.3 19.1 %all-to-all-start = ((bf16[512,16,128]{2,1,0:T(8,128)(2,1)}), bf16[512,16,128]{2,1,0:T(8,128)(2,1)}, u32[]{:S(2)}, u32[]{:S(2)}) async-start(bf16[512,16,128]{2,1,0:T(8,128)(2,1)} %bitcast.22), calls=%async_computation | async-start | bytes 4194304 | tf_op jit(solution)/shard_map/all_to_all | solution.py:304
  89.4 0.1 copy.17
  89.5 2.0 copy.18.ids_ref
  91.5 7.8 %shard_map.48 = bf16[4096,128]{1,0:T(8,128)(2,1)} custom-call(s32[4096,1]{1,0:T(8,128)} %copy.18.ids_ref, bf16[1024,128]{1,0:T(8,128)(2,1)} %table_ref.3), custom_call_target="tpu_custom_call" | custom-call | flops 1073741824 | bytes 1310720 | tf_op jit(solution)/shard_map/pallas_call | solution.py:77
  99.3 28.6 %shard_map.49.x_ref = bf16[32,128,128]{2,1,0:T(8,128)(2,1)} custom-call(bf16[32,128,128]{2,1,0:T(8,128)(2,1)} %bitcast.23), custom_call_target="tpu_custom_call" | custom-call | bytes 2097152 | tf_op jit(solution)/shard_map/pallas_call | solution.py:253
  127.9 0.1 multiply_subtract_fusion.taper_ref
  128.0 0.5 fusion.14
  128.5 1.0 fusion.9
  129.6 5.0 %subtract_convert_fusion = (bf16[32,64,1024]{2,1,0:T(8,128)(2,1)}, bf16[32,64,1024]{2,1,0:T(8,128)(2,1)}) fusion(f32[64,1024]{1,0:T(8,128)S(1)} %get-tuple-element.11, f32[32,1024]{1,0:T(8,128)S(1)} %get-tuple-element.13, f32[64,1024]{1,0:T(8,128)S(1)} %get-tuple-element.12, f32[32,1024]{1,0:T(8,128)S(1)} %get-tuple-element.14), kind=kLoop, calls=%fused_computation.3 | loop fusion | flops 18874368 | bytes 9175040 | tf_op jit(solution)/shard_map/convert.3
  134.5 0.0 copy-start.1
  134.5 8.2 %pad_maximum_fusion.table_ref = bf16[2048,2048]{1,0:T(8,128)(2,1)} fusion(bf16[2048,1024]{1,0:T(8,128)(2,1)} %bitcast.21, bf16[2048,1024]{1,0:T(8,128)(2,1)} %bitcast.20), kind=kLoop, calls=%fused_computation.1 | loop fusion | flops 16777216 | bytes 16777216 | tf_op jit(solution)/shard_map/concatenate | solution.py:29
  142.8 0.0 copy-done.1
  142.8 12.6 %shard_map.50.first_ref = bf16[4,128,1024]{2,1,0:T(8,128)(2,1)S(1)} custom-call(bf16[32,128,128]{2,1,0:T(8,128)(2,1)S(1)} %copy-done.1, bf16[2048,2048]{1,0:T(8,128)(2,1)} %pad_maximum_fusion.table_ref, f32[16,128]{1,0:T(8,128)S(1)} %multiply_subtract_fusion.taper_ref), custom_call_target="tpu_custom_call" | custom-call | flops 2147483648 | bytes 10485760 | tf_op jit(solution)/shard_map/pallas_call | solution.py:186
  155.3 31.9 %all-to-all-done = bf16[512,16,128]{2,1,0:T(8,128)(2,1)} async-done(((bf16[512,16,128]{2,1,0:T(8,128)(2,1)}), bf16[512,16,128]{2,1,0:T(8,128)(2,1)}, u32[]{:S(2)}, u32[]{:S(2)}) %all-to-all-start) | async-done | bytes 2097184 | tf_op jit(solution)/shard_map/all_to_all | solution.py:304
  187.2 1.7 reshape.118.ids_ref
  188.9 4.0 %shard_map.51.x_ref = bf16[32,128,128]{2,1,0:T(8,128)(2,1)} custom-call(s32[32,128,1]{2,1,0:T(8,128)} %reshape.118.ids_ref, bf16[16,32,16,128]{3,2,1,0:T(8,128)(2,1)} %bitcast.13.table_ref), custom_call_target="tpu_custom_call" | custom-call | flops 268435456 | bytes 3145728 | tf_op jit(solution)/shard_map/pallas_call | solution.py:104
  192.9 0.0 copy-start
  192.9 1.2 copy-done
  194.1 13.5 %shard_map.52 = bf16[128,2048]{1,0:T(8,128)(2,1)} custom-call(bf16[32,128,128]{2,1,0:T(8,128)(2,1)S(1)} %copy-done, bf16[4,128,1024]{2,1,0:T(8,128)(2,1)S(1)} %shard_map.50.first_ref, bf16[2048,2048]{1,0:T(8,128)(2,1)} %pad_maximum_fusion.table_ref, f32[16,128]{1,0:T(8,128)S(1)} %multiply_subtract_fusion.taper_ref), custom_call_target="tpu_custom_call" | custom-call | flops 2147483648 | bytes 12582912 | tf_op jit(solution)/shard_map/pallas_call | solution.py:204
  (2 shorter events, 0.0 us)
Async XLA Ops:
  70.3 116.9 %all-to-all-start = ((bf16[512,16,128]{2,1,0:T(8,128)(2,1)}), bf16[512,16,128]{2,1,0:T(8,128)(2,1)}, u32[]{:S(2)}, u32[]{:S(2)}) async-start(bf16[512,16,128]{2,1,0:T(8,128)(2,1)} %bitcast.22), calls=%async_computation | async-start | bytes 4194304 | tf_op jit(solution)/shard_map/all_to_all | solution.py:304
  134.5 8.2 %copy-start.1 = (bf16[32,128,128]{2,1,0:T(8,128)(2,1)S(1)}, bf16[32,128,128]{2,1,0:T(8,128)(2,1)}, u32[]{:S(2)}) copy-start(bf16[32,128,128]{2,1,0:T(8,128)(2,1)} %shard_map.49.x_ref) | copy-start | bytes 3145732
  192.9 1.2 copy-start

commit v8 on v7

--- a/solution.py
+++ b/solution.py
@@ -284,21 +284,17 @@
         .at[slot_index]
         .set(second_station)
     )
-    packed = jnp.concatenate([first_station, slot_index, requests])
-    plane = lax.all_gather(packed, "slab", axis=0, tiled=False)
-    firsts = plane[:, :pair_count]
-    slots = plane[:, pair_count : 2 * pair_count]
-    plane_requests = plane[:, 2 * pair_count :].reshape(slabs, regions, capacity)
-
+    outgoing = jnp.broadcast_to(requests.reshape(regions, 1, capacity), (regions, slabs, capacity))
+    asked = lax.all_to_all(outgoing.reshape(regions * slabs, capacity), ("region", "slab"), split_axis=0, concat_axis=0, tiled=True)
+    asked = asked.reshape(-1)
+
+    firsts = lax.all_gather(first_station, "slab", axis=0, tiled=False)
     first_parts = pick_rows(records, firsts.reshape(-1)).reshape(slabs, pair_count, width)
     first_arrived = exchange(first_parts, "slab", 0)
     table = dft_table()
     taper = taper_table(slabs // SEG, width)
     first_white = white_rows(first_arrived, table, taper)
 
-    outgoing = jnp.transpose(plane_requests, (1, 0, 2)).reshape(regions, -1, 128)
-    outgoing = jnp.pad(outgoing, ((0, 0), (0, (-outgoing.shape[1]) % 8), (0, 0)))
-    asked = exchange(outgoing, "region", 1)[:, : slabs * capacity // 128].reshape(-1)
     served = pick_rows(records, asked)
     served = served.reshape(regions * slabs, capacity, width)
     arrived = lax.all_to_all(served, ("region", "slab"), split_axis=0, concat_axis=0, tiled=True)

time: 209 us -> 204 us (0.976)
  blocking collectives: 27.9 us -> 71.1 us
  Pallas kernels: 99.5 us -> 79 us
  waiting for transfers between devices: 31.9 us -> 11.7 us
  starting transfers between devices: 19.1 us -> 11.6 us
    all_to_all x0 -> x1, blocking collectives: none -> 48.9 us  [local(): lax.all_to_all(outgoing.reshape(regions * slabs, capacity), ('region', 's...]
    pallas_call x2 -> x1, Pallas kernels: 47.3 us -> 26.8 us  [exchange(): pl.pallas_call(functools.partial(_exchange_kernel, axis), out_shape=jax.S...]
    all_to_all x1, waiting for transfers between devices: 31.9 us -> 11.7 us  [local(): lax.all_to_all(served, ('region', 'slab'), split_axis=0, concat_axis=0, t...]
    all_to_all x1, starting transfers between devices: 19.1 us -> 11.6 us  [local(): lax.all_to_all(served, ('region', 'slab'), split_axis=0, concat_axis=0, t...]
    all_gather x1, blocking collectives: 27.9 us -> 22.2 us  [local(): firsts = lax.all_gather(first_station, 'slab', axis=0, tiled=False)]
  transfers between devices with their start and end apart: 1 -> 1, of which waited for: 1 -> 1; matrix products, arithmetic and copies ran while one was open for 8% -> 8% of each run, Pallas kernels for 24% -> 23%
where the time goes in v8:
time: 204 us; the launch traced here: 202 us
  Pallas kernels  79 us (39%)
  blocking collectives  71.1 us (35%)
  other arithmetic  18.5 us (9%)
  waiting for transfers between devices  11.7 us (6%)
  starting transfers between devices  11.6 us (6%)
  local copies, waits for them, and re-layouts  10.3 us (5%)
    all_to_all x1, blocking collectives, local(): lax.all_to_all(outgoing.reshape(regions * slabs, capacity), ('region', 's...  48.9 us
    pallas_call x1, Pallas kernels, exchange(): pl.pallas_call(functools.partial(_exchange_kernel, axis), out_shape=jax.S...  26.8 us
    pallas_call x2, Pallas kernels, pick_rows(): pl.pallas_call(_pick_kernel, out_shape=jax.ShapeDtypeStruct((count, width...  22.2 us
    all_gather x1, blocking collectives, local(): firsts = lax.all_gather(first_station, 'slab', axis=0, tiled=False)  22.2 us
    pallas_call x1, Pallas kernels, cross_rows(): pl.pallas_call(_cross_kernel, out_shape=jax.ShapeDtypeStruct((rows, 2 * B...  13.5 us
    pallas_call x1, Pallas kernels, white_rows(): pl.pallas_call(_white_kernel, out_shape=jax.ShapeDtypeStruct((2 * SEG, ro...  12.5 us
    all_to_all x1, waiting for transfers between devices, local(): lax.all_to_all(served, ('region', 'slab'), split_axis=0, concat_axis=0, t...  11.7 us
    all_to_all x1, starting transfers between devices, local(): lax.all_to_all(served, ('region', 'slab'), split_axis=0, concat_axis=0, t...  11.6 us
  transfers between devices with their start and end apart: 1, of which 1 were waited for; matrix products, arithmetic and copies ran while one was open for 8% of the time, Pallas kernels for 23%

profile of v8, /device:TPU:1, one launch (start us, length us, event | category | flops | bytes accessed | tf_op | source)
XLA Modules:
  0.0 202.2 jit_solution(2697600917997605328)
XLA Ops:
  0.0 0.7 fusion.16
  0.7 0.2 reduce_window_sum.11
  0.9 0.8 select_reduce_fusion
  1.7 0.7 fusion.17
  2.4 1.1 scatter_custom_fusion
  3.5 0.1 broadcast_in_dim.7
  3.6 48.9 %all_to_all.14 = s32[512,1,16]{2,1,0:T(1,128)S(1)} all-to-all(s32[512,1,16]{2,1,0:T(1,128)S(1)} %bitcast.20), channel_id=1, replica_groups=mesh['region'=16,'slab'=32] {'region','slab'}, dimensions={0} | all-to-all | bytes 65536 | tf_op jit(solution)/shard_map/all_to_all | solution.py:288
  52.5 0.5 broadcast.156
  53.0 1.3 reduce.3
  54.3 0.0 copy-start.3
  54.3 3.6 %reshape_reshape.8.ids_ref = s32[8192,1]{1,0:T(8,128)} reshape(s32[512,16]{1,0:T(8,128)S(1)} %reduce.3) | data formatting | bytes 65536 | tf_op jit(solution)/shard_map/reshape;reshape | solution.py:89
  57.9 14.4 %shard_map.46 = bf16[8192,128]{1,0:T(8,128)(2,1)} custom-call(s32[8192,1]{1,0:T(8,128)} %reshape_reshape.8.ids_ref, bf16[1024,128]{1,0:T(8,128)(2,1)} %table_ref.3), custom_call_target="tpu_custom_call" | custom-call | flops 2147483648 | bytes 2359296 | tf_op jit(solution)/shard_map/pallas_call | solution.py:77
  72.3 11.6 %all-to-all-start.1 = ((bf16[512,16,128]{2,1,0:T(8,128)(2,1)}), bf16[512,16,128]{2,1,0:T(8,128)(2,1)}, u32[]{:S(2)}, u32[]{:S(2)}) async-start(bf16[512,16,128]{2,1,0:T(8,128)(2,1)} %bitcast.18), calls=%async_computation.1 | async-start | bytes 4194304 | tf_op jit(solution)/shard_map/all_to_all | solution.py:300
  83.9 0.0 copy-done.3
  83.9 22.2 %all-gather.1 = s32[32,1,128]{2,1,0:T(1,128)S(1)} all-gather(s32[1,1,128]{2,1,0:T(1,128)S(1)} %bitcast.24), channel_id=2, replica_groups=mesh['region'=16,'slab'=32] {'slab'}, dimensions={0}, use_global_device_ids=true | all-gather | bytes 16896 | tf_op jit(solution)/shard_map/all_gather | solution.py:291
  106.1 2.0 copy.8.ids_ref
  108.1 7.8 %shard_map.47 = bf16[4096,128]{1,0:T(8,128)(2,1)} custom-call(s32[4096,1]{1,0:T(8,128)} %copy.8.ids_ref, bf16[1024,128]{1,0:T(8,128)(2,1)} %table_ref.3), custom_call_target="tpu_custom_call" | custom-call | flops 1073741824 | bytes 1310720 | tf_op jit(solution)/shard_map/pallas_call | solution.py:77
  115.9 26.8 %shard_map.48.x_ref = bf16[32,128,128]{2,1,0:T(8,128)(2,1)} custom-call(bf16[32,128,128]{2,1,0:T(8,128)(2,1)} %bitcast.19), custom_call_target="tpu_custom_call" | custom-call | bytes 2097152 | tf_op jit(solution)/shard_map/pallas_call | solution.py:253
  142.7 0.1 multiply_subtract_fusion.taper_ref
  142.8 0.5 fusion.14
  143.3 1.0 fusion.9
  144.4 5.0 %subtract_convert_fusion = (bf16[32,64,1024]{2,1,0:T(8,128)(2,1)}, bf16[32,64,1024]{2,1,0:T(8,128)(2,1)}) fusion(f32[64,1024]{1,0:T(8,128)S(1)} %get-tuple-element.11, f32[32,1024]{1,0:T(8,128)S(1)} %get-tuple-element.13, f32[64,1024]{1,0:T(8,128)S(1)} %get-tuple-element.12, f32[32,1024]{1,0:T(8,128)S(1)} %get-tuple-element.14), kind=kLoop, calls=%fused_computation.3 | loop fusion | flops 18874368 | bytes 9175040 | tf_op jit(solution)/shard_map/convert.3
  149.4 0.0 copy-start.1
  149.4 8.2 %pad_maximum_fusion.table_ref = bf16[2048,2048]{1,0:T(8,128)(2,1)} fusion(bf16[2048,1024]{1,0:T(8,128)(2,1)} %bitcast.17, bf16[2048,1024]{1,0:T(8,128)(2,1)} %bitcast.16), kind=kLoop, calls=%fused_computation.1 | loop fusion | flops 16777216 | bytes 16777216 | tf_op jit(solution)/shard_map/concatenate | solution.py:29
  157.6 0.0 copy-done.1
  157.6 0.0 copy-start.2
  157.6 12.5 %shard_map.49.first_ref = bf16[4,128,1024]{2,1,0:T(8,128)(2,1)S(1)} custom-call(bf16[32,128,128]{2,1,0:T(8,128)(2,1)S(1)} %copy-done.1, bf16[2048,2048]{1,0:T(8,128)(2,1)} %pad_maximum_fusion.table_ref, f32[16,128]{1,0:T(8,128)S(1)} %multiply_subtract_fusion.taper_ref), custom_call_target="tpu_custom_call" | custom-call | flops 2147483648 | bytes 10485760 | tf_op jit(solution)/shard_map/pallas_call | solution.py:186
  170.1 0.0 copy-done.2
  170.2 11.7 %all-to-all-done.1 = bf16[512,16,128]{2,1,0:T(8,128)(2,1)} async-done(((bf16[512,16,128]{2,1,0:T(8,128)(2,1)}), bf16[512,16,128]{2,1,0:T(8,128)(2,1)}, u32[]{:S(2)}, u32[]{:S(2)}) %all-to-all-start.1) | async-done | bytes 2097184 | tf_op jit(solution)/shard_map/all_to_all | solution.py:300
  181.9 1.7 reshape.119.ids_ref
  183.6 4.0 %shard_map.50.x_ref = bf16[32,128,128]{2,1,0:T(8,128)(2,1)} custom-call(s32[32,128,1]{2,1,0:T(8,128)} %reshape.119.ids_ref, bf16[16,32,16,128]{3,2,1,0:T(8,128)(2,1)} %bitcast.10.table_ref), custom_call_target="tpu_custom_call" | custom-call | flops 268435456 | bytes 3145728 | tf_op jit(solution)/shard_map/pallas_call | solution.py:104
  187.5 0.0 copy-start
  187.5 1.2 copy-done
  188.7 13.5 %shard_map.51 = bf16[128,2048]{1,0:T(8,128)(2,1)} custom-call(bf16[32,128,128]{2,1,0:T(8,128)(2,1)S(1)} %copy-done, bf16[4,128,1024]{2,1,0:T(8,128)(2,1)S(1)} %shard_map.49.first_ref, bf16[2048,2048]{1,0:T(8,128)(2,1)} %pad_maximum_fusion.table_ref, f32[16,128]{1,0:T(8,128)S(1)} %multiply_subtract_fusion.taper_ref), custom_call_target="tpu_custom_call" | custom-call | flops 2147483648 | bytes 12582912 | tf_op jit(solution)/shard_map/pallas_call | solution.py:204
  (2 shorter events, 0.0 us)
Async XLA Ops:
  54.3 29.6 %copy-start.3 = (s32[128]{0:T(128)S(1)}, s32[128]{0:T(128)}, u32[]{:S(2)}) copy-start(s32[128]{0:T(128)} %param.5) | copy-start | bytes 1540
  72.3 109.6 %all-to-all-start.1 = ((bf16[512,16,128]{2,1,0:T(8,128)(2,1)}), bf16[512,16,128]{2,1,0:T(8,128)(2,1)}, u32[]{:S(2)}, u32[]{:S(2)}) async-start(bf16[512,16,128]{2,1,0:T(8,128)(2,1)} %bitcast.18), calls=%async_computation.1 | async-start | bytes 4194304 | tf_op jit(solution)/shard_map/all_to_all | solution.py:300
  149.4 8.2 %copy-start.1 = (bf16[32,128,128]{2,1,0:T(8,128)(2,1)S(1)}, bf16[32,128,128]{2,1,0:T(8,128)(2,1)}, u32[]{:S(2)}) copy-start(bf16[32,128,128]{2,1,0:T(8,128)(2,1)} %shard_map.48.x_ref) | copy-start | bytes 3145732
  157.6 12.6 %copy-start.2 = (s32[128,1]{0,1:T(1,128)S(1)}, s32[128,1]{0,1:T(1,128)}, u32[]{:S(2)}) copy-start(s32[128,1]{0,1:T(1,128)} %param.6) | copy-start | bytes 1540
  187.5 1.2 copy-start

commit v9 on v8

--- a/solution.py
+++ b/solution.py
@@ -112,14 +112,15 @@
     )(slots.reshape(slabs, pairs, 1), arrived)
 
 
-def _white_block(x, table, taper):
-    slabs, rows, width = x.shape
-    per_segment = slabs // SEG
-    signal = x.astype(jnp.float32)
+def _white_block(slices, table, taper):
+    per_segment = len(slices) // SEG
     tapered = []
     for segment in range(SEG):
-        part = signal[segment * per_segment : (segment + 1) * per_segment]
-        mean = jnp.sum(jnp.sum(part, axis=2, keepdims=True), axis=0) / NFFT
+        part = [piece.astype(jnp.float32) for piece in slices[segment * per_segment : (segment + 1) * per_segment]]
+        total = jnp.sum(part[0], axis=1, keepdims=True)
+        for piece in part[1:]:
+            total = total + jnp.sum(piece, axis=1, keepdims=True)
+        mean = total / NFFT
         pieces = [((part[i] - mean) * taper[i : i + 1, :]).astype(jnp.bfloat16) for i in range(per_segment)]
         tapered.append(jnp.concatenate(pieces, axis=1))
     spectrum = jnp.dot(jnp.concatenate(tapered, axis=0), table, preferred_element_type=jnp.float32)
@@ -142,15 +143,25 @@
 
 def _white_kernel(x_ref, table_ref, taper_ref, out_ref):
     rows = x_ref.shape[1]
-    white_real, white_imag = _white_block(x_ref[...], table_ref[...], taper_ref[...])
+    slices = [x_ref[i] for i in range(x_ref.shape[0])]
+    white_real, white_imag = _white_block(slices, table_ref[...], taper_ref[...])
     for segment in range(SEG):
         out_ref[2 * segment] = white_real[segment * rows : (segment + 1) * rows]
         out_ref[2 * segment + 1] = white_imag[segment * rows : (segment + 1) * rows]
 
 
-def _cross_kernel(x_ref, first_ref, table_ref, taper_ref, out_ref):
-    rows = x_ref.shape[1]
-    white_real, white_imag = _white_block(x_ref[...], table_ref[...], taper_ref[...])
+def _cross_kernel(ids_ref, arrived_ref, first_ref, table_ref, taper_ref, out_ref):
+    buckets, slabs, capacity, width = arrived_ref.shape
+    ids = ids_ref[...]
+    rows = ids.shape[0]
+    onehot = (lax.broadcasted_iota(jnp.int32, (rows, buckets * capacity), 1) == ids).astype(arrived_ref.dtype)
+    slices = [
+        jnp.dot(onehot, arrived_ref[:, s].reshape(buckets * capacity, width), preferred_element_type=jnp.float32).astype(
+            arrived_ref.dtype
+        )
+        for s in range(slabs)
+    ]
+    white_real, white_imag = _white_block(slices, table_ref[...], taper_ref[...])
     real_sum = None
     imag_sum = None
     for segment in range(SEG):
@@ -197,22 +208,27 @@
     )(parts, table, taper)
 
 
-def cross_rows(parts, first_white, table, taper, block=32):
-    slabs, rows, width = parts.shape
-    specs = _white_specs(slabs, block, width, slabs // SEG)
-    specs.insert(1, pl.BlockSpec((2 * SEG, block, BINS), lambda i: (0, i, 0)))
+def cross_rows(arrived, slots, first_white, table, taper, block=32):
+    buckets, slabs, capacity, width = arrived.shape
+    rows = slots.shape[0]
     return pl.pallas_call(
         _cross_kernel,
         out_shape=jax.ShapeDtypeStruct((rows, 2 * BINS), jnp.bfloat16),
         grid=(rows // block,),
-        in_specs=specs,
+        in_specs=[
+            pl.BlockSpec((block, 1), lambda i: (i, 0)),
+            pl.BlockSpec(arrived.shape, lambda i: (0, 0, 0, 0), pipeline_mode=pl.Buffered(1)),
+            pl.BlockSpec((2 * SEG, block, BINS), lambda i: (0, i, 0)),
+            pl.BlockSpec((NFFT, 2 * BINS), lambda i: (0, 0), pipeline_mode=pl.Buffered(1)),
+            pl.BlockSpec((slabs // SEG, width), lambda i: (0, 0)),
+        ],
         out_specs=pl.BlockSpec((block, 2 * BINS), lambda i: (i, 0)),
         compiler_params=pltpu.CompilerParams(vmem_limit_bytes=48 * 1024 * 1024),
         cost_estimate=pl.CostEstimate(
             flops=2 * SEG * rows * NFFT * 2 * BINS, transcendentals=SEG * rows * BINS,
-            bytes_accessed=NFFT * 2 * BINS * 2 + 8 * slabs * rows * width,
+            bytes_accessed=NFFT * 2 * BINS * 2 + 2 * arrived.size,
         ),
-    )(parts, first_white, table, taper)
+    )(slots.reshape(rows, 1), arrived, first_white, table, taper)
 
 
 def _exchange_kernel(axis, x_ref, out_ref, landed, send_sems, recv_sems):
@@ -299,10 +315,7 @@
     served = served.reshape(regions * slabs, capacity, width)
     arrived = lax.all_to_all(served, ("region", "slab"), split_axis=0, concat_axis=0, tiled=True)
     arrived, first_white = lax.optimization_barrier((arrived, first_white))
-    own_slots = jnp.broadcast_to(slot_index[None, :], (slabs, pair_count))
-    second_arrived = compact_rows(arrived.reshape(regions, slabs, capacity, width), own_slots)
-    return cross_rows(second_arrived, first_white, table, taper)
-
+    return cross_rows(arrived.reshape(regions, slabs, capacity, width), slot_index, first_white, table, taper)
 
 def solution(mesh):
     placed = (

time: 204 us -> 199 us (0.975)
  Pallas kernels: 79 us -> 75.3 us
  starting transfers between devices: 11.6 us -> 8.9 us
  waiting for transfers between devices: 11.7 us -> 13.8 us
    pallas_call x1 -> x0, Pallas kernels: 3.96 us -> none  [compact_rows(): pl.pallas_call(_compact_kernel, out_shape=jax.ShapeDtypeStruct((slabs, pa...]
    all_to_all x1, starting transfers between devices: 11.6 us -> 8.9 us  [local(): lax.all_to_all(served, ('region', 'slab'), split_axis=0, concat_axis=0, t...]
    all_to_all x1, waiting for transfers between devices: 11.7 us -> 13.8 us  [local(): lax.all_to_all(served, ('region', 'slab'), split_axis=0, concat_axis=0, t...]
  transfers between devices with their start and end apart: 1 -> 1, of which waited for: 1 -> 1; matrix products, arithmetic and copies ran while one was open for 8% -> 9% of each run, Pallas kernels for 23% -> 23%
where the time goes in v9:
time: 199 us; the launch traced here: 198 us
  Pallas kernels  75.3 us (38%)
  blocking collectives  71.1 us (36%)
  other arithmetic  18.6 us (9%)
  waiting for transfers between devices  13.8 us (7%)
  local copies, waits for them, and re-layouts  9.85 us (5%)
  starting transfers between devices  8.9 us (4%)
    all_to_all x1, blocking collectives, local(): lax.all_to_all(outgoing.reshape(regions * slabs, capacity), ('region', 's...  48.9 us
    pallas_call x1, Pallas kernels, exchange(): pl.pallas_call(functools.partial(_exchange_kernel, axis), out_shape=jax.S...  25.7 us
    pallas_call x2, Pallas kernels, pick_rows(): pl.pallas_call(_pick_kernel, out_shape=jax.ShapeDtypeStruct((count, width...  22.2 us
    all_gather x1, blocking collectives, local(): firsts = lax.all_gather(first_station, 'slab', axis=0, tiled=False)  22.2 us
    pallas_call x1, Pallas kernels, cross_rows(): pl.pallas_call(_cross_kernel, out_shape=jax.ShapeDtypeStruct((rows, 2 * B...  14.9 us
    all_to_all x1, waiting for transfers between devices, local(): lax.all_to_all(served, ('region', 'slab'), split_axis=0, concat_axis=0, t...  13.8 us
    pallas_call x1, Pallas kernels, white_rows(): pl.pallas_call(_white_kernel, out_shape=jax.ShapeDtypeStruct((2 * SEG, ro...  12.6 us
    all_to_all x1, starting transfers between devices, local(): lax.all_to_all(served, ('region', 'slab'), split_axis=0, concat_axis=0, t...  8.9 us
  transfers between devices with their start and end apart: 1, of which 1 were waited for; matrix products, arithmetic and copies ran while one was open for 9% of the time, Pallas kernels for 23%

profile of v9, /device:TPU:1, one launch (start us, length us, event | category | flops | bytes accessed | tf_op | source)
XLA Modules:
  0.0 197.6 jit_solution(5306501943667809630)
XLA Ops:
  0.0 0.7 broadcast_multiply_fusion
  0.7 0.7 fusion.17
  1.4 0.2 reduce_window_sum.11
  1.6 0.8 select_reduce_fusion
  2.4 0.1 copy.19
  2.5 0.1 copy.18
  2.6 0.1 fusion.14
  2.8 1.1 scatter_custom_fusion
  3.9 0.1 broadcast_in_dim.7
  4.0 48.9 %all_to_all.14 = s32[512,1,16]{2,1,0:T(1,128)S(1)} all-to-all(s32[512,1,16]{2,1,0:T(1,128)S(1)} %bitcast.15), channel_id=1, replica_groups=mesh['region'=16,'slab'=32] {'region','slab'}, dimensions={0} | all-to-all | bytes 65536 | tf_op jit(solution)/shard_map/all_to_all | solution.py:304
  52.8 0.5 broadcast.153
  53.4 1.3 reduce.5
  54.7 0.0 copy-start.3
  54.7 3.6 %reshape_reshape.8.ids_ref = s32[8192,1]{1,0:T(8,128)} reshape(s32[512,16]{1,0:T(8,128)S(1)} %reduce.5) | data formatting | bytes 65536 | tf_op jit(solution)/shard_map/reshape;reshape | solution.py:89
  58.3 14.4 %shard_map.46 = bf16[8192,128]{1,0:T(8,128)(2,1)} custom-call(s32[8192,1]{1,0:T(8,128)} %reshape_reshape.8.ids_ref, bf16[1024,128]{1,0:T(8,128)(2,1)} %table_ref.3), custom_call_target="tpu_custom_call" | custom-call | flops 2147483648 | bytes 2359296 | tf_op jit(solution)/shard_map/pallas_call | solution.py:77
  72.6 8.9 %all-to-all-start.1 = ((bf16[512,16,128]{2,1,0:T(8,128)(2,1)}), bf16[512,16,128]{2,1,0:T(8,128)(2,1)S(1)}, u32[]{:S(2)}, u32[]{:S(2)}) async-start(bf16[512,16,128]{2,1,0:T(8,128)(2,1)} %bitcast.13), calls=%async_computation.1 | async-start | bytes 4194304 | tf_op jit(solution)/shard_map/all_to_all | solution.py:316
  81.5 0.0 copy-done.3
  81.6 22.2 %all-gather.1 = s32[32,1,128]{2,1,0:T(1,128)S(1)} all-gather(s32[1,1,128]{2,1,0:T(1,128)S(1)} %bitcast.20), channel_id=2, replica_groups=mesh['region'=16,'slab'=32] {'slab'}, dimensions={0}, use_global_device_ids=true | all-gather | bytes 16896 | tf_op jit(solution)/shard_map/all_gather | solution.py:307
  103.8 2.0 %copy.21.ids_ref = s32[4096,1]{1,0:T(8,128)} copy(s32[4096,1]{0,1:T(1,128)S(1)} %bitcast.16) | data formatting | bytes 32768 | tf_op jit(solution)/shard_map/reshape;reshape | solution.py:89
  105.8 7.8 %shard_map.47 = bf16[4096,128]{1,0:T(8,128)(2,1)} custom-call(s32[4096,1]{1,0:T(8,128)} %copy.21.ids_ref, bf16[1024,128]{1,0:T(8,128)(2,1)} %table_ref.3), custom_call_target="tpu_custom_call" | custom-call | flops 1073741824 | bytes 1310720 | tf_op jit(solution)/shard_map/pallas_call | solution.py:77
  113.6 25.7 %shard_map.48.x_ref = bf16[32,128,128]{2,1,0:T(8,128)(2,1)} custom-call(bf16[32,128,128]{2,1,0:T(8,128)(2,1)} %bitcast.14), custom_call_target="tpu_custom_call" | custom-call | bytes 2097152 | tf_op jit(solution)/shard_map/pallas_call | solution.py:269
  139.3 0.1 multiply_subtract_fusion.taper_ref
  139.3 0.5 fusion.15
  139.9 1.0 fusion.9
  140.9 5.0 %subtract_convert_fusion = (bf16[32,64,1024]{2,1,0:T(8,128)(2,1)}, bf16[32,64,1024]{2,1,0:T(8,128)(2,1)}) fusion(f32[64,1024]{1,0:T(8,128)S(1)} %get-tuple-element.13, f32[32,1024]{1,0:T(8,128)S(1)} %get-tuple-element.15, f32[64,1024]{1,0:T(8,128)S(1)} %get-tuple-element.14, f32[32,1024]{1,0:T(8,128)S(1)} %get-tuple-element.16), kind=kLoop, calls=%fused_computation.3 | loop fusion | flops 18874368 | bytes 9175040 | tf_op jit(solution)/shard_map/convert.3
  145.9 0.0 copy-start
  145.9 8.2 %pad_maximum_fusion.table_ref = bf16[2048,2048]{1,0:T(8,128)(2,1)} fusion(bf16[2048,1024]{1,0:T(8,128)(2,1)} %bitcast.12, bf16[2048,1024]{1,0:T(8,128)(2,1)} %bitcast.11), kind=kLoop, calls=%fused_computation.1 | loop fusion | flops 16777216 | bytes 16777216 | tf_op jit(solution)/shard_map/concatenate | solution.py:29
  154.1 0.0 copy-done
  154.1 12.6 %shard_map.49.first_ref = bf16[4,128,1024]{2,1,0:T(8,128)(2,1)S(1)} custom-call(bf16[32,128,128]{2,1,0:T(8,128)(2,1)S(1)} %copy-done, bf16[2048,2048]{1,0:T(8,128)(2,1)} %pad_maximum_fusion.table_ref, f32[16,128]{1,0:T(8,128)S(1)} %multiply_subtract_fusion.taper_ref), custom_call_target="tpu_custom_call" | custom-call | flops 2147483648 | bytes 10485760 | tf_op jit(solution)/shard_map/pallas_call | solution.py:197
  166.7 0.0 copy-start.1
  166.7 1.1 copy-done.1
  167.7 13.8 %all-to-all-done.1 = bf16[512,16,128]{2,1,0:T(8,128)(2,1)S(1)} async-done(((bf16[512,16,128]{2,1,0:T(8,128)(2,1)}), bf16[512,16,128]{2,1,0:T(8,128)(2,1)S(1)}, u32[]{:S(2)}, u32[]{:S(2)}) %all-to-all-start.1) | async-done | bytes 2097184 | tf_op jit(solution)/shard_map/all_to_all | solution.py:316
  181.5 0.0 copy-start.2
  181.5 1.2 copy-done.2
  182.7 14.9 %shard_map.50 = bf16[128,2048]{1,0:T(8,128)(2,1)} custom-call(s32[128,1]{1,0:T(8,128)S(1)} %get-tuple-element.10.ids_ref, bf16[16,32,16,128]{3,2,1,0:T(8,128)(2,1)S(1)} %bitcast.10, bf16[4,128,1024]{2,1,0:T(8,128)(2,1)S(1)} %copy-done.2, bf16[2048,2048]{1,0:T(8,128)(2,1)} %pad_maximum_fusion.table_ref, f32[16,128]{1,0:T(8,128)S(1)} %multiply_subtract_fusion.taper_ref), custom_call_target="tpu_custom_call" | custom-call | flops 2147483648 | bytes 10485760 | tf_op jit(solution)/shard_map/pallas_call | solution.py:214
  (1 shorter events, 0.0 us)
Async XLA Ops:
  54.7 26.9 %copy-start.3 = (s32[128]{0:T(128)S(1)}, s32[128]{0:T(128)}, u32[]{:S(2)}) copy-start(s32[128]{0:T(128)} %param.5) | copy-start | bytes 1540
  72.6 108.9 %all-to-all-start.1 = ((bf16[512,16,128]{2,1,0:T(8,128)(2,1)}), bf16[512,16,128]{2,1,0:T(8,128)(2,1)S(1)}, u32[]{:S(2)}, u32[]{:S(2)}) async-start(bf16[512,16,128]{2,1,0:T(8,128)(2,1)} %bitcast.13), calls=%async_computation.1 | async-start | bytes 4194304 | tf_op jit(solution)/shard_map/all_to_all | solution.py:316
  145.9 8.2 %copy-start = (bf16[32,128,128]{2,1,0:T(8,128)(2,1)S(1)}, bf16[32,128,128]{2,1,0:T(8,128)(2,1)}, u32[]{:S(2)}) copy-start(bf16[32,128,128]{2,1,0:T(8,128)(2,1)} %shard_map.48.x_ref) | copy-start | bytes 3145732
  166.7 1.1 copy-start.1
  181.5 1.2 copy-start.2

commit v10 on v9

--- a/solution.py
+++ b/solution.py
@@ -191,7 +191,7 @@
     ]
 
 
-def white_rows(parts, table, taper, block=32):
+def white_rows(parts, table, taper, block=128):
     slabs, rows, width = parts.shape
     specs = _white_specs(slabs, block, width, slabs // SEG)
     return pl.pallas_call(
@@ -208,7 +208,7 @@
     )(parts, table, taper)
 
 
-def cross_rows(arrived, slots, first_white, table, taper, block=32):
+def cross_rows(arrived, slots, first_white, table, taper, block=128):
     buckets, slabs, capacity, width = arrived.shape
     rows = slots.shape[0]
     return pl.pallas_call(

time: 199 us -> 194 us (0.975)
  Pallas kernels: 75.3 us -> 66 us
  waiting for transfers between devices: 13.8 us -> 18 us
    pallas_call x1, Pallas kernels: 14.9 us -> 9.75 us  [cross_rows(): pl.pallas_call(_cross_kernel, out_shape=jax.ShapeDtypeStruct((rows, 2 * B...]
    all_to_all x1, waiting for transfers between devices: 13.8 us -> 18 us  [local(): lax.all_to_all(served, ('region', 'slab'), split_axis=0, concat_axis=0, t...]
    pallas_call x1, Pallas kernels: 12.6 us -> 8.34 us  [white_rows(): pl.pallas_call(_white_kernel, out_shape=jax.ShapeDtypeStruct((2 * SEG, ro...]
  transfers between devices with their start and end apart: 1 -> 1, of which waited for: 1 -> 1; matrix products, arithmetic and copies ran while one was open for 9% -> 9% of each run, Pallas kernels for 23% -> 22%
where the time goes in v10:
time: 194 us; the launch traced here: 192 us
  blocking collectives  71.1 us (37%)
  Pallas kernels  66 us (34%)
  other arithmetic  18.6 us (10%)
  waiting for transfers between devices  18 us (9%)
  local copies, waits for them, and re-layouts  9.85 us (5%)
  starting transfers between devices  8.9 us (5%)
    all_to_all x1, blocking collectives, local(): lax.all_to_all(outgoing.reshape(regions * slabs, capacity), ('region', 's...  48.9 us
    pallas_call x1, Pallas kernels, exchange(): pl.pallas_call(functools.partial(_exchange_kernel, axis), out_shape=jax.S...  25.7 us
    pallas_call x2, Pallas kernels, pick_rows(): pl.pallas_call(_pick_kernel, out_shape=jax.ShapeDtypeStruct((count, width...  22.2 us
    all_gather x1, blocking collectives, local(): firsts = lax.all_gather(first_station, 'slab', axis=0, tiled=False)  22.2 us
    all_to_all x1, waiting for transfers between devices, local(): lax.all_to_all(served, ('region', 'slab'), split_axis=0, concat_axis=0, t...  18 us
    pallas_call x1, Pallas kernels, cross_rows(): pl.pallas_call(_cross_kernel, out_shape=jax.ShapeDtypeStruct((rows, 2 * B...  9.75 us
    all_to_all x1, starting transfers between devices, local(): lax.all_to_all(served, ('region', 'slab'), split_axis=0, concat_axis=0, t...  8.9 us
    pallas_call x1, Pallas kernels, white_rows(): pl.pallas_call(_white_kernel, out_shape=jax.ShapeDtypeStruct((2 * SEG, ro...  8.34 us
  transfers between devices with their start and end apart: 1, of which 1 were waited for; matrix products, arithmetic and copies ran while one was open for 9% of the time, Pallas kernels for 22%

profile of v10, /device:TPU:1, one launch (start us, length us, event | category | flops | bytes accessed | tf_op | source)
XLA Modules:
  0.0 192.5 jit_solution(27013860874185073)
XLA Ops:
  0.0 0.7 broadcast_multiply_fusion
  0.7 0.7 fusion.17
  1.4 0.2 reduce_window_sum.11
  1.6 0.8 select_reduce_fusion
  2.4 0.1 copy.19
  2.5 0.1 copy.18
  2.6 0.1 fusion.14
  2.8 1.1 scatter_custom_fusion
  3.9 0.1 broadcast_in_dim.7
  4.0 48.9 %all_to_all.14 = s32[512,1,16]{2,1,0:T(1,128)S(1)} all-to-all(s32[512,1,16]{2,1,0:T(1,128)S(1)} %bitcast.15), channel_id=1, replica_groups=mesh['region'=16,'slab'=32] {'region','slab'}, dimensions={0} | all-to-all | bytes 65536 | tf_op jit(solution)/shard_map/all_to_all | solution.py:304
  52.8 0.5 broadcast.153
  53.4 1.3 reduce.5
  54.7 0.0 copy-start.3
  54.7 3.6 %reshape_reshape.8.ids_ref = s32[8192,1]{1,0:T(8,128)} reshape(s32[512,16]{1,0:T(8,128)S(1)} %reduce.5) | data formatting | bytes 65536 | tf_op jit(solution)/shard_map/reshape;reshape | solution.py:89
  58.3 14.4 %shard_map.46 = bf16[8192,128]{1,0:T(8,128)(2,1)} custom-call(s32[8192,1]{1,0:T(8,128)} %reshape_reshape.8.ids_ref, bf16[1024,128]{1,0:T(8,128)(2,1)} %table_ref.3), custom_call_target="tpu_custom_call" | custom-call | flops 2147483648 | bytes 2359296 | tf_op jit(solution)/shard_map/pallas_call | solution.py:77
  72.6 8.9 %all-to-all-start.1 = ((bf16[512,16,128]{2,1,0:T(8,128)(2,1)}), bf16[512,16,128]{2,1,0:T(8,128)(2,1)S(1)}, u32[]{:S(2)}, u32[]{:S(2)}) async-start(bf16[512,16,128]{2,1,0:T(8,128)(2,1)} %bitcast.13), calls=%async_computation.1 | async-start | bytes 4194304 | tf_op jit(solution)/shard_map/all_to_all | solution.py:316
  81.5 0.0 copy-done.3
  81.6 22.2 %all-gather.1 = s32[32,1,128]{2,1,0:T(1,128)S(1)} all-gather(s32[1,1,128]{2,1,0:T(1,128)S(1)} %bitcast.20), channel_id=2, replica_groups=mesh['region'=16,'slab'=32] {'slab'}, dimensions={0}, use_global_device_ids=true | all-gather | bytes 16896 | tf_op jit(solution)/shard_map/all_gather | solution.py:307
  103.8 2.0 %copy.21.ids_ref = s32[4096,1]{1,0:T(8,128)} copy(s32[4096,1]{0,1:T(1,128)S(1)} %bitcast.16) | data formatting | bytes 32768 | tf_op jit(solution)/shard_map/reshape;reshape | solution.py:89
  105.8 7.8 %shard_map.47 = bf16[4096,128]{1,0:T(8,128)(2,1)} custom-call(s32[4096,1]{1,0:T(8,128)} %copy.21.ids_ref, bf16[1024,128]{1,0:T(8,128)(2,1)} %table_ref.3), custom_call_target="tpu_custom_call" | custom-call | flops 1073741824 | bytes 1310720 | tf_op jit(solution)/shard_map/pallas_call | solution.py:77
  113.6 25.7 %shard_map.48.x_ref = bf16[32,128,128]{2,1,0:T(8,128)(2,1)} custom-call(bf16[32,128,128]{2,1,0:T(8,128)(2,1)} %bitcast.14), custom_call_target="tpu_custom_call" | custom-call | bytes 2097152 | tf_op jit(solution)/shard_map/pallas_call | solution.py:269
  139.3 0.1 multiply_subtract_fusion.taper_ref
  139.3 0.5 fusion.15
  139.9 1.0 fusion.9
  140.9 5.0 %subtract_convert_fusion = (bf16[32,64,1024]{2,1,0:T(8,128)(2,1)}, bf16[32,64,1024]{2,1,0:T(8,128)(2,1)}) fusion(f32[64,1024]{1,0:T(8,128)S(1)} %get-tuple-element.13, f32[32,1024]{1,0:T(8,128)S(1)} %get-tuple-element.15, f32[64,1024]{1,0:T(8,128)S(1)} %get-tuple-element.14, f32[32,1024]{1,0:T(8,128)S(1)} %get-tuple-element.16), kind=kLoop, calls=%fused_computation.3 | loop fusion | flops 18874368 | bytes 9175040 | tf_op jit(solution)/shard_map/convert.3
  145.9 0.0 copy-start
  145.9 8.2 %pad_maximum_fusion.table_ref = bf16[2048,2048]{1,0:T(8,128)(2,1)} fusion(bf16[2048,1024]{1,0:T(8,128)(2,1)} %bitcast.12, bf16[2048,1024]{1,0:T(8,128)(2,1)} %bitcast.11), kind=kLoop, calls=%fused_computation.1 | loop fusion | flops 16777216 | bytes 16777216 | tf_op jit(solution)/shard_map/concatenate | solution.py:29
  154.1 0.0 copy-done
  154.1 8.3 %shard_map.49.first_ref = bf16[4,128,1024]{2,1,0:T(8,128)(2,1)S(1)} custom-call(bf16[32,128,128]{2,1,0:T(8,128)(2,1)S(1)} %copy-done, bf16[2048,2048]{1,0:T(8,128)(2,1)} %pad_maximum_fusion.table_ref, f32[16,128]{1,0:T(8,128)S(1)} %multiply_subtract_fusion.taper_ref), custom_call_target="tpu_custom_call" | custom-call | flops 2147483648 | bytes 10485760 | tf_op jit(solution)/shard_map/pallas_call | solution.py:197
  162.5 0.0 copy-start.1
  162.5 1.1 copy-done.1
  163.5 18.0 %all-to-all-done.1 = bf16[512,16,128]{2,1,0:T(8,128)(2,1)S(1)} async-done(((bf16[512,16,128]{2,1,0:T(8,128)(2,1)}), bf16[512,16,128]{2,1,0:T(8,128)(2,1)S(1)}, u32[]{:S(2)}, u32[]{:S(2)}) %all-to-all-start.1) | async-done | bytes 2097184 | tf_op jit(solution)/shard_map/all_to_all | solution.py:316
  181.5 0.0 copy-start.2
  181.5 1.2 copy-done.2
  182.7 9.8 %shard_map.50 = bf16[128,2048]{1,0:T(8,128)(2,1)} custom-call(s32[128,1]{1,0:T(8,128)S(1)} %get-tuple-element.10.ids_ref, bf16[16,32,16,128]{3,2,1,0:T(8,128)(2,1)S(1)} %bitcast.10, bf16[4,128,1024]{2,1,0:T(8,128)(2,1)S(1)} %copy-done.2, bf16[2048,2048]{1,0:T(8,128)(2,1)} %pad_maximum_fusion.table_ref, f32[16,128]{1,0:T(8,128)S(1)} %multiply_subtract_fusion.taper_ref), custom_call_target="tpu_custom_call" | custom-call | flops 2147483648 | bytes 10485760 | tf_op jit(solution)/shard_map/pallas_call | solution.py:214
  (1 shorter events, 0.0 us)
Async XLA Ops:
  54.7 26.9 %copy-start.3 = (s32[128]{0:T(128)S(1)}, s32[128]{0:T(128)}, u32[]{:S(2)}) copy-start(s32[128]{0:T(128)} %param.5) | copy-start | bytes 1540
  72.6 108.9 %all-to-all-start.1 = ((bf16[512,16,128]{2,1,0:T(8,128)(2,1)}), bf16[512,16,128]{2,1,0:T(8,128)(2,1)S(1)}, u32[]{:S(2)}, u32[]{:S(2)}) async-start(bf16[512,16,128]{2,1,0:T(8,128)(2,1)} %bitcast.13), calls=%async_computation.1 | async-start | bytes 4194304 | tf_op jit(solution)/shard_map/all_to_all | solution.py:316
  145.9 8.2 %copy-start = (bf16[32,128,128]{2,1,0:T(8,128)(2,1)S(1)}, bf16[32,128,128]{2,1,0:T(8,128)(2,1)}, u32[]{:S(2)}) copy-start(bf16[32,128,128]{2,1,0:T(8,128)(2,1)} %shard_map.48.x_ref) | copy-start | bytes 3145732
  162.5 1.1 copy-start.1
  181.5 1.2 copy-start.2

commit v11 on v10

--- a/solution.py
+++ b/solution.py
@@ -300,9 +300,12 @@
         .at[slot_index]
         .set(second_station)
     )
-    outgoing = jnp.broadcast_to(requests.reshape(regions, 1, capacity), (regions, slabs, capacity))
-    asked = lax.all_to_all(outgoing.reshape(regions * slabs, capacity), ("region", "slab"), split_axis=0, concat_axis=0, tiled=True)
-    asked = asked.reshape(-1)
+    own = jnp.pad(requests.reshape(-1, 128), ((0, (-(regions * capacity // 128)) % 8), (0, 0)))
+    plane = exchange(jnp.broadcast_to(own[None], (slabs,) + own.shape), "slab", 2)
+    plane_requests = plane[:, : regions * capacity // 128].reshape(slabs, regions, capacity)
+    outgoing = jnp.transpose(plane_requests, (1, 0, 2)).reshape(regions, -1, 128)
+    outgoing = jnp.pad(outgoing, ((0, 0), (0, (-outgoing.shape[1]) % 8), (0, 0)))
+    asked = exchange(outgoing, "region", 1)[:, : slabs * capacity // 128].reshape(-1)
 
     firsts = lax.all_gather(first_station, "slab", axis=0, tiled=False)
     first_parts = pick_rows(records, firsts.reshape(-1)).reshape(slabs, pair_count, width)

time: 194 us -> 189 us (0.974)
  blocking collectives: 71.1 us -> 21.9 us
  Pallas kernels: 66 us -> 101 us
  starting transfers between devices: 8.9 us -> 17.4 us
    all_to_all x1 -> x0, blocking collectives: 48.9 us -> none  [local(): lax.all_to_all(outgoing.reshape(regions * slabs, capacity), ('region', 's...]
    pallas_call x1 -> x3, Pallas kernels: 25.7 us -> 60.7 us  [exchange(): pl.pallas_call(functools.partial(_exchange_kernel, axis), out_shape=jax.S...]
    all_to_all x1, starting transfers between devices: 8.9 us -> 17.4 us  [local(): lax.all_to_all(served, ('region', 'slab'), split_axis=0, concat_axis=0, t...]
  transfers between devices with their start and end apart: 1 -> 1, of which waited for: 1 -> 1; matrix products, arithmetic and copies ran while one was open for 9% -> 9% of each run, Pallas kernels for 22% -> 23%
where the time goes in v11:
time: 189 us; the launch traced here: 187 us
  Pallas kernels  101 us (53%)
  blocking collectives  21.9 us (12%)
  waiting for transfers between devices  17.6 us (9%)
  starting transfers between devices  17.4 us (9%)
  other arithmetic  17.3 us (9%)
  local copies, waits for them, and re-layouts  11.7 us (6%)
    pallas_call x3, Pallas kernels, exchange(): pl.pallas_call(functools.partial(_exchange_kernel, axis), out_shape=jax.S...  60.7 us
    pallas_call x2, Pallas kernels, pick_rows(): pl.pallas_call(_pick_kernel, out_shape=jax.ShapeDtypeStruct((count, width...  22.2 us
    all_gather x1, blocking collectives, local(): firsts = lax.all_gather(first_station, 'slab', axis=0, tiled=False)  21.9 us
    all_to_all x1, waiting for transfers between devices, local(): lax.all_to_all(served, ('region', 'slab'), split_axis=0, concat_axis=0, t...  17.6 us
    all_to_all x1, starting transfers between devices, local(): lax.all_to_all(served, ('region', 'slab'), split_axis=0, concat_axis=0, t...  17.4 us
    pallas_call x1, Pallas kernels, cross_rows(): pl.pallas_call(_cross_kernel, out_shape=jax.ShapeDtypeStruct((rows, 2 * B...  9.75 us
    pallas_call x1, Pallas kernels, white_rows(): pl.pallas_call(_white_kernel, out_shape=jax.ShapeDtypeStruct((2 * SEG, ro...  8.34 us
    concatenate x1, other arithmetic, dft_table(): return jnp.concatenate([cos_part, -sin_part], axis=1).astype(jnp.bfloat16)  8.22 us
  transfers between devices with their start and end apart: 1, of which 1 were waited for; matrix products, arithmetic and copies ran while one was open for 9% of the time, Pallas kernels for 23%

profile of v11, /device:TPU:1, one launch (start us, length us, event | category | flops | bytes accessed | tf_op | source)
XLA Modules:
  0.0 187.1 jit_solution(9509741146517961489)
XLA Ops:
  0.0 0.7 broadcast_multiply_fusion
  0.7 0.7 fusion.17
  1.4 0.2 reduce_window_sum.11
  1.6 0.8 select_reduce_fusion
  2.4 0.1 copy.24
  2.5 0.1 copy.23
  2.6 0.1 fusion.14
  2.8 1.1 scatter_custom_fusion
  3.9 0.7 broadcast_in_dim.5.x_ref
  4.6 17.4 %shard_map.46 = s32[32,8,128]{2,1,0:T(8,128)} custom-call(s32[32,8,128]{2,1,0:T(8,128)} %broadcast_in_dim.5.x_ref), custom_call_target="tpu_custom_call" | custom-call | bytes 131072 | tf_op jit(solution)/shard_map/pallas_call | solution.py:269
  22.0 0.9 slice.6
  22.9 0.1 copy.25
  23.0 0.1 copy.26
  23.1 0.1 reshape.115
  23.3 0.0 copy-start.3
  23.3 0.6 pad.9.x_ref
  23.9 17.1 %shard_map.47 = s32[16,8,128]{2,1,0:T(8,128)} custom-call(s32[16,8,128]{2,1,0:T(8,128)} %pad.9.x_ref), custom_call_target="tpu_custom_call" | custom-call | bytes 65536 | tf_op jit(solution)/shard_map/pallas_call | solution.py:269
  41.1 0.8 slice.7
  41.9 2.6 %copy.27.ids_ref = s32[8192,1]{1,0:T(8,128)} copy(s32[8192,1]{0,1:T(1,128)S(1)} %bitcast.20) | data formatting | bytes 65536 | tf_op jit(solution)/shard_map/reshape;reshape | solution.py:89
  44.5 14.4 %shard_map.48 = bf16[8192,128]{1,0:T(8,128)(2,1)} custom-call(s32[8192,1]{1,0:T(8,128)} %copy.27.ids_ref, bf16[1024,128]{1,0:T(8,128)(2,1)} %table_ref.3), custom_call_target="tpu_custom_call" | custom-call | flops 2147483648 | bytes 2359296 | tf_op jit(solution)/shard_map/pallas_call | solution.py:77
  58.9 17.4 %all-to-all-start = ((bf16[512,16,128]{2,1,0:T(8,128)(2,1)}), bf16[512,16,128]{2,1,0:T(8,128)(2,1)S(1)}, u32[]{:S(2)}, u32[]{:S(2)}) async-start(bf16[512,16,128]{2,1,0:T(8,128)(2,1)} %bitcast.17), calls=%async_computation | async-start | bytes 4194304 | tf_op jit(solution)/shard_map/all_to_all | solution.py:319
  76.3 0.0 copy-done.3
  76.3 21.9 %all-gather.1 = s32[32,1,128]{2,1,0:T(1,128)S(1)} all-gather(s32[1,1,128]{2,1,0:T(1,128)S(1)} %bitcast.26), channel_id=2, replica_groups=mesh['region'=16,'slab'=32] {'slab'}, dimensions={0}, use_global_device_ids=true | all-gather | bytes 16896 | tf_op jit(solution)/shard_map/all_gather | solution.py:310
  98.2 2.0 %copy.28.ids_ref = s32[4096,1]{1,0:T(8,128)} copy(s32[4096,1]{0,1:T(1,128)S(1)} %bitcast.21) | data formatting | bytes 32768 | tf_op jit(solution)/shard_map/reshape;reshape | solution.py:89
  100.2 7.8 %shard_map.49 = bf16[4096,128]{1,0:T(8,128)(2,1)} custom-call(s32[4096,1]{1,0:T(8,128)} %copy.28.ids_ref, bf16[1024,128]{1,0:T(8,128)(2,1)} %table_ref.3), custom_call_target="tpu_custom_call" | custom-call | flops 1073741824 | bytes 1310720 | tf_op jit(solution)/shard_map/pallas_call | solution.py:77
  108.0 26.2 %shard_map.50.x_ref = bf16[32,128,128]{2,1,0:T(8,128)(2,1)} custom-call(bf16[32,128,128]{2,1,0:T(8,128)(2,1)} %bitcast.18), custom_call_target="tpu_custom_call" | custom-call | bytes 2097152 | tf_op jit(solution)/shard_map/pallas_call | solution.py:269
  134.2 0.1 multiply_subtract_fusion.taper_ref
  134.3 0.5 fusion.15
  134.8 1.0 fusion.9
  135.9 5.0 %subtract_convert_fusion = (bf16[32,64,1024]{2,1,0:T(8,128)(2,1)}, bf16[32,64,1024]{2,1,0:T(8,128)(2,1)}) fusion(f32[64,1024]{1,0:T(8,128)S(1)} %get-tuple-element.13, f32[32,1024]{1,0:T(8,128)S(1)} %get-tuple-element.15, f32[64,1024]{1,0:T(8,128)S(1)} %get-tuple-element.14, f32[32,1024]{1,0:T(8,128)S(1)} %get-tuple-element.16), kind=kLoop, calls=%fused_computation.3 | loop fusion | flops 18874368 | bytes 9175040 | tf_op jit(solution)/shard_map/convert.3
  140.8 0.0 copy-start
  140.8 8.2 %pad_maximum_fusion.table_ref = bf16[2048,2048]{1,0:T(8,128)(2,1)} fusion(bf16[2048,1024]{1,0:T(8,128)(2,1)} %bitcast.16, bf16[2048,1024]{1,0:T(8,128)(2,1)} %bitcast.15), kind=kLoop, calls=%fused_computation.1 | loop fusion | flops 16777216 | bytes 16777216 | tf_op jit(solution)/shard_map/concatenate | solution.py:29
  149.1 0.0 copy-done
  149.1 8.3 %shard_map.51.first_ref = bf16[4,128,1024]{2,1,0:T(8,128)(2,1)S(1)} custom-call(bf16[32,128,128]{2,1,0:T(8,128)(2,1)S(1)} %copy-done, bf16[2048,2048]{1,0:T(8,128)(2,1)} %pad_maximum_fusion.table_ref, f32[16,128]{1,0:T(8,128)S(1)} %multiply_subtract_fusion.taper_ref), custom_call_target="tpu_custom_call" | custom-call | flops 2147483648 | bytes 10485760 | tf_op jit(solution)/shard_map/pallas_call | solution.py:197
  157.4 0.0 copy-start.1
  157.4 1.1 copy-done.1
  158.5 17.6 %all-to-all-done = bf16[512,16,128]{2,1,0:T(8,128)(2,1)S(1)} async-done(((bf16[512,16,128]{2,1,0:T(8,128)(2,1)}), bf16[512,16,128]{2,1,0:T(8,128)(2,1)S(1)}, u32[]{:S(2)}, u32[]{:S(2)}) %all-to-all-start) | async-done | bytes 2097184 | tf_op jit(solution)/shard_map/all_to_all | solution.py:319
  176.1 0.0 copy-start.2
  176.1 1.2 copy-done.2
  177.3 9.8 %shard_map.52 = bf16[128,2048]{1,0:T(8,128)(2,1)} custom-call(s32[128,1]{1,0:T(8,128)S(1)} %get-tuple-element.10.ids_ref, bf16[16,32,16,128]{3,2,1,0:T(8,128)(2,1)S(1)} %bitcast.14, bf16[4,128,1024]{2,1,0:T(8,128)(2,1)S(1)} %copy-done.2, bf16[2048,2048]{1,0:T(8,128)(2,1)} %pad_maximum_fusion.table_ref, f32[16,128]{1,0:T(8,128)S(1)} %multiply_subtract_fusion.taper_ref), custom_call_target="tpu_custom_call" | custom-call | flops 2147483648 | bytes 10485760 | tf_op jit(solution)/shard_map/pallas_call | solution.py:214
  (1 shorter events, 0.0 us)
Async XLA Ops:
  23.3 53.0 %copy-start.3 = (s32[128]{0:T(128)S(1)}, s32[128]{0:T(128)}, u32[]{:S(2)}) copy-start(s32[128]{0:T(128)} %param.5) | copy-start | bytes 1540
  58.9 117.2 %all-to-all-start = ((bf16[512,16,128]{2,1,0:T(8,128)(2,1)}), bf16[512,16,128]{2,1,0:T(8,128)(2,1)S(1)}, u32[]{:S(2)}, u32[]{:S(2)}) async-start(bf16[512,16,128]{2,1,0:T(8,128)(2,1)} %bitcast.17), calls=%async_computation | async-start | bytes 4194304 | tf_op jit(solution)/shard_map/all_to_all | solution.py:319
  140.8 8.2 %copy-start = (bf16[32,128,128]{2,1,0:T(8,128)(2,1)S(1)}, bf16[32,128,128]{2,1,0:T(8,128)(2,1)}, u32[]{:S(2)}) copy-start(bf16[32,128,128]{2,1,0:T(8,128)(2,1)} %shard_map.50.x_ref) | copy-start | bytes 3145732
  157.4 1.1 copy-start.1
  176.1 1.2 copy-start.2

commit v12 on v11

--- a/solution.py
+++ b/solution.py
@@ -70,7 +70,7 @@
     out_ref[...] = jnp.dot(onehot, table_ref[...], preferred_element_type=jnp.float32).astype(out_ref.dtype)
 
 
-def pick_rows(table, ids, block=512):
+def pick_rows(table, ids, block=1024):
     rows, width = table.shape
     count = ids.shape[0]
     block = min(block, count)

time: 189 us -> 183 us (0.968)
  Pallas kernels: 101 us -> 92.9 us
  waiting for transfers between devices: 17.6 us -> 20.6 us
    pallas_call x2, Pallas kernels: 22.2 us -> 14.5 us  [pick_rows(): pl.pallas_call(_pick_kernel, out_shape=jax.ShapeDtypeStruct((count, width...]
    all_to_all x1, waiting for transfers between devices: 17.6 us -> 20.6 us  [local(): lax.all_to_all(served, ('region', 'slab'), split_axis=0, concat_axis=0, t...]
  transfers between devices with their start and end apart: 1 -> 1, of which waited for: 1 -> 1; matrix products, arithmetic and copies ran while one was open for 9% -> 9% of each run, Pallas kernels for 23% -> 22%
where the time goes in v12:
time: 183 us; the launch traced here: 182 us
  Pallas kernels  92.9 us (51%)
  blocking collectives  21.9 us (12%)
  waiting for transfers between devices  20.6 us (11%)
  starting transfers between devices  17.4 us (10%)
  other arithmetic  17.3 us (9%)
  local copies, waits for them, and re-layouts  11.7 us (6%)
    pallas_call x3, Pallas kernels, exchange(): pl.pallas_call(functools.partial(_exchange_kernel, axis), out_shape=jax.S...  60.3 us
    all_gather x1, blocking collectives, local(): firsts = lax.all_gather(first_station, 'slab', axis=0, tiled=False)  21.9 us
    all_to_all x1, waiting for transfers between devices, local(): lax.all_to_all(served, ('region', 'slab'), split_axis=0, concat_axis=0, t...  20.6 us
    all_to_all x1, starting transfers between devices, local(): lax.all_to_all(served, ('region', 'slab'), split_axis=0, concat_axis=0, t...  17.4 us
    pallas_call x2, Pallas kernels, pick_rows(): pl.pallas_call(_pick_kernel, out_shape=jax.ShapeDtypeStruct((count, width...  14.5 us
    pallas_call x1, Pallas kernels, cross_rows(): pl.pallas_call(_cross_kernel, out_shape=jax.ShapeDtypeStruct((rows, 2 * B...  9.75 us
    pallas_call x1, Pallas kernels, white_rows(): pl.pallas_call(_white_kernel, out_shape=jax.ShapeDtypeStruct((2 * SEG, ro...  8.34 us
    concatenate x1, other arithmetic, dft_table(): return jnp.concatenate([cos_part, -sin_part], axis=1).astype(jnp.bfloat16)  8.22 us
  transfers between devices with their start and end apart: 1, of which 1 were waited for; matrix products, arithmetic and copies ran while one was open for 9% of the time, Pallas kernels for 22%

profile of v12, /device:TPU:1, one launch (start us, length us, event | category | flops | bytes accessed | tf_op | source)
XLA Modules:
  0.0 181.9 jit_solution(16062255949551297147)
XLA Ops:
  0.0 0.7 broadcast_multiply_fusion
  0.7 0.7 fusion.17
  1.4 0.2 reduce_window_sum.11
  1.6 0.8 select_reduce_fusion
  2.4 0.1 copy.24
  2.5 0.1 copy.23
  2.6 0.1 fusion.14
  2.8 1.1 scatter_custom_fusion
  3.9 0.7 broadcast_in_dim.5.x_ref
  4.6 17.4 %shard_map.46 = s32[32,8,128]{2,1,0:T(8,128)} custom-call(s32[32,8,128]{2,1,0:T(8,128)} %broadcast_in_dim.5.x_ref), custom_call_target="tpu_custom_call" | custom-call | bytes 131072 | tf_op jit(solution)/shard_map/pallas_call | solution.py:269
  22.0 0.9 slice.6
  22.9 0.1 copy.25
  23.0 0.1 copy.26
  23.1 0.1 reshape.115
  23.3 0.0 copy-start.3
  23.3 0.6 pad.9.x_ref
  23.9 17.1 %shard_map.47 = s32[16,8,128]{2,1,0:T(8,128)} custom-call(s32[16,8,128]{2,1,0:T(8,128)} %pad.9.x_ref), custom_call_target="tpu_custom_call" | custom-call | bytes 65536 | tf_op jit(solution)/shard_map/pallas_call | solution.py:269
  41.1 0.8 slice.7
  41.9 2.6 %copy.27.ids_ref = s32[8192,1]{1,0:T(8,128)} copy(s32[8192,1]{0,1:T(1,128)S(1)} %bitcast.20) | data formatting | bytes 65536 | tf_op jit(solution)/shard_map/reshape;reshape | solution.py:89
  44.5 9.2 %shard_map.48 = bf16[8192,128]{1,0:T(8,128)(2,1)} custom-call(s32[8192,1]{1,0:T(8,128)} %copy.27.ids_ref, bf16[1024,128]{1,0:T(8,128)(2,1)} %table_ref.3), custom_call_target="tpu_custom_call" | custom-call | flops 2147483648 | bytes 2359296 | tf_op jit(solution)/shard_map/pallas_call | solution.py:77
  53.7 17.4 %all-to-all-start = ((bf16[512,16,128]{2,1,0:T(8,128)(2,1)}), bf16[512,16,128]{2,1,0:T(8,128)(2,1)S(1)}, u32[]{:S(2)}, u32[]{:S(2)}) async-start(bf16[512,16,128]{2,1,0:T(8,128)(2,1)} %bitcast.17), calls=%async_computation | async-start | bytes 4194304 | tf_op jit(solution)/shard_map/all_to_all | solution.py:319
  71.1 0.0 copy-done.3
  71.1 21.9 %all-gather.1 = s32[32,1,128]{2,1,0:T(1,128)S(1)} all-gather(s32[1,1,128]{2,1,0:T(1,128)S(1)} %bitcast.26), channel_id=2, replica_groups=mesh['region'=16,'slab'=32] {'slab'}, dimensions={0}, use_global_device_ids=true | all-gather | bytes 16896 | tf_op jit(solution)/shard_map/all_gather | solution.py:310
  93.0 2.0 %copy.28.ids_ref = s32[4096,1]{1,0:T(8,128)} copy(s32[4096,1]{0,1:T(1,128)S(1)} %bitcast.21) | data formatting | bytes 32768 | tf_op jit(solution)/shard_map/reshape;reshape | solution.py:89
  95.0 5.3 %shard_map.49 = bf16[4096,128]{1,0:T(8,128)(2,1)} custom-call(s32[4096,1]{1,0:T(8,128)} %copy.28.ids_ref, bf16[1024,128]{1,0:T(8,128)(2,1)} %table_ref.3), custom_call_target="tpu_custom_call" | custom-call | flops 1073741824 | bytes 1310720 | tf_op jit(solution)/shard_map/pallas_call | solution.py:77
  100.3 25.8 %shard_map.50.x_ref = bf16[32,128,128]{2,1,0:T(8,128)(2,1)} custom-call(bf16[32,128,128]{2,1,0:T(8,128)(2,1)} %bitcast.18), custom_call_target="tpu_custom_call" | custom-call | bytes 2097152 | tf_op jit(solution)/shard_map/pallas_call | solution.py:269
  126.1 0.1 multiply_subtract_fusion.taper_ref
  126.1 0.5 fusion.15
  126.7 1.0 fusion.9
  127.7 5.0 %subtract_convert_fusion = (bf16[32,64,1024]{2,1,0:T(8,128)(2,1)}, bf16[32,64,1024]{2,1,0:T(8,128)(2,1)}) fusion(f32[64,1024]{1,0:T(8,128)S(1)} %get-tuple-element.13, f32[32,1024]{1,0:T(8,128)S(1)} %get-tuple-element.15, f32[64,1024]{1,0:T(8,128)S(1)} %get-tuple-element.14, f32[32,1024]{1,0:T(8,128)S(1)} %get-tuple-element.16), kind=kLoop, calls=%fused_computation.3 | loop fusion | flops 18874368 | bytes 9175040 | tf_op jit(solution)/shard_map/convert.3
  132.7 0.0 copy-start
  132.7 8.2 %pad_maximum_fusion.table_ref = bf16[2048,2048]{1,0:T(8,128)(2,1)} fusion(bf16[2048,1024]{1,0:T(8,128)(2,1)} %bitcast.16, bf16[2048,1024]{1,0:T(8,128)(2,1)} %bitcast.15), kind=kLoop, calls=%fused_computation.1 | loop fusion | flops 16777216 | bytes 16777216 | tf_op jit(solution)/shard_map/concatenate | solution.py:29
  140.9 0.0 copy-done
  140.9 8.3 %shard_map.51.first_ref = bf16[4,128,1024]{2,1,0:T(8,128)(2,1)S(1)} custom-call(bf16[32,128,128]{2,1,0:T(8,128)(2,1)S(1)} %copy-done, bf16[2048,2048]{1,0:T(8,128)(2,1)} %pad_maximum_fusion.table_ref, f32[16,128]{1,0:T(8,128)S(1)} %multiply_subtract_fusion.taper_ref), custom_call_target="tpu_custom_call" | custom-call | flops 2147483648 | bytes 10485760 | tf_op jit(solution)/shard_map/pallas_call | solution.py:197
  149.2 0.0 copy-start.1
  149.3 1.1 copy-done.1
  150.3 20.6 %all-to-all-done = bf16[512,16,128]{2,1,0:T(8,128)(2,1)S(1)} async-done(((bf16[512,16,128]{2,1,0:T(8,128)(2,1)}), bf16[512,16,128]{2,1,0:T(8,128)(2,1)S(1)}, u32[]{:S(2)}, u32[]{:S(2)}) %all-to-all-start) | async-done | bytes 2097184 | tf_op jit(solution)/shard_map/all_to_all | solution.py:319
  170.9 0.0 copy-start.2
  170.9 1.2 copy-done.2
  172.1 9.7 %shard_map.52 = bf16[128,2048]{1,0:T(8,128)(2,1)} custom-call(s32[128,1]{1,0:T(8,128)S(1)} %get-tuple-element.10.ids_ref, bf16[16,32,16,128]{3,2,1,0:T(8,128)(2,1)S(1)} %bitcast.14, bf16[4,128,1024]{2,1,0:T(8,128)(2,1)S(1)} %copy-done.2, bf16[2048,2048]{1,0:T(8,128)(2,1)} %pad_maximum_fusion.table_ref, f32[16,128]{1,0:T(8,128)S(1)} %multiply_subtract_fusion.taper_ref), custom_call_target="tpu_custom_call" | custom-call | flops 2147483648 | bytes 10485760 | tf_op jit(solution)/shard_map/pallas_call | solution.py:214
  (1 shorter events, 0.0 us)
Async XLA Ops:
  23.3 47.8 %copy-start.3 = (s32[128]{0:T(128)S(1)}, s32[128]{0:T(128)}, u32[]{:S(2)}) copy-start(s32[128]{0:T(128)} %param.5) | copy-start | bytes 1540
  53.7 117.2 %all-to-all-start = ((bf16[512,16,128]{2,1,0:T(8,128)(2,1)}), bf16[512,16,128]{2,1,0:T(8,128)(2,1)S(1)}, u32[]{:S(2)}, u32[]{:S(2)}) async-start(bf16[512,16,128]{2,1,0:T(8,128)(2,1)} %bitcast.17), calls=%async_computation | async-start | bytes 4194304 | tf_op jit(solution)/shard_map/all_to_all | solution.py:319
  132.7 8.2 %copy-start = (bf16[32,128,128]{2,1,0:T(8,128)(2,1)S(1)}, bf16[32,128,128]{2,1,0:T(8,128)(2,1)}, u32[]{:S(2)}) copy-start(bf16[32,128,128]{2,1,0:T(8,128)(2,1)} %shard_map.50.x_ref) | copy-start | bytes 3145732
  149.2 1.1 copy-start.1
  170.9 1.2 copy-start.2

commit v13 on v12

--- a/solution.py
+++ b/solution.py
@@ -70,7 +70,7 @@
     out_ref[...] = jnp.dot(onehot, table_ref[...], preferred_element_type=jnp.float32).astype(out_ref.dtype)
 
 
-def pick_rows(table, ids, block=1024):
+def pick_rows(table, ids, block=2048):
     rows, width = table.shape
     count = ids.shape[0]
     block = min(block, count)

time: 183 us -> 182 us (level)
  Pallas kernels: 92.9 us -> 91 us
    pallas_call x2, Pallas kernels: 14.5 us -> 12.2 us  [pick_rows(): pl.pallas_call(_pick_kernel, out_shape=jax.ShapeDtypeStruct((count, width...]
where the time goes in v13:
time: 182 us; the launch traced here: 180 us
  Pallas kernels  91 us (50%)
  blocking collectives  22.1 us (12%)
  waiting for transfers between devices  20.6 us (11%)
  starting transfers between devices  17.4 us (10%)
  other arithmetic  17.3 us (10%)
  local copies, waits for them, and re-layouts  11.7 us (6%)
    pallas_call x3, Pallas kernels, exchange(): pl.pallas_call(functools.partial(_exchange_kernel, axis), out_shape=jax.S...  60.8 us
    all_gather x1, blocking collectives, local(): firsts = lax.all_gather(first_station, 'slab', axis=0, tiled=False)  22.1 us
    all_to_all x1, waiting for transfers between devices, local(): lax.all_to_all(served, ('region', 'slab'), split_axis=0, concat_axis=0, t...  20.6 us
    all_to_all x1, starting transfers between devices, local(): lax.all_to_all(served, ('region', 'slab'), split_axis=0, concat_axis=0, t...  17.4 us
    pallas_call x2, Pallas kernels, pick_rows(): pl.pallas_call(_pick_kernel, out_shape=jax.ShapeDtypeStruct((count, width...  12.2 us
    pallas_call x1, Pallas kernels, cross_rows(): pl.pallas_call(_cross_kernel, out_shape=jax.ShapeDtypeStruct((rows, 2 * B...  9.75 us
    pallas_call x1, Pallas kernels, white_rows(): pl.pallas_call(_white_kernel, out_shape=jax.ShapeDtypeStruct((2 * SEG, ro...  8.34 us
    concatenate x1, other arithmetic, dft_table(): return jnp.concatenate([cos_part, -sin_part], axis=1).astype(jnp.bfloat16)  8.22 us
  transfers between devices with their start and end apart: 1, of which 1 were waited for; matrix products, arithmetic and copies ran while one was open for 9% of the time, Pallas kernels for 22%

profile of v13, /device:TPU:1, one launch (start us, length us, event | category | flops | bytes accessed | tf_op | source)
XLA Modules:
  0.0 180.2 jit_solution(3125483494606999059)
XLA Ops:
  0.0 0.7 broadcast_multiply_fusion
  0.7 0.7 fusion.17
  1.4 0.2 reduce_window_sum.11
  1.6 0.8 select_reduce_fusion
  2.4 0.1 copy.24
  2.5 0.1 copy.23
  2.6 0.1 fusion.14
  2.8 1.1 scatter_custom_fusion
  3.9 0.7 broadcast_in_dim.5.x_ref
  4.6 17.4 %shard_map.46 = s32[32,8,128]{2,1,0:T(8,128)} custom-call(s32[32,8,128]{2,1,0:T(8,128)} %broadcast_in_dim.5.x_ref), custom_call_target="tpu_custom_call" | custom-call | bytes 131072 | tf_op jit(solution)/shard_map/pallas_call | solution.py:269
  22.0 0.9 slice.6
  22.9 0.1 copy.25
  23.0 0.1 copy.26
  23.1 0.1 reshape.115
  23.3 0.0 copy-start.3
  23.3 0.6 pad.9.x_ref
  23.9 17.1 %shard_map.47 = s32[16,8,128]{2,1,0:T(8,128)} custom-call(s32[16,8,128]{2,1,0:T(8,128)} %pad.9.x_ref), custom_call_target="tpu_custom_call" | custom-call | bytes 65536 | tf_op jit(solution)/shard_map/pallas_call | solution.py:269
  41.1 0.8 slice.7
  41.9 2.6 %copy.27.ids_ref = s32[8192,1]{1,0:T(8,128)} copy(s32[8192,1]{0,1:T(1,128)S(1)} %bitcast.20) | data formatting | bytes 65536 | tf_op jit(solution)/shard_map/reshape;reshape | solution.py:89
  44.5 7.5 %shard_map.48 = bf16[8192,128]{1,0:T(8,128)(2,1)} custom-call(s32[8192,1]{1,0:T(8,128)} %copy.27.ids_ref, bf16[1024,128]{1,0:T(8,128)(2,1)} %table_ref.3), custom_call_target="tpu_custom_call" | custom-call | flops 2147483648 | bytes 2359296 | tf_op jit(solution)/shard_map/pallas_call | solution.py:77
  52.0 17.4 %all-to-all-start = ((bf16[512,16,128]{2,1,0:T(8,128)(2,1)}), bf16[512,16,128]{2,1,0:T(8,128)(2,1)S(1)}, u32[]{:S(2)}, u32[]{:S(2)}) async-start(bf16[512,16,128]{2,1,0:T(8,128)(2,1)} %bitcast.17), calls=%async_computation | async-start | bytes 4194304 | tf_op jit(solution)/shard_map/all_to_all | solution.py:319
  69.4 0.0 copy-done.3
  69.4 22.1 %all-gather.1 = s32[32,1,128]{2,1,0:T(1,128)S(1)} all-gather(s32[1,1,128]{2,1,0:T(1,128)S(1)} %bitcast.26), channel_id=2, replica_groups=mesh['region'=16,'slab'=32] {'slab'}, dimensions={0}, use_global_device_ids=true | all-gather | bytes 16896 | tf_op jit(solution)/shard_map/all_gather | solution.py:310
  91.4 2.0 %copy.28.ids_ref = s32[4096,1]{1,0:T(8,128)} copy(s32[4096,1]{0,1:T(1,128)S(1)} %bitcast.21) | data formatting | bytes 32768 | tf_op jit(solution)/shard_map/reshape;reshape | solution.py:89
  93.4 4.7 %shard_map.49 = bf16[4096,128]{1,0:T(8,128)(2,1)} custom-call(s32[4096,1]{1,0:T(8,128)} %copy.28.ids_ref, bf16[1024,128]{1,0:T(8,128)(2,1)} %table_ref.3), custom_call_target="tpu_custom_call" | custom-call | flops 1073741824 | bytes 1310720 | tf_op jit(solution)/shard_map/pallas_call | solution.py:77
  98.1 26.2 %shard_map.50.x_ref = bf16[32,128,128]{2,1,0:T(8,128)(2,1)} custom-call(bf16[32,128,128]{2,1,0:T(8,128)(2,1)} %bitcast.18), custom_call_target="tpu_custom_call" | custom-call | bytes 2097152 | tf_op jit(solution)/shard_map/pallas_call | solution.py:269
  124.4 0.1 multiply_subtract_fusion.taper_ref
  124.4 0.5 fusion.15
  125.0 1.0 fusion.9
  126.0 5.0 %subtract_convert_fusion = (bf16[32,64,1024]{2,1,0:T(8,128)(2,1)}, bf16[32,64,1024]{2,1,0:T(8,128)(2,1)}) fusion(f32[64,1024]{1,0:T(8,128)S(1)} %get-tuple-element.13, f32[32,1024]{1,0:T(8,128)S(1)} %get-tuple-element.15, f32[64,1024]{1,0:T(8,128)S(1)} %get-tuple-element.14, f32[32,1024]{1,0:T(8,128)S(1)} %get-tuple-element.16), kind=kLoop, calls=%fused_computation.3 | loop fusion | flops 18874368 | bytes 9175040 | tf_op jit(solution)/shard_map/convert.3
  131.0 0.0 copy-start
  131.0 8.2 %pad_maximum_fusion.table_ref = bf16[2048,2048]{1,0:T(8,128)(2,1)} fusion(bf16[2048,1024]{1,0:T(8,128)(2,1)} %bitcast.16, bf16[2048,1024]{1,0:T(8,128)(2,1)} %bitcast.15), kind=kLoop, calls=%fused_computation.1 | loop fusion | flops 16777216 | bytes 16777216 | tf_op jit(solution)/shard_map/concatenate | solution.py:29
  139.2 0.0 copy-done
  139.2 8.3 %shard_map.51.first_ref = bf16[4,128,1024]{2,1,0:T(8,128)(2,1)S(1)} custom-call(bf16[32,128,128]{2,1,0:T(8,128)(2,1)S(1)} %copy-done, bf16[2048,2048]{1,0:T(8,128)(2,1)} %pad_maximum_fusion.table_ref, f32[16,128]{1,0:T(8,128)S(1)} %multiply_subtract_fusion.taper_ref), custom_call_target="tpu_custom_call" | custom-call | flops 2147483648 | bytes 10485760 | tf_op jit(solution)/shard_map/pallas_call | solution.py:197
  147.6 0.0 copy-start.1
  147.6 1.1 copy-done.1
  148.6 20.6 %all-to-all-done = bf16[512,16,128]{2,1,0:T(8,128)(2,1)S(1)} async-done(((bf16[512,16,128]{2,1,0:T(8,128)(2,1)}), bf16[512,16,128]{2,1,0:T(8,128)(2,1)S(1)}, u32[]{:S(2)}, u32[]{:S(2)}) %all-to-all-start) | async-done | bytes 2097184 | tf_op jit(solution)/shard_map/all_to_all | solution.py:319
  169.2 0.0 copy-start.2
  169.2 1.2 copy-done.2
  170.4 9.7 %shard_map.52 = bf16[128,2048]{1,0:T(8,128)(2,1)} custom-call(s32[128,1]{1,0:T(8,128)S(1)} %get-tuple-element.10.ids_ref, bf16[16,32,16,128]{3,2,1,0:T(8,128)(2,1)S(1)} %bitcast.14, bf16[4,128,1024]{2,1,0:T(8,128)(2,1)S(1)} %copy-done.2, bf16[2048,2048]{1,0:T(8,128)(2,1)} %pad_maximum_fusion.table_ref, f32[16,128]{1,0:T(8,128)S(1)} %multiply_subtract_fusion.taper_ref), custom_call_target="tpu_custom_call" | custom-call | flops 2147483648 | bytes 10485760 | tf_op jit(solution)/shard_map/pallas_call | solution.py:214
  (1 shorter events, 0.0 us)
Async XLA Ops:
  23.3 46.1 %copy-start.3 = (s32[128]{0:T(128)S(1)}, s32[128]{0:T(128)}, u32[]{:S(2)}) copy-start(s32[128]{0:T(128)} %param.5) | copy-start | bytes 1540
  52.0 117.2 %all-to-all-start = ((bf16[512,16,128]{2,1,0:T(8,128)(2,1)}), bf16[512,16,128]{2,1,0:T(8,128)(2,1)S(1)}, u32[]{:S(2)}, u32[]{:S(2)}) async-start(bf16[512,16,128]{2,1,0:T(8,128)(2,1)} %bitcast.17), calls=%async_computation | async-start | bytes 4194304 | tf_op jit(solution)/shard_map/all_to_all | solution.py:319
  131.0 8.2 %copy-start = (bf16[32,128,128]{2,1,0:T(8,128)(2,1)S(1)}, bf16[32,128,128]{2,1,0:T(8,128)(2,1)}, u32[]{:S(2)}) copy-start(bf16[32,128,128]{2,1,0:T(8,128)(2,1)} %shard_map.50.x_ref) | copy-start | bytes 3145732
  147.6 1.1 copy-start.1
  169.2 1.2 copy-start.2

commit v14 on v13

--- a/solution.py
+++ b/solution.py
@@ -150,17 +150,23 @@
         out_ref[2 * segment + 1] = white_imag[segment * rows : (segment + 1) * rows]
 
 
-def _cross_kernel(ids_ref, arrived_ref, first_ref, table_ref, taper_ref, out_ref):
+def _cross_kernel(ids_ref, arrived_hbm, first_ref, table_hbm, taper_ref, out_ref, arrived_ref, table_ref, sems):
+    arrived_copy = pltpu.make_async_copy(arrived_hbm, arrived_ref, sems.at[0])
+    table_copy = pltpu.make_async_copy(table_hbm, table_ref, sems.at[1])
+    arrived_copy.start()
+    table_copy.start()
     buckets, slabs, capacity, width = arrived_ref.shape
     ids = ids_ref[...]
     rows = ids.shape[0]
     onehot = (lax.broadcasted_iota(jnp.int32, (rows, buckets * capacity), 1) == ids).astype(arrived_ref.dtype)
+    arrived_copy.wait()
     slices = [
         jnp.dot(onehot, arrived_ref[:, s].reshape(buckets * capacity, width), preferred_element_type=jnp.float32).astype(
             arrived_ref.dtype
         )
         for s in range(slabs)
     ]
+    table_copy.wait()
     white_real, white_imag = _white_block(slices, table_ref[...], taper_ref[...])
     real_sum = None
     imag_sum = None
@@ -208,21 +214,26 @@
     )(parts, table, taper)
 
 
-def cross_rows(arrived, slots, first_white, table, taper, block=128):
+def cross_rows(arrived, slots, first_white, table, taper):
     buckets, slabs, capacity, width = arrived.shape
     rows = slots.shape[0]
+    vmem = pltpu.MemorySpace.VMEM
     return pl.pallas_call(
         _cross_kernel,
         out_shape=jax.ShapeDtypeStruct((rows, 2 * BINS), jnp.bfloat16),
-        grid=(rows // block,),
         in_specs=[
-            pl.BlockSpec((block, 1), lambda i: (i, 0)),
-            pl.BlockSpec(arrived.shape, lambda i: (0, 0, 0, 0), pipeline_mode=pl.Buffered(1)),
-            pl.BlockSpec((2 * SEG, block, BINS), lambda i: (0, i, 0)),
-            pl.BlockSpec((NFFT, 2 * BINS), lambda i: (0, 0), pipeline_mode=pl.Buffered(1)),
-            pl.BlockSpec((slabs // SEG, width), lambda i: (0, 0)),
+            pl.BlockSpec(memory_space=vmem),
+            pl.BlockSpec(memory_space=pl.ANY),
+            pl.BlockSpec(memory_space=vmem),
+            pl.BlockSpec(memory_space=pl.ANY),
+            pl.BlockSpec(memory_space=vmem),
         ],
-        out_specs=pl.BlockSpec((block, 2 * BINS), lambda i: (i, 0)),
+        out_specs=pl.BlockSpec(memory_space=vmem),
+        scratch_shapes=[
+            pltpu.VMEM(arrived.shape, arrived.dtype),
+            pltpu.VMEM(table.shape, table.dtype),
+            pltpu.SemaphoreType.DMA((2,)),
+        ],
         compiler_params=pltpu.CompilerParams(vmem_limit_bytes=48 * 1024 * 1024),
         cost_estimate=pl.CostEstimate(
             flops=2 * SEG * rows * NFFT * 2 * BINS, transcendentals=SEG * rows * BINS,

time: 182 us -> 182 us (level)
  no operation moved by 1% of the time
where the time goes in v14:
time: 182 us; the launch traced here: 181 us
  Pallas kernels  91.3 us (50%)
  blocking collectives  22.1 us (12%)
  waiting for transfers between devices  20.6 us (11%)
  starting transfers between devices  17.4 us (10%)
  other arithmetic  17.3 us (10%)
  local copies, waits for them, and re-layouts  11.7 us (6%)
    pallas_call x3, Pallas kernels, exchange(): pl.pallas_call(functools.partial(_exchange_kernel, axis), out_shape=jax.S...  60.8 us
    all_gather x1, blocking collectives, local(): firsts = lax.all_gather(first_station, 'slab', axis=0, tiled=False)  22.1 us
    all_to_all x1, waiting for transfers between devices, local(): lax.all_to_all(served, ('region', 'slab'), split_axis=0, concat_axis=0, t...  20.6 us
    all_to_all x1, starting transfers between devices, local(): lax.all_to_all(served, ('region', 'slab'), split_axis=0, concat_axis=0, t...  17.4 us
    pallas_call x2, Pallas kernels, pick_rows(): pl.pallas_call(_pick_kernel, out_shape=jax.ShapeDtypeStruct((count, width...  12.2 us
    pallas_call x1, Pallas kernels, cross_rows(): pl.pallas_call(_cross_kernel, out_shape=jax.ShapeDtypeStruct((rows, 2 * B...  10.1 us
    pallas_call x1, Pallas kernels, white_rows(): pl.pallas_call(_white_kernel, out_shape=jax.ShapeDtypeStruct((2 * SEG, ro...  8.34 us
    concatenate x1, other arithmetic, dft_table(): return jnp.concatenate([cos_part, -sin_part], axis=1).astype(jnp.bfloat16)  8.22 us
  transfers between devices with their start and end apart: 1, of which 1 were waited for; matrix products, arithmetic and copies ran while one was open for 9% of the time, Pallas kernels for 22%

profile of v14, /device:TPU:1, one launch (start us, length us, event | category | flops | bytes accessed | tf_op | source)
XLA Modules:
  0.0 180.7 jit_solution(12005377625630511511)
XLA Ops:
  0.0 0.7 broadcast_multiply_fusion
  0.7 0.7 fusion.17
  1.4 0.2 reduce_window_sum.11
  1.6 0.8 select_reduce_fusion
  2.4 0.1 copy.24
  2.5 0.1 copy.23
  2.6 0.1 fusion.14
  2.8 1.1 scatter_custom_fusion
  3.9 0.7 broadcast_in_dim.5.x_ref
  4.6 17.4 %shard_map.46 = s32[32,8,128]{2,1,0:T(8,128)} custom-call(s32[32,8,128]{2,1,0:T(8,128)} %broadcast_in_dim.5.x_ref), custom_call_target="tpu_custom_call" | custom-call | bytes 131072 | tf_op jit(solution)/shard_map/pallas_call | solution.py:280
  22.0 0.9 slice.6
  22.9 0.1 copy.25
  23.0 0.1 copy.26
  23.1 0.1 reshape.115
  23.3 0.0 copy-start.3
  23.3 0.6 pad.9.x_ref
  23.9 17.1 %shard_map.47 = s32[16,8,128]{2,1,0:T(8,128)} custom-call(s32[16,8,128]{2,1,0:T(8,128)} %pad.9.x_ref), custom_call_target="tpu_custom_call" | custom-call | bytes 65536 | tf_op jit(solution)/shard_map/pallas_call | solution.py:280
  41.1 0.8 slice.7
  41.9 2.6 %copy.27.ids_ref = s32[8192,1]{1,0:T(8,128)} copy(s32[8192,1]{0,1:T(1,128)S(1)} %bitcast.20) | data formatting | bytes 65536 | tf_op jit(solution)/shard_map/reshape;reshape | solution.py:89
  44.5 7.5 %shard_map.48 = bf16[8192,128]{1,0:T(8,128)(2,1)} custom-call(s32[8192,1]{1,0:T(8,128)} %copy.27.ids_ref, bf16[1024,128]{1,0:T(8,128)(2,1)} %table_ref.3), custom_call_target="tpu_custom_call" | custom-call | flops 2147483648 | bytes 2359296 | tf_op jit(solution)/shard_map/pallas_call | solution.py:77
  52.0 17.4 %all-to-all-start = ((bf16[512,16,128]{2,1,0:T(8,128)(2,1)}), bf16[512,16,128]{2,1,0:T(8,128)(2,1)S(1)}, u32[]{:S(2)}, u32[]{:S(2)}) async-start(bf16[512,16,128]{2,1,0:T(8,128)(2,1)} %bitcast.17), calls=%async_computation | async-start | bytes 4194304 | tf_op jit(solution)/shard_map/all_to_all | solution.py:330
  69.4 0.0 copy-done.3
  69.4 22.1 %all-gather.1 = s32[32,1,128]{2,1,0:T(1,128)S(1)} all-gather(s32[1,1,128]{2,1,0:T(1,128)S(1)} %bitcast.26), channel_id=2, replica_groups=mesh['region'=16,'slab'=32] {'slab'}, dimensions={0}, use_global_device_ids=true | all-gather | bytes 16896 | tf_op jit(solution)/shard_map/all_gather | solution.py:321
  91.4 2.0 %copy.28.ids_ref = s32[4096,1]{1,0:T(8,128)} copy(s32[4096,1]{0,1:T(1,128)S(1)} %bitcast.21) | data formatting | bytes 32768 | tf_op jit(solution)/shard_map/reshape;reshape | solution.py:89
  93.4 4.7 %shard_map.49 = bf16[4096,128]{1,0:T(8,128)(2,1)} custom-call(s32[4096,1]{1,0:T(8,128)} %copy.28.ids_ref, bf16[1024,128]{1,0:T(8,128)(2,1)} %table_ref.3), custom_call_target="tpu_custom_call" | custom-call | flops 1073741824 | bytes 1310720 | tf_op jit(solution)/shard_map/pallas_call | solution.py:77
  98.1 26.2 %shard_map.50.x_ref = bf16[32,128,128]{2,1,0:T(8,128)(2,1)} custom-call(bf16[32,128,128]{2,1,0:T(8,128)(2,1)} %bitcast.18), custom_call_target="tpu_custom_call" | custom-call | bytes 2097152 | tf_op jit(solution)/shard_map/pallas_call | solution.py:280
  124.4 0.1 multiply_subtract_fusion.taper_ref
  124.4 0.5 fusion.15
  125.0 1.0 fusion.9
  126.0 5.0 %subtract_convert_fusion = (bf16[32,64,1024]{2,1,0:T(8,128)(2,1)}, bf16[32,64,1024]{2,1,0:T(8,128)(2,1)}) fusion(f32[64,1024]{1,0:T(8,128)S(1)} %get-tuple-element.13, f32[32,1024]{1,0:T(8,128)S(1)} %get-tuple-element.15, f32[64,1024]{1,0:T(8,128)S(1)} %get-tuple-element.14, f32[32,1024]{1,0:T(8,128)S(1)} %get-tuple-element.16), kind=kLoop, calls=%fused_computation.3 | loop fusion | flops 18874368 | bytes 9175040 | tf_op jit(solution)/shard_map/convert.3
  131.0 0.0 copy-start
  131.0 8.2 %pad_maximum_fusion.table_ref.table_hbm = bf16[2048,2048]{1,0:T(8,128)(2,1)} fusion(bf16[2048,1024]{1,0:T(8,128)(2,1)} %bitcast.16, bf16[2048,1024]{1,0:T(8,128)(2,1)} %bitcast.15), kind=kLoop, calls=%fused_computation.1 | loop fusion | flops 16777216 | bytes 16777216 | tf_op jit(solution)/shard_map/concatenate | solution.py:29
  139.2 0.0 copy-done
  139.2 8.3 %shard_map.51.first_ref = bf16[4,128,1024]{2,1,0:T(8,128)(2,1)S(1)} custom-call(bf16[32,128,128]{2,1,0:T(8,128)(2,1)S(1)} %copy-done, bf16[2048,2048]{1,0:T(8,128)(2,1)} %pad_maximum_fusion.table_ref.table_hbm, f32[16,128]{1,0:T(8,128)S(1)} %multiply_subtract_fusion.taper_ref), custom_call_target="tpu_custom_call" | custom-call | flops 2147483648 | bytes 10485760 | tf_op jit(solution)/shard_map/pallas_call | solution.py:203
  147.6 0.0 copy-start.1
  147.6 1.1 copy-done.1
  148.6 20.6 %all-to-all-done = bf16[512,16,128]{2,1,0:T(8,128)(2,1)S(1)} async-done(((bf16[512,16,128]{2,1,0:T(8,128)(2,1)}), bf16[512,16,128]{2,1,0:T(8,128)(2,1)S(1)}, u32[]{:S(2)}, u32[]{:S(2)}) %all-to-all-start) | async-done | bytes 2097184 | tf_op jit(solution)/shard_map/all_to_all | solution.py:330
  169.2 0.0 copy-start.2
  169.2 1.2 copy-done.2
  170.4 10.1 %shard_map.52 = bf16[128,2048]{1,0:T(8,128)(2,1)} custom-call(s32[128,1]{1,0:T(8,128)S(1)} %get-tuple-element.10.ids_ref, bf16[16,32,16,128]{3,2,1,0:T(8,128)(2,1)S(1)} %bitcast.14, bf16[4,128,1024]{2,1,0:T(8,128)(2,1)S(1)} %copy-done.2, bf16[2048,2048]{1,0:T(8,128)(2,1)} %pad_maximum_fusion.table_ref.table_hbm, f32[16,128]{1,0:T(8,128)S(1)} %multiply_subtract_fusion.taper_ref), custom_call_target="tpu_custom_call" | custom-call | flops 2147483648 | bytes 10485760 | tf_op jit(solution)/shard_map/pallas_call | solution.py:221
  (1 shorter events, 0.0 us)
Async XLA Ops:
  23.3 46.1 %copy-start.3 = (s32[128]{0:T(128)S(1)}, s32[128]{0:T(128)}, u32[]{:S(2)}) copy-start(s32[128]{0:T(128)} %param.5) | copy-start | bytes 1540
  52.0 117.2 %all-to-all-start = ((bf16[512,16,128]{2,1,0:T(8,128)(2,1)}), bf16[512,16,128]{2,1,0:T(8,128)(2,1)S(1)}, u32[]{:S(2)}, u32[]{:S(2)}) async-start(bf16[512,16,128]{2,1,0:T(8,128)(2,1)} %bitcast.17), calls=%async_computation | async-start | bytes 4194304 | tf_op jit(solution)/shard_map/all_to_all | solution.py:330
  131.0 8.2 %copy-start = (bf16[32,128,128]{2,1,0:T(8,128)(2,1)S(1)}, bf16[32,128,128]{2,1,0:T(8,128)(2,1)}, u32[]{:S(2)}) copy-start(bf16[32,128,128]{2,1,0:T(8,128)(2,1)} %shard_map.50.x_ref) | copy-start | bytes 3145732
  147.6 1.1 copy-start.1
  169.2 1.2 copy-start.2

commit v15 on v14

--- a/solution.py
+++ b/solution.py
@@ -150,10 +150,12 @@
         out_ref[2 * segment + 1] = white_imag[segment * rows : (segment + 1) * rows]
 
 
-def _cross_kernel(ids_ref, arrived_hbm, first_ref, table_hbm, taper_ref, out_ref, arrived_ref, table_ref, sems):
+def _cross_kernel(ids_ref, arrived_hbm, first_hbm, table_hbm, taper_ref, out_ref, arrived_ref, first_ref, table_ref, sems):
     arrived_copy = pltpu.make_async_copy(arrived_hbm, arrived_ref, sems.at[0])
     table_copy = pltpu.make_async_copy(table_hbm, table_ref, sems.at[1])
+    first_copy = pltpu.make_async_copy(first_hbm, first_ref, sems.at[2])
     arrived_copy.start()
+    first_copy.start()
     table_copy.start()
     buckets, slabs, capacity, width = arrived_ref.shape
     ids = ids_ref[...]
@@ -168,6 +170,7 @@
     ]
     table_copy.wait()
     white_real, white_imag = _white_block(slices, table_ref[...], taper_ref[...])
+    first_copy.wait()
     real_sum = None
     imag_sum = None
     for segment in range(SEG):
@@ -224,15 +227,16 @@
         in_specs=[
             pl.BlockSpec(memory_space=vmem),
             pl.BlockSpec(memory_space=pl.ANY),
-            pl.BlockSpec(memory_space=vmem),
+            pl.BlockSpec(memory_space=pltpu.MemorySpace.HBM),
             pl.BlockSpec(memory_space=pl.ANY),
             pl.BlockSpec(memory_space=vmem),
         ],
         out_specs=pl.BlockSpec(memory_space=vmem),
         scratch_shapes=[
             pltpu.VMEM(arrived.shape, arrived.dtype),
+            pltpu.VMEM(first_white.shape, first_white.dtype),
             pltpu.VMEM(table.shape, table.dtype),
-            pltpu.SemaphoreType.DMA((2,)),
+            pltpu.SemaphoreType.DMA((3,)),
         ],
         compiler_params=pltpu.CompilerParams(vmem_limit_bytes=48 * 1024 * 1024),
         cost_estimate=pl.CostEstimate(
@@ -328,7 +332,8 @@
     served = pick_rows(records, asked)
     served = served.reshape(regions * slabs, capacity, width)
     arrived = lax.all_to_all(served, ("region", "slab"), split_axis=0, concat_axis=0, tiled=True)
-    arrived, first_white = lax.optimization_barrier((arrived, first_white))
+    arrived, _ = lax.optimization_barrier((arrived, first_white[0, :8, :128]))
+    first_white = pltpu.with_memory_space_constraint(first_white, pltpu.MemorySpace.HBM)
     return cross_rows(arrived.reshape(regions, slabs, capacity, width), slot_index, first_white, table, taper)
 
 def solution(mesh):

time: 182 us -> 181 us (level)
  no operation moved by 1% of the time
where the time goes in v15:
time: 181 us; the launch traced here: 180 us
  Pallas kernels  91.6 us (51%)
  blocking collectives  22.1 us (12%)
  waiting for transfers between devices  20.6 us (11%)
  starting transfers between devices  17.4 us (10%)
  other arithmetic  17.3 us (10%)
  local copies, waits for them, and re-layouts  10.4 us (6%)
    pallas_call x3, Pallas kernels, exchange(): pl.pallas_call(functools.partial(_exchange_kernel, axis), out_shape=jax.S...  60.8 us
    all_gather x1, blocking collectives, local(): firsts = lax.all_gather(first_station, 'slab', axis=0, tiled=False)  22.1 us
    all_to_all x1, waiting for transfers between devices, local(): lax.all_to_all(served, ('region', 'slab'), split_axis=0, concat_axis=0, t...  20.6 us
    all_to_all x1, starting transfers between devices, local(): lax.all_to_all(served, ('region', 'slab'), split_axis=0, concat_axis=0, t...  17.4 us
    pallas_call x2, Pallas kernels, pick_rows(): pl.pallas_call(_pick_kernel, out_shape=jax.ShapeDtypeStruct((count, width...  12.2 us
    pallas_call x1, Pallas kernels, cross_rows(): pl.pallas_call(_cross_kernel, out_shape=jax.ShapeDtypeStruct((rows, 2 * B...  10.4 us
    pallas_call x1, Pallas kernels, white_rows(): pl.pallas_call(_white_kernel, out_shape=jax.ShapeDtypeStruct((2 * SEG, ro...  8.34 us
    concatenate x1, other arithmetic, dft_table(): return jnp.concatenate([cos_part, -sin_part], axis=1).astype(jnp.bfloat16)  8.22 us
  transfers between devices with their start and end apart: 1, of which 1 were waited for; matrix products, arithmetic and copies ran while one was open for 9% of the time, Pallas kernels for 22%

profile of v15, /device:TPU:1, one launch (start us, length us, event | category | flops | bytes accessed | tf_op | source)
XLA Modules:
  0.0 179.7 jit_solution(5301930200951379266)
XLA Ops:
  0.0 0.7 broadcast_multiply_fusion
  0.7 0.7 fusion.17
  1.4 0.2 reduce_window_sum.11
  1.6 0.8 select_reduce_fusion
  2.4 0.1 copy.24
  2.5 0.1 copy.23
  2.6 0.1 fusion.14
  2.8 1.1 scatter_custom_fusion
  3.9 0.7 broadcast_in_dim.5.x_ref
  4.6 17.4 %shard_map.46 = s32[32,8,128]{2,1,0:T(8,128)} custom-call(s32[32,8,128]{2,1,0:T(8,128)} %broadcast_in_dim.5.x_ref), custom_call_target="tpu_custom_call" | custom-call | bytes 131072 | tf_op jit(solution)/shard_map/pallas_call | solution.py:284
  22.0 0.9 slice.7
  22.9 0.1 copy.25
  23.0 0.1 copy.26
  23.1 0.1 reshape.115
  23.3 0.0 copy-start.2
  23.3 0.6 pad.9.x_ref
  23.9 17.1 %shard_map.47 = s32[16,8,128]{2,1,0:T(8,128)} custom-call(s32[16,8,128]{2,1,0:T(8,128)} %pad.9.x_ref), custom_call_target="tpu_custom_call" | custom-call | bytes 65536 | tf_op jit(solution)/shard_map/pallas_call | solution.py:284
  41.1 0.8 slice.8
  41.9 2.6 %copy.27.ids_ref = s32[8192,1]{1,0:T(8,128)} copy(s32[8192,1]{0,1:T(1,128)S(1)} %bitcast.20) | data formatting | bytes 65536 | tf_op jit(solution)/shard_map/reshape;reshape | solution.py:89
  44.5 7.5 %shard_map.48 = bf16[8192,128]{1,0:T(8,128)(2,1)} custom-call(s32[8192,1]{1,0:T(8,128)} %copy.27.ids_ref, bf16[1024,128]{1,0:T(8,128)(2,1)} %table_ref.3), custom_call_target="tpu_custom_call" | custom-call | flops 2147483648 | bytes 2359296 | tf_op jit(solution)/shard_map/pallas_call | solution.py:77
  52.0 17.4 %all-to-all-start = ((bf16[512,16,128]{2,1,0:T(8,128)(2,1)}), bf16[512,16,128]{2,1,0:T(8,128)(2,1)S(1)}, u32[]{:S(2)}, u32[]{:S(2)}) async-start(bf16[512,16,128]{2,1,0:T(8,128)(2,1)} %bitcast.17), calls=%async_computation | async-start | bytes 4194304 | tf_op jit(solution)/shard_map/all_to_all | solution.py:334
  69.4 0.0 copy-done.2
  69.4 22.1 %all-gather.1 = s32[32,1,128]{2,1,0:T(1,128)S(1)} all-gather(s32[1,1,128]{2,1,0:T(1,128)S(1)} %bitcast.26), channel_id=2, replica_groups=mesh['region'=16,'slab'=32] {'slab'}, dimensions={0}, use_global_device_ids=true | all-gather | bytes 16896 | tf_op jit(solution)/shard_map/all_gather | solution.py:325
  91.4 2.0 %copy.28.ids_ref = s32[4096,1]{1,0:T(8,128)} copy(s32[4096,1]{0,1:T(1,128)S(1)} %bitcast.21) | data formatting | bytes 32768 | tf_op jit(solution)/shard_map/reshape;reshape | solution.py:89
  93.4 4.7 %shard_map.49 = bf16[4096,128]{1,0:T(8,128)(2,1)} custom-call(s32[4096,1]{1,0:T(8,128)} %copy.28.ids_ref, bf16[1024,128]{1,0:T(8,128)(2,1)} %table_ref.3), custom_call_target="tpu_custom_call" | custom-call | flops 1073741824 | bytes 1310720 | tf_op jit(solution)/shard_map/pallas_call | solution.py:77
  98.1 26.2 %shard_map.50.x_ref = bf16[32,128,128]{2,1,0:T(8,128)(2,1)} custom-call(bf16[32,128,128]{2,1,0:T(8,128)(2,1)} %bitcast.18), custom_call_target="tpu_custom_call" | custom-call | bytes 2097152 | tf_op jit(solution)/shard_map/pallas_call | solution.py:284
  124.4 0.1 multiply_subtract_fusion.taper_ref
  124.4 0.5 fusion.15
  125.0 1.0 fusion.9
  126.0 5.0 %subtract_convert_fusion = (bf16[32,64,1024]{2,1,0:T(8,128)(2,1)}, bf16[32,64,1024]{2,1,0:T(8,128)(2,1)}) fusion(f32[64,1024]{1,0:T(8,128)S(1)} %get-tuple-element.9, f32[32,1024]{1,0:T(8,128)S(1)} %get-tuple-element.11, f32[64,1024]{1,0:T(8,128)S(1)} %get-tuple-element.10, f32[32,1024]{1,0:T(8,128)S(1)} %get-tuple-element.12), kind=kLoop, calls=%fused_computation.3 | loop fusion | flops 18874368 | bytes 9175040 | tf_op jit(solution)/shard_map/convert.3
  131.0 0.0 copy-start
  131.0 8.2 %pad_maximum_fusion.table_ref.table_hbm = bf16[2048,2048]{1,0:T(8,128)(2,1)} fusion(bf16[2048,1024]{1,0:T(8,128)(2,1)} %bitcast.16, bf16[2048,1024]{1,0:T(8,128)(2,1)} %bitcast.15), kind=kLoop, calls=%fused_computation.1 | loop fusion | flops 16777216 | bytes 16777216 | tf_op jit(solution)/shard_map/concatenate | solution.py:29
  139.2 0.0 copy-done
  139.2 8.3 %shard_map.51.first_hbm = bf16[4,128,1024]{2,1,0:T(8,128)(2,1)S(1)} custom-call(bf16[32,128,128]{2,1,0:T(8,128)(2,1)S(1)} %copy-done, bf16[2048,2048]{1,0:T(8,128)(2,1)} %pad_maximum_fusion.table_ref.table_hbm, f32[16,128]{1,0:T(8,128)S(1)} %multiply_subtract_fusion.taper_ref), custom_call_target="tpu_custom_call" | custom-call | flops 2147483648 | bytes 10485760 | tf_op jit(solution)/shard_map/pallas_call | solution.py:206
  147.6 0.0 copy-start.1
  147.6 1.1 copy-done.1
  148.6 20.6 %all-to-all-done = bf16[512,16,128]{2,1,0:T(8,128)(2,1)S(1)} async-done(((bf16[512,16,128]{2,1,0:T(8,128)(2,1)}), bf16[512,16,128]{2,1,0:T(8,128)(2,1)S(1)}, u32[]{:S(2)}, u32[]{:S(2)}) %all-to-all-start) | async-done | bytes 2097184 | tf_op jit(solution)/shard_map/all_to_all | solution.py:334
  169.2 10.4 %shard_map.52 = bf16[128,2048]{1,0:T(8,128)(2,1)} custom-call(s32[128,1]{1,0:T(8,128)S(1)} %get-tuple-element.6.ids_ref, bf16[16,32,16,128]{3,2,1,0:T(8,128)(2,1)S(1)} %bitcast.14, bf16[4,128,1024]{2,1,0:T(8,128)(2,1)} %copy-done.1, bf16[2048,2048]{1,0:T(8,128)(2,1)} %pad_maximum_fusion.table_ref.table_hbm, f32[16,128]{1,0:T(8,128)S(1)} %multiply_subtract_fusion.taper_ref), custom_call_target="tpu_custom_call" | custom-call | flops 2147483648 | bytes 10485760 | tf_op jit(solution)/shard_map/pallas_call | solution.py:224
  (1 shorter events, 0.0 us)
Async XLA Ops:
  23.3 46.1 %copy-start.2 = (s32[128]{0:T(128)S(1)}, s32[128]{0:T(128)}, u32[]{:S(2)}) copy-start(s32[128]{0:T(128)} %param.5) | copy-start | bytes 1540
  52.0 117.2 %all-to-all-start = ((bf16[512,16,128]{2,1,0:T(8,128)(2,1)}), bf16[512,16,128]{2,1,0:T(8,128)(2,1)S(1)}, u32[]{:S(2)}, u32[]{:S(2)}) async-start(bf16[512,16,128]{2,1,0:T(8,128)(2,1)} %bitcast.17), calls=%async_computation | async-start | bytes 4194304 | tf_op jit(solution)/shard_map/all_to_all | solution.py:334
  131.0 8.2 %copy-start = (bf16[32,128,128]{2,1,0:T(8,128)(2,1)S(1)}, bf16[32,128,128]{2,1,0:T(8,128)(2,1)}, u32[]{:S(2)}) copy-start(bf16[32,128,128]{2,1,0:T(8,128)(2,1)} %shard_map.50.x_ref) | copy-start | bytes 3145732
  147.6 1.1 copy-start.1

commit v16 on v15

--- a/solution.py
+++ b/solution.py
@@ -64,7 +64,7 @@
 
 
 def _pick_kernel(ids_ref, table_ref, out_ref):
-    ids = ids_ref[...]
+    ids = jnp.transpose(ids_ref[...])[:, :1]
     rows = table_ref.shape[0]
     onehot = (lax.broadcasted_iota(jnp.int32, (ids.shape[0], rows), 1) == ids).astype(table_ref.dtype)
     out_ref[...] = jnp.dot(onehot, table_ref[...], preferred_element_type=jnp.float32).astype(out_ref.dtype)
@@ -79,14 +79,14 @@
         out_shape=jax.ShapeDtypeStruct((count, width), table.dtype),
         grid=(count // block,),
         in_specs=[
-            pl.BlockSpec((block, 1), lambda i: (i, 0)),
+            pl.BlockSpec((8, block), lambda i: (0, i)),
             pl.BlockSpec((rows, width), lambda i: (0, 0)),
         ],
         out_specs=pl.BlockSpec((block, width), lambda i: (i, 0)),
         cost_estimate=pl.CostEstimate(
             flops=2 * count * rows * width, transcendentals=0, bytes_accessed=2 * (rows + count) * width
         ),
-    )(ids.reshape(count, 1), table)
+    )(jnp.broadcast_to(ids[None, :], (8, count)), table)
 
 
 def _compact_kernel(ids_ref, table_ref, out_ref):

time: 181 us -> 181 us (level)
  local copies, waits for them, and re-layouts: 10.4 us -> 7.23 us
  Pallas kernels: 91.6 us -> 94.7 us
    another operation x2 -> x0, local copies, waits for them, and re-layouts: 4.6 us -> none  [pick_rows(): ids.reshape(count, 1)]
    pallas_call x2, Pallas kernels: 12.2 us -> 15.4 us  [pick_rows(): pl.pallas_call(_pick_kernel, out_shape=jax.ShapeDtypeStruct((count, width...]
where the time goes in v16:
time: 181 us; the launch traced here: 180 us
  Pallas kernels  94.7 us (52%)
  blocking collectives  22.1 us (12%)
  waiting for transfers between devices  21 us (12%)
  starting transfers between devices  17.4 us (10%)
  other arithmetic  17.3 us (10%)
  local copies, waits for them, and re-layouts  7.23 us (4%)
    pallas_call x3, Pallas kernels, exchange(): pl.pallas_call(functools.partial(_exchange_kernel, axis), out_shape=jax.S...  60.6 us
    all_gather x1, blocking collectives, local(): firsts = lax.all_gather(first_station, 'slab', axis=0, tiled=False)  22.1 us
    all_to_all x1, waiting for transfers between devices, local(): lax.all_to_all(served, ('region', 'slab'), split_axis=0, concat_axis=0, t...  21 us
    all_to_all x1, starting transfers between devices, local(): lax.all_to_all(served, ('region', 'slab'), split_axis=0, concat_axis=0, t...  17.4 us
    pallas_call x2, Pallas kernels, pick_rows(): pl.pallas_call(_pick_kernel, out_shape=jax.ShapeDtypeStruct((count, width...  15.4 us
    pallas_call x1, Pallas kernels, cross_rows(): pl.pallas_call(_cross_kernel, out_shape=jax.ShapeDtypeStruct((rows, 2 * B...  10.4 us
    pallas_call x1, Pallas kernels, white_rows(): pl.pallas_call(_white_kernel, out_shape=jax.ShapeDtypeStruct((2 * SEG, ro...  8.34 us
    concatenate x1, other arithmetic, dft_table(): return jnp.concatenate([cos_part, -sin_part], axis=1).astype(jnp.bfloat16)  8.22 us
  transfers between devices with their start and end apart: 1, of which 1 were waited for; matrix products, arithmetic and copies ran while one was open for 9% of the time, Pallas kernels for 22%

profile of v16, /device:TPU:1, one launch (start us, length us, event | category | flops | bytes accessed | tf_op | source)
XLA Modules:
  0.0 180.1 jit_solution(13654086211441802735)
XLA Ops:
  0.0 0.0 copy-start.2
  0.0 0.7 broadcast_multiply_fusion
  0.7 0.7 fusion.17
  1.4 0.2 reduce_window_sum.11
  1.6 0.8 select_reduce_fusion
  2.4 0.1 copy.20
  2.5 0.1 copy.19
  2.7 0.1 fusion.14
  2.8 1.1 scatter_custom_fusion
  3.9 0.7 broadcast_in_dim.13.x_ref
  4.6 17.4 %shard_map.46 = s32[32,8,128]{2,1,0:T(8,128)} custom-call(s32[32,8,128]{2,1,0:T(8,128)} %broadcast_in_dim.13.x_ref), custom_call_target="tpu_custom_call" | custom-call | bytes 131072 | tf_op jit(solution)/shard_map/pallas_call | solution.py:284
  22.0 0.9 slice.7
  22.9 0.1 copy.21
  23.0 0.1 copy.22
  23.1 0.1 reshape.117
  23.3 0.6 pad.9.x_ref
  23.9 17.1 %shard_map.47 = s32[16,8,128]{2,1,0:T(8,128)} custom-call(s32[16,8,128]{2,1,0:T(8,128)} %pad.9.x_ref), custom_call_target="tpu_custom_call" | custom-call | bytes 65536 | tf_op jit(solution)/shard_map/pallas_call | solution.py:284
  41.1 0.8 slice.8
  41.9 0.7 broadcast_in_dim.15.ids_ref
  42.6 9.6 %shard_map.48 = bf16[8192,128]{1,0:T(8,128)(2,1)} custom-call(s32[8,8192]{1,0:T(8,128)} %broadcast_in_dim.15.ids_ref, bf16[1024,128]{1,0:T(8,128)(2,1)} %table_ref.3), custom_call_target="tpu_custom_call" | custom-call | flops 2147483648 | bytes 2359296 | tf_op jit(solution)/shard_map/pallas_call | solution.py:77
  52.3 17.4 %all-to-all-start = ((bf16[512,16,128]{2,1,0:T(8,128)(2,1)}), bf16[512,16,128]{2,1,0:T(8,128)(2,1)S(1)}, u32[]{:S(2)}, u32[]{:S(2)}) async-start(bf16[512,16,128]{2,1,0:T(8,128)(2,1)} %bitcast.17), calls=%async_computation | async-start | bytes 4194304 | tf_op jit(solution)/shard_map/all_to_all | solution.py:334
  69.7 0.0 copy-done.2
  69.7 22.1 %all-gather.1 = s32[32,1,128]{2,1,0:T(1,128)S(1)} all-gather(s32[1,1,128]{2,1,0:T(1,128)S(1)} %bitcast.26), channel_id=2, replica_groups=mesh['region'=16,'slab'=32] {'slab'}, dimensions={0}, use_global_device_ids=true | all-gather | bytes 16896 | tf_op jit(solution)/shard_map/all_gather | solution.py:325
  91.8 0.7 broadcast_in_dim.17.ids_ref
  92.4 5.7 %shard_map.49 = bf16[4096,128]{1,0:T(8,128)(2,1)} custom-call(s32[8,4096]{1,0:T(8,128)} %broadcast_in_dim.17.ids_ref, bf16[1024,128]{1,0:T(8,128)(2,1)} %table_ref.3), custom_call_target="tpu_custom_call" | custom-call | flops 1073741824 | bytes 1310720 | tf_op jit(solution)/shard_map/pallas_call | solution.py:77
  98.1 26.1 %shard_map.50.x_ref = bf16[32,128,128]{2,1,0:T(8,128)(2,1)} custom-call(bf16[32,128,128]{2,1,0:T(8,128)(2,1)} %bitcast.18), custom_call_target="tpu_custom_call" | custom-call | bytes 2097152 | tf_op jit(solution)/shard_map/pallas_call | solution.py:284
  124.2 0.1 multiply_subtract_fusion.taper_ref
  124.3 0.5 fusion.15
  124.8 1.0 fusion.9
  125.9 5.0 %subtract_convert_fusion = (bf16[32,64,1024]{2,1,0:T(8,128)(2,1)}, bf16[32,64,1024]{2,1,0:T(8,128)(2,1)}) fusion(f32[64,1024]{1,0:T(8,128)S(1)} %get-tuple-element.9, f32[32,1024]{1,0:T(8,128)S(1)} %get-tuple-element.11, f32[64,1024]{1,0:T(8,128)S(1)} %get-tuple-element.10, f32[32,1024]{1,0:T(8,128)S(1)} %get-tuple-element.12), kind=kLoop, calls=%fused_computation.3 | loop fusion | flops 18874368 | bytes 9175040 | tf_op jit(solution)/shard_map/convert.3
  130.9 0.0 copy-start
  130.9 8.2 %pad_maximum_fusion.table_ref.table_hbm = bf16[2048,2048]{1,0:T(8,128)(2,1)} fusion(bf16[2048,1024]{1,0:T(8,128)(2,1)} %bitcast.16, bf16[2048,1024]{1,0:T(8,128)(2,1)} %bitcast.15), kind=kLoop, calls=%fused_computation.1 | loop fusion | flops 16777216 | bytes 16777216 | tf_op jit(solution)/shard_map/concatenate | solution.py:29
  139.1 0.0 copy-done
  139.1 8.3 %shard_map.51.first_hbm = bf16[4,128,1024]{2,1,0:T(8,128)(2,1)S(1)} custom-call(bf16[32,128,128]{2,1,0:T(8,128)(2,1)S(1)} %copy-done, bf16[2048,2048]{1,0:T(8,128)(2,1)} %pad_maximum_fusion.table_ref.table_hbm, f32[16,128]{1,0:T(8,128)S(1)} %multiply_subtract_fusion.taper_ref), custom_call_target="tpu_custom_call" | custom-call | flops 2147483648 | bytes 10485760 | tf_op jit(solution)/shard_map/pallas_call | solution.py:206
  147.4 0.0 copy-start.1
  147.4 1.1 copy-done.1
  148.5 21.0 %all-to-all-done = bf16[512,16,128]{2,1,0:T(8,128)(2,1)S(1)} async-done(((bf16[512,16,128]{2,1,0:T(8,128)(2,1)}), bf16[512,16,128]{2,1,0:T(8,128)(2,1)S(1)}, u32[]{:S(2)}, u32[]{:S(2)}) %all-to-all-start) | async-done | bytes 2097184 | tf_op jit(solution)/shard_map/all_to_all | solution.py:334
  169.5 10.4 %shard_map.52 = bf16[128,2048]{1,0:T(8,128)(2,1)} custom-call(s32[128,1]{1,0:T(8,128)S(1)} %get-tuple-element.6.ids_ref, bf16[16,32,16,128]{3,2,1,0:T(8,128)(2,1)S(1)} %bitcast.14, bf16[4,128,1024]{2,1,0:T(8,128)(2,1)} %copy-done.1, bf16[2048,2048]{1,0:T(8,128)(2,1)} %pad_maximum_fusion.table_ref.table_hbm, f32[16,128]{1,0:T(8,128)S(1)} %multiply_subtract_fusion.taper_ref), custom_call_target="tpu_custom_call" | custom-call | flops 2147483648 | bytes 10485760 | tf_op jit(solution)/shard_map/pallas_call | solution.py:224
  (1 shorter events, 0.0 us)
Async XLA Ops:
  0.0 69.7 %copy-start.2 = (s32[128]{0:T(128)S(1)}, s32[128]{0:T(128)}, u32[]{:S(2)}) copy-start(s32[128]{0:T(128)} %param.5) | copy-start | bytes 1540
  52.3 117.2 %all-to-all-start = ((bf16[512,16,128]{2,1,0:T(8,128)(2,1)}), bf16[512,16,128]{2,1,0:T(8,128)(2,1)S(1)}, u32[]{:S(2)}, u32[]{:S(2)}) async-start(bf16[512,16,128]{2,1,0:T(8,128)(2,1)} %bitcast.17), calls=%async_computation | async-start | bytes 4194304 | tf_op jit(solution)/shard_map/all_to_all | solution.py:334
  130.9 8.2 %copy-start = (bf16[32,128,128]{2,1,0:T(8,128)(2,1)S(1)}, bf16[32,128,128]{2,1,0:T(8,128)(2,1)}, u32[]{:S(2)}) copy-start(bf16[32,128,128]{2,1,0:T(8,128)(2,1)} %shard_map.50.x_ref) | copy-start | bytes 3145732
  147.4 1.1 copy-start.1

commit v17 on v15

--- a/solution.py
+++ b/solution.py
@@ -136,8 +136,9 @@
     smooth = smooth / (2 * HALF + 1)
     level = jnp.sum(amplitude, axis=1, keepdims=True) / BINS
     divisor = smooth + level + 1e-06
-    white_real = (real_part / divisor).astype(jnp.bfloat16)
-    white_imag = (imag_part / divisor).astype(jnp.bfloat16)
+    inverse = 1.0 / divisor
+    white_real = (real_part * inverse).astype(jnp.bfloat16)
+    white_imag = (imag_part * inverse).astype(jnp.bfloat16)
     return white_real, white_imag
 
 

time: 181 us -> 181 us (level)
  no operation moved by 1% of the time
where the time goes in v17:
time: 181 us; the launch traced here: 180 us
  Pallas kernels  91.6 us (51%)
  blocking collectives  22.1 us (12%)
  waiting for transfers between devices  20.6 us (11%)
  starting transfers between devices  17.4 us (10%)
  other arithmetic  17.3 us (10%)
  local copies, waits for them, and re-layouts  10.4 us (6%)
    pallas_call x3, Pallas kernels, exchange(): pl.pallas_call(functools.partial(_exchange_kernel, axis), out_shape=jax.S...  60.8 us
    all_gather x1, blocking collectives, local(): firsts = lax.all_gather(first_station, 'slab', axis=0, tiled=False)  22.1 us
    all_to_all x1, waiting for transfers between devices, local(): lax.all_to_all(served, ('region', 'slab'), split_axis=0, concat_axis=0, t...  20.6 us
    all_to_all x1, starting transfers between devices, local(): lax.all_to_all(served, ('region', 'slab'), split_axis=0, concat_axis=0, t...  17.4 us
    pallas_call x2, Pallas kernels, pick_rows(): pl.pallas_call(_pick_kernel, out_shape=jax.ShapeDtypeStruct((count, width...  12.2 us
    pallas_call x1, Pallas kernels, cross_rows(): pl.pallas_call(_cross_kernel, out_shape=jax.ShapeDtypeStruct((rows, 2 * B...  10.4 us
    pallas_call x1, Pallas kernels, white_rows(): pl.pallas_call(_white_kernel, out_shape=jax.ShapeDtypeStruct((2 * SEG, ro...  8.34 us
    concatenate x1, other arithmetic, dft_table(): return jnp.concatenate([cos_part, -sin_part], axis=1).astype(jnp.bfloat16)  8.22 us
  transfers between devices with their start and end apart: 1, of which 1 were waited for; matrix products, arithmetic and copies ran while one was open for 9% of the time, Pallas kernels for 22%

profile of v17, /device:TPU:1, one launch (start us, length us, event | category | flops | bytes accessed | tf_op | source)
XLA Modules:
  0.0 179.7 jit_solution(9817004582867929689)
XLA Ops:
  0.0 0.7 broadcast_multiply_fusion
  0.7 0.7 fusion.17
  1.4 0.2 reduce_window_sum.11
  1.6 0.8 select_reduce_fusion
  2.4 0.1 copy.24
  2.5 0.1 copy.23
  2.6 0.1 fusion.14
  2.8 1.1 scatter_custom_fusion
  3.9 0.7 broadcast_in_dim.5.x_ref
  4.6 17.4 %shard_map.46 = s32[32,8,128]{2,1,0:T(8,128)} custom-call(s32[32,8,128]{2,1,0:T(8,128)} %broadcast_in_dim.5.x_ref), custom_call_target="tpu_custom_call" | custom-call | bytes 131072 | tf_op jit(solution)/shard_map/pallas_call | solution.py:285
  22.0 0.9 slice.7
  22.9 0.1 copy.25
  23.0 0.1 copy.26
  23.1 0.1 reshape.115
  23.3 0.0 copy-start.2
  23.3 0.6 pad.9.x_ref
  23.9 17.1 %shard_map.47 = s32[16,8,128]{2,1,0:T(8,128)} custom-call(s32[16,8,128]{2,1,0:T(8,128)} %pad.9.x_ref), custom_call_target="tpu_custom_call" | custom-call | bytes 65536 | tf_op jit(solution)/shard_map/pallas_call | solution.py:285
  41.1 0.8 slice.8
  41.9 2.6 %copy.27.ids_ref = s32[8192,1]{1,0:T(8,128)} copy(s32[8192,1]{0,1:T(1,128)S(1)} %bitcast.20) | data formatting | bytes 65536 | tf_op jit(solution)/shard_map/reshape;reshape | solution.py:89
  44.5 7.5 %shard_map.48 = bf16[8192,128]{1,0:T(8,128)(2,1)} custom-call(s32[8192,1]{1,0:T(8,128)} %copy.27.ids_ref, bf16[1024,128]{1,0:T(8,128)(2,1)} %table_ref.3), custom_call_target="tpu_custom_call" | custom-call | flops 2147483648 | bytes 2359296 | tf_op jit(solution)/shard_map/pallas_call | solution.py:77
  52.0 17.4 %all-to-all-start = ((bf16[512,16,128]{2,1,0:T(8,128)(2,1)}), bf16[512,16,128]{2,1,0:T(8,128)(2,1)S(1)}, u32[]{:S(2)}, u32[]{:S(2)}) async-start(bf16[512,16,128]{2,1,0:T(8,128)(2,1)} %bitcast.17), calls=%async_computation | async-start | bytes 4194304 | tf_op jit(solution)/shard_map/all_to_all | solution.py:335
  69.4 0.0 copy-done.2
  69.4 22.1 %all-gather.1 = s32[32,1,128]{2,1,0:T(1,128)S(1)} all-gather(s32[1,1,128]{2,1,0:T(1,128)S(1)} %bitcast.26), channel_id=2, replica_groups=mesh['region'=16,'slab'=32] {'slab'}, dimensions={0}, use_global_device_ids=true | all-gather | bytes 16896 | tf_op jit(solution)/shard_map/all_gather | solution.py:326
  91.4 2.0 %copy.28.ids_ref = s32[4096,1]{1,0:T(8,128)} copy(s32[4096,1]{0,1:T(1,128)S(1)} %bitcast.21) | data formatting | bytes 32768 | tf_op jit(solution)/shard_map/reshape;reshape | solution.py:89
  93.4 4.7 %shard_map.49 = bf16[4096,128]{1,0:T(8,128)(2,1)} custom-call(s32[4096,1]{1,0:T(8,128)} %copy.28.ids_ref, bf16[1024,128]{1,0:T(8,128)(2,1)} %table_ref.3), custom_call_target="tpu_custom_call" | custom-call | flops 1073741824 | bytes 1310720 | tf_op jit(solution)/shard_map/pallas_call | solution.py:77
  98.1 26.2 %shard_map.50.x_ref = bf16[32,128,128]{2,1,0:T(8,128)(2,1)} custom-call(bf16[32,128,128]{2,1,0:T(8,128)(2,1)} %bitcast.18), custom_call_target="tpu_custom_call" | custom-call | bytes 2097152 | tf_op jit(solution)/shard_map/pallas_call | solution.py:285
  124.4 0.1 multiply_subtract_fusion.taper_ref
  124.4 0.5 fusion.15
  125.0 1.0 fusion.9
  126.0 5.0 %subtract_convert_fusion = (bf16[32,64,1024]{2,1,0:T(8,128)(2,1)}, bf16[32,64,1024]{2,1,0:T(8,128)(2,1)}) fusion(f32[64,1024]{1,0:T(8,128)S(1)} %get-tuple-element.9, f32[32,1024]{1,0:T(8,128)S(1)} %get-tuple-element.11, f32[64,1024]{1,0:T(8,128)S(1)} %get-tuple-element.10, f32[32,1024]{1,0:T(8,128)S(1)} %get-tuple-element.12), kind=kLoop, calls=%fused_computation.3 | loop fusion | flops 18874368 | bytes 9175040 | tf_op jit(solution)/shard_map/convert.3
  131.0 0.0 copy-start
  131.0 8.2 %pad_maximum_fusion.table_ref.table_hbm = bf16[2048,2048]{1,0:T(8,128)(2,1)} fusion(bf16[2048,1024]{1,0:T(8,128)(2,1)} %bitcast.16, bf16[2048,1024]{1,0:T(8,128)(2,1)} %bitcast.15), kind=kLoop, calls=%fused_computation.1 | loop fusion | flops 16777216 | bytes 16777216 | tf_op jit(solution)/shard_map/concatenate | solution.py:29
  139.2 0.0 copy-done
  139.2 8.3 %shard_map.51.first_hbm = bf16[4,128,1024]{2,1,0:T(8,128)(2,1)S(1)} custom-call(bf16[32,128,128]{2,1,0:T(8,128)(2,1)S(1)} %copy-done, bf16[2048,2048]{1,0:T(8,128)(2,1)} %pad_maximum_fusion.table_ref.table_hbm, f32[16,128]{1,0:T(8,128)S(1)} %multiply_subtract_fusion.taper_ref), custom_call_target="tpu_custom_call" | custom-call | flops 2147483648 | bytes 10485760 | tf_op jit(solution)/shard_map/pallas_call | solution.py:207
  147.6 0.0 copy-start.1
  147.6 1.1 copy-done.1
  148.6 20.6 %all-to-all-done = bf16[512,16,128]{2,1,0:T(8,128)(2,1)S(1)} async-done(((bf16[512,16,128]{2,1,0:T(8,128)(2,1)}), bf16[512,16,128]{2,1,0:T(8,128)(2,1)S(1)}, u32[]{:S(2)}, u32[]{:S(2)}) %all-to-all-start) | async-done | bytes 2097184 | tf_op jit(solution)/shard_map/all_to_all | solution.py:335
  169.2 10.4 %shard_map.52 = bf16[128,2048]{1,0:T(8,128)(2,1)} custom-call(s32[128,1]{1,0:T(8,128)S(1)} %get-tuple-element.6.ids_ref, bf16[16,32,16,128]{3,2,1,0:T(8,128)(2,1)S(1)} %bitcast.14, bf16[4,128,1024]{2,1,0:T(8,128)(2,1)} %copy-done.1, bf16[2048,2048]{1,0:T(8,128)(2,1)} %pad_maximum_fusion.table_ref.table_hbm, f32[16,128]{1,0:T(8,128)S(1)} %multiply_subtract_fusion.taper_ref), custom_call_target="tpu_custom_call" | custom-call | flops 2147483648 | bytes 10485760 | tf_op jit(solution)/shard_map/pallas_call | solution.py:225
  (1 shorter events, 0.0 us)
Async XLA Ops:
  23.3 46.1 %copy-start.2 = (s32[128]{0:T(128)S(1)}, s32[128]{0:T(128)}, u32[]{:S(2)}) copy-start(s32[128]{0:T(128)} %param.5) | copy-start | bytes 1540
  52.0 117.2 %all-to-all-start = ((bf16[512,16,128]{2,1,0:T(8,128)(2,1)}), bf16[512,16,128]{2,1,0:T(8,128)(2,1)S(1)}, u32[]{:S(2)}, u32[]{:S(2)}) async-start(bf16[512,16,128]{2,1,0:T(8,128)(2,1)} %bitcast.17), calls=%async_computation | async-start | bytes 4194304 | tf_op jit(solution)/shard_map/all_to_all | solution.py:335
  131.0 8.2 %copy-start = (bf16[32,128,128]{2,1,0:T(8,128)(2,1)S(1)}, bf16[32,128,128]{2,1,0:T(8,128)(2,1)}, u32[]{:S(2)}) copy-start(bf16[32,128,128]{2,1,0:T(8,128)(2,1)} %shard_map.50.x_ref) | copy-start | bytes 3145732
  147.6 1.1 copy-start.1

commit v18 on v15

--- a/solution.py
+++ b/solution.py
@@ -322,7 +322,9 @@
     outgoing = jnp.pad(outgoing, ((0, 0), (0, (-outgoing.shape[1]) % 8), (0, 0)))
     asked = exchange(outgoing, "region", 1)[:, : slabs * capacity // 128].reshape(-1)
 
-    firsts = lax.all_gather(first_station, "slab", axis=0, tiled=False)
+    own_firsts = jnp.pad(first_station.reshape(-1, 128), ((0, (-(pair_count // 128)) % 8), (0, 0)))
+    firsts = exchange(jnp.broadcast_to(own_firsts[None], (slabs,) + own_firsts.shape), "slab", 3)
+    firsts = firsts[:, : pair_count // 128].reshape(slabs, pair_count)
     first_parts = pick_rows(records, firsts.reshape(-1)).reshape(slabs, pair_count, width)
     first_arrived = exchange(first_parts, "slab", 0)
     table = dft_table()

time: 181 us -> 181 us (level)
  blocking collectives: 22.1 us -> 0 us
  Pallas kernels: 91.6 us -> 106 us
  waiting for transfers between devices: 20.6 us -> 27.1 us
    all_gather x1 -> x0, blocking collectives: 22.1 us -> none  [local(): firsts = lax.all_gather(first_station, 'slab', axis=0, tiled=False)]
    pallas_call x3 -> x4, Pallas kernels: 60.8 us -> 74.7 us  [exchange(): pl.pallas_call(functools.partial(_exchange_kernel, axis), out_shape=jax.S...]
    all_to_all x1, waiting for transfers between devices: 20.6 us -> 27.1 us  [local(): lax.all_to_all(served, ('region', 'slab'), split_axis=0, concat_axis=0, t...]
    another operation x2 -> x3, local copies, waits for them, and re-layouts: 4.6 us -> 5.51 us  [pick_rows(): ids.reshape(count, 1)]
  transfers between devices with their start and end apart: 1 -> 1, of which waited for: 1 -> 1; matrix products, arithmetic and copies ran while one was open for 9% -> 10% of each run, Pallas kernels for 22% -> 30%
where the time goes in v18:
time: 181 us; the launch traced here: 180 us
  Pallas kernels  106 us (59%)
  waiting for transfers between devices  27.1 us (15%)
  starting transfers between devices  17.4 us (10%)
  other arithmetic  17.3 us (10%)
  local copies, waits for them, and re-layouts  12 us (7%)
    pallas_call x4, Pallas kernels, exchange(): pl.pallas_call(functools.partial(_exchange_kernel, axis), out_shape=jax.S...  74.7 us
    all_to_all x1, waiting for transfers between devices, local(): lax.all_to_all(served, ('region', 'slab'), split_axis=0, concat_axis=0, t...  27.1 us
    all_to_all x1, starting transfers between devices, local(): lax.all_to_all(served, ('region', 'slab'), split_axis=0, concat_axis=0, t...  17.4 us
    pallas_call x2, Pallas kernels, pick_rows(): pl.pallas_call(_pick_kernel, out_shape=jax.ShapeDtypeStruct((count, width...  12.2 us
    pallas_call x1, Pallas kernels, cross_rows(): pl.pallas_call(_cross_kernel, out_shape=jax.ShapeDtypeStruct((rows, 2 * B...  10.4 us
    pallas_call x1, Pallas kernels, white_rows(): pl.pallas_call(_white_kernel, out_shape=jax.ShapeDtypeStruct((2 * SEG, ro...  8.34 us
    concatenate x1, other arithmetic, dft_table(): return jnp.concatenate([cos_part, -sin_part], axis=1).astype(jnp.bfloat16)  8.22 us
    another operation x3, local copies, waits for them, and re-layouts, pick_rows(): ids.reshape(count, 1)  5.51 us
  transfers between devices with their start and end apart: 1, of which 1 were waited for; matrix products, arithmetic and copies ran while one was open for 10% of the time, Pallas kernels for 30%

profile of v18, /device:TPU:1, one launch (start us, length us, event | category | flops | bytes accessed | tf_op | source)
XLA Modules:
  0.0 179.7 jit_solution(5468803351369307374)
XLA Ops:
  0.0 0.7 broadcast_multiply_fusion
  0.7 0.7 fusion.17
  1.4 0.2 reduce_window_sum.11
  1.6 0.8 select_reduce_fusion
  2.4 0.1 copy.17
  2.5 0.1 copy.16
  2.6 0.1 fusion.14
  2.8 1.1 scatter_custom_fusion
  3.9 0.7 broadcast_in_dim.7.x_ref
  4.6 17.4 %shard_map.46 = s32[32,8,128]{2,1,0:T(8,128)} custom-call(s32[32,8,128]{2,1,0:T(8,128)} %broadcast_in_dim.7.x_ref), custom_call_target="tpu_custom_call" | custom-call | bytes 131072 | tf_op jit(solution)/shard_map/pallas_call | solution.py:284
  22.0 0.9 slice.10
  22.9 0.1 copy.18
  23.0 0.1 copy.19
  23.1 0.1 reshape.119
  23.3 0.0 copy-start.2
  23.3 0.6 pad.13.x_ref
  23.9 17.1 %shard_map.47 = s32[16,8,128]{2,1,0:T(8,128)} custom-call(s32[16,8,128]{2,1,0:T(8,128)} %pad.13.x_ref), custom_call_target="tpu_custom_call" | custom-call | bytes 65536 | tf_op jit(solution)/shard_map/pallas_call | solution.py:284
  41.1 0.8 slice.11
  41.9 2.6 %copy.20.ids_ref = s32[8192,1]{1,0:T(8,128)} copy(s32[8192,1]{0,1:T(1,128)S(1)} %bitcast.21) | data formatting | bytes 65536 | tf_op jit(solution)/shard_map/reshape;reshape | solution.py:89
  44.5 7.5 %shard_map.48 = bf16[8192,128]{1,0:T(8,128)(2,1)} custom-call(s32[8192,1]{1,0:T(8,128)} %copy.20.ids_ref, bf16[1024,128]{1,0:T(8,128)(2,1)} %table_ref.3), custom_call_target="tpu_custom_call" | custom-call | flops 2147483648 | bytes 2359296 | tf_op jit(solution)/shard_map/pallas_call | solution.py:77
  52.0 17.4 %all-to-all-start = ((bf16[512,16,128]{2,1,0:T(8,128)(2,1)}), bf16[512,16,128]{2,1,0:T(8,128)(2,1)S(1)}, u32[]{:S(2)}, u32[]{:S(2)}) async-start(bf16[512,16,128]{2,1,0:T(8,128)(2,1)} %bitcast.18), calls=%async_computation | async-start | bytes 4194304 | tf_op jit(solution)/shard_map/all_to_all | solution.py:336
  69.4 0.0 copy-done.2
  69.4 0.7 broadcast_in_dim.8.x_ref
  70.1 15.3 %shard_map.49 = s32[32,8,128]{2,1,0:T(8,128)} custom-call(s32[32,8,128]{2,1,0:T(8,128)} %broadcast_in_dim.8.x_ref), custom_call_target="tpu_custom_call" | custom-call | bytes 131072 | tf_op jit(solution)/shard_map/pallas_call | solution.py:284
  85.4 0.9 slice_bitcast_fusion
  86.3 2.0 %copy.21.ids_ref = s32[4096,1]{1,0:T(8,128)} copy(s32[4096,1]{0,1:T(1,128)S(1)} %slice_bitcast_fusion) | data formatting | bytes 32768 | tf_op jit(solution)/shard_map/reshape;reshape;reshape | solution.py:89
  88.3 4.7 %shard_map.50 = bf16[4096,128]{1,0:T(8,128)(2,1)} custom-call(s32[4096,1]{1,0:T(8,128)} %copy.21.ids_ref, bf16[1024,128]{1,0:T(8,128)(2,1)} %table_ref.3), custom_call_target="tpu_custom_call" | custom-call | flops 1073741824 | bytes 1310720 | tf_op jit(solution)/shard_map/pallas_call | solution.py:77
  93.0 24.8 %shard_map.51.x_ref = bf16[32,128,128]{2,1,0:T(8,128)(2,1)} custom-call(bf16[32,128,128]{2,1,0:T(8,128)(2,1)} %bitcast.19), custom_call_target="tpu_custom_call" | custom-call | bytes 2097152 | tf_op jit(solution)/shard_map/pallas_call | solution.py:284
  117.9 0.1 multiply_subtract_fusion.taper_ref
  117.9 0.5 fusion.15
  118.5 1.0 fusion.9
  119.5 5.0 %subtract_convert_fusion = (bf16[32,64,1024]{2,1,0:T(8,128)(2,1)}, bf16[32,64,1024]{2,1,0:T(8,128)(2,1)}) fusion(f32[64,1024]{1,0:T(8,128)S(1)} %get-tuple-element.9, f32[32,1024]{1,0:T(8,128)S(1)} %get-tuple-element.11, f32[64,1024]{1,0:T(8,128)S(1)} %get-tuple-element.10, f32[32,1024]{1,0:T(8,128)S(1)} %get-tuple-element.12), kind=kLoop, calls=%fused_computation.3 | loop fusion | flops 18874368 | bytes 9175040 | tf_op jit(solution)/shard_map/convert.3
  124.5 0.0 copy-start
  124.5 8.2 %pad_maximum_fusion.table_ref.table_hbm = bf16[2048,2048]{1,0:T(8,128)(2,1)} fusion(bf16[2048,1024]{1,0:T(8,128)(2,1)} %bitcast.17, bf16[2048,1024]{1,0:T(8,128)(2,1)} %bitcast.16), kind=kLoop, calls=%fused_computation.1 | loop fusion | flops 16777216 | bytes 16777216 | tf_op jit(solution)/shard_map/concatenate | solution.py:29
  132.7 0.0 copy-done
  132.7 8.3 %shard_map.52.first_hbm = bf16[4,128,1024]{2,1,0:T(8,128)(2,1)S(1)} custom-call(bf16[32,128,128]{2,1,0:T(8,128)(2,1)S(1)} %copy-done, bf16[2048,2048]{1,0:T(8,128)(2,1)} %pad_maximum_fusion.table_ref.table_hbm, f32[16,128]{1,0:T(8,128)S(1)} %multiply_subtract_fusion.taper_ref), custom_call_target="tpu_custom_call" | custom-call | flops 2147483648 | bytes 10485760 | tf_op jit(solution)/shard_map/pallas_call | solution.py:206
  141.0 0.0 copy-start.1
  141.0 1.1 copy-done.1
  142.1 27.1 %all-to-all-done = bf16[512,16,128]{2,1,0:T(8,128)(2,1)S(1)} async-done(((bf16[512,16,128]{2,1,0:T(8,128)(2,1)}), bf16[512,16,128]{2,1,0:T(8,128)(2,1)S(1)}, u32[]{:S(2)}, u32[]{:S(2)}) %all-to-all-start) | async-done | bytes 2097184 | tf_op jit(solution)/shard_map/all_to_all | solution.py:336
  169.2 10.4 %shard_map.53 = bf16[128,2048]{1,0:T(8,128)(2,1)} custom-call(s32[128,1]{1,0:T(8,128)S(1)} %get-tuple-element.6.ids_ref, bf16[16,32,16,128]{3,2,1,0:T(8,128)(2,1)S(1)} %bitcast.15, bf16[4,128,1024]{2,1,0:T(8,128)(2,1)} %copy-done.1, bf16[2048,2048]{1,0:T(8,128)(2,1)} %pad_maximum_fusion.table_ref.table_hbm, f32[16,128]{1,0:T(8,128)S(1)} %multiply_subtract_fusion.taper_ref), custom_call_target="tpu_custom_call" | custom-call | flops 2147483648 | bytes 10485760 | tf_op jit(solution)/shard_map/pallas_call | solution.py:224
  (2 shorter events, 0.0 us)
Async XLA Ops:
  23.3 46.1 %copy-start.2 = (s32[128]{0:T(128)S(1)}, s32[128]{0:T(128)}, u32[]{:S(2)}) copy-start(s32[128]{0:T(128)} %param.5) | copy-start | bytes 1540
  52.0 117.2 %all-to-all-start = ((bf16[512,16,128]{2,1,0:T(8,128)(2,1)}), bf16[512,16,128]{2,1,0:T(8,128)(2,1)S(1)}, u32[]{:S(2)}, u32[]{:S(2)}) async-start(bf16[512,16,128]{2,1,0:T(8,128)(2,1)} %bitcast.18), calls=%async_computation | async-start | bytes 4194304 | tf_op jit(solution)/shard_map/all_to_all | solution.py:336
  124.5 8.2 %copy-start = (bf16[32,128,128]{2,1,0:T(8,128)(2,1)S(1)}, bf16[32,128,128]{2,1,0:T(8,128)(2,1)}, u32[]{:S(2)}) copy-start(bf16[32,128,128]{2,1,0:T(8,128)(2,1)} %shard_map.51.x_ref) | copy-start | bytes 3145732
  141.0 1.1 copy-start.1

commit v19 on v16

--- a/solution.py
+++ b/solution.py
@@ -322,7 +322,9 @@
     outgoing = jnp.pad(outgoing, ((0, 0), (0, (-outgoing.shape[1]) % 8), (0, 0)))
     asked = exchange(outgoing, "region", 1)[:, : slabs * capacity // 128].reshape(-1)
 
-    firsts = lax.all_gather(first_station, "slab", axis=0, tiled=False)
+    own_firsts = jnp.pad(first_station.reshape(-1, 128), ((0, (-(pair_count // 128)) % 8), (0, 0)))
+    firsts = exchange(jnp.broadcast_to(own_firsts[None], (slabs,) + own_firsts.shape), "slab", 3)
+    firsts = firsts[:, : pair_count // 128].reshape(slabs, pair_count)
     first_parts = pick_rows(records, firsts.reshape(-1)).reshape(slabs, pair_count, width)
     first_arrived = exchange(first_parts, "slab", 0)
     table = dft_table()

time: 181 us -> 181 us (level)
  blocking collectives: 22.1 us -> 0 us
  Pallas kernels: 94.7 us -> 109 us
  waiting for transfers between devices: 21 us -> 27.5 us
    all_gather x1 -> x0, blocking collectives: 22.1 us -> none  [local(): firsts = lax.all_gather(first_station, 'slab', axis=0, tiled=False)]
    pallas_call x3 -> x4, Pallas kernels: 60.6 us -> 74.6 us  [exchange(): pl.pallas_call(functools.partial(_exchange_kernel, axis), out_shape=jax.S...]
    all_to_all x1, waiting for transfers between devices: 21 us -> 27.5 us  [local(): lax.all_to_all(served, ('region', 'slab'), split_axis=0, concat_axis=0, t...]
  transfers between devices with their start and end apart: 1 -> 1, of which waited for: 1 -> 1; matrix products, arithmetic and copies ran while one was open for 9% -> 9% of each run, Pallas kernels for 22% -> 30%
where the time goes in v19:
time: 181 us; the launch traced here: 180 us
  Pallas kernels  109 us (60%)
  waiting for transfers between devices  27.5 us (15%)
  starting transfers between devices  17.4 us (10%)
  other arithmetic  17.3 us (10%)
  local copies, waits for them, and re-layouts  8.82 us (5%)
    pallas_call x4, Pallas kernels, exchange(): pl.pallas_call(functools.partial(_exchange_kernel, axis), out_shape=jax.S...  74.6 us
    all_to_all x1, waiting for transfers between devices, local(): lax.all_to_all(served, ('region', 'slab'), split_axis=0, concat_axis=0, t...  27.5 us
    all_to_all x1, starting transfers between devices, local(): lax.all_to_all(served, ('region', 'slab'), split_axis=0, concat_axis=0, t...  17.4 us
    pallas_call x2, Pallas kernels, pick_rows(): pl.pallas_call(_pick_kernel, out_shape=jax.ShapeDtypeStruct((count, width...  15.4 us
    pallas_call x1, Pallas kernels, cross_rows(): pl.pallas_call(_cross_kernel, out_shape=jax.ShapeDtypeStruct((rows, 2 * B...  10.4 us
    pallas_call x1, Pallas kernels, white_rows(): pl.pallas_call(_white_kernel, out_shape=jax.ShapeDtypeStruct((2 * SEG, ro...  8.34 us
    concatenate x1, other arithmetic, dft_table(): return jnp.concatenate([cos_part, -sin_part], axis=1).astype(jnp.bfloat16)  8.22 us
    another operation x1, other arithmetic  4.98 us
  transfers between devices with their start and end apart: 1, of which 1 were waited for; matrix products, arithmetic and copies ran while one was open for 9% of the time, Pallas kernels for 30%

profile of v19, /device:TPU:1, one launch (start us, length us, event | category | flops | bytes accessed | tf_op | source)
XLA Modules:
  0.0 180.1 jit_solution(17964357749863521517)
XLA Ops:
  0.0 0.0 copy-start.2
  0.0 0.7 broadcast_multiply_fusion
  0.7 0.7 fusion.17
  1.4 0.2 reduce_window_sum.11
  1.6 0.8 select_reduce_fusion
  2.4 0.1 copy.15
  2.5 0.1 copy.14
  2.7 0.1 fusion.14
  2.8 1.1 scatter_custom_fusion
  3.9 0.7 broadcast_in_dim.15.x_ref
  4.6 17.4 %shard_map.46 = s32[32,8,128]{2,1,0:T(8,128)} custom-call(s32[32,8,128]{2,1,0:T(8,128)} %broadcast_in_dim.15.x_ref), custom_call_target="tpu_custom_call" | custom-call | bytes 131072 | tf_op jit(solution)/shard_map/pallas_call | solution.py:284
  22.0 0.9 slice.10
  22.9 0.1 copy.16
  23.0 0.1 copy.17
  23.1 0.1 reshape.121
  23.3 0.6 pad.13.x_ref
  23.9 17.1 %shard_map.47 = s32[16,8,128]{2,1,0:T(8,128)} custom-call(s32[16,8,128]{2,1,0:T(8,128)} %pad.13.x_ref), custom_call_target="tpu_custom_call" | custom-call | bytes 65536 | tf_op jit(solution)/shard_map/pallas_call | solution.py:284
  41.1 0.8 slice.11
  41.9 0.7 broadcast_in_dim.17.ids_ref
  42.6 9.6 %shard_map.48 = bf16[8192,128]{1,0:T(8,128)(2,1)} custom-call(s32[8,8192]{1,0:T(8,128)} %broadcast_in_dim.17.ids_ref, bf16[1024,128]{1,0:T(8,128)(2,1)} %table_ref.3), custom_call_target="tpu_custom_call" | custom-call | flops 2147483648 | bytes 2359296 | tf_op jit(solution)/shard_map/pallas_call | solution.py:77
  52.3 17.4 %all-to-all-start = ((bf16[512,16,128]{2,1,0:T(8,128)(2,1)}), bf16[512,16,128]{2,1,0:T(8,128)(2,1)S(1)}, u32[]{:S(2)}, u32[]{:S(2)}) async-start(bf16[512,16,128]{2,1,0:T(8,128)(2,1)} %bitcast.17), calls=%async_computation | async-start | bytes 4194304 | tf_op jit(solution)/shard_map/all_to_all | solution.py:336
  69.7 0.0 copy-done.2
  69.7 0.7 broadcast_in_dim.18.x_ref
  70.4 15.3 %shard_map.49 = s32[32,8,128]{2,1,0:T(8,128)} custom-call(s32[32,8,128]{2,1,0:T(8,128)} %broadcast_in_dim.18.x_ref), custom_call_target="tpu_custom_call" | custom-call | bytes 131072 | tf_op jit(solution)/shard_map/pallas_call | solution.py:284
  85.7 0.9 slice.12
  86.6 0.7 broadcast_in_dim.20.ids_ref
  87.3 5.7 %shard_map.50 = bf16[4096,128]{1,0:T(8,128)(2,1)} custom-call(s32[8,4096]{1,0:T(8,128)} %broadcast_in_dim.20.ids_ref, bf16[1024,128]{1,0:T(8,128)(2,1)} %table_ref.3), custom_call_target="tpu_custom_call" | custom-call | flops 1073741824 | bytes 1310720 | tf_op jit(solution)/shard_map/pallas_call | solution.py:77
  93.0 24.7 %shard_map.51.x_ref = bf16[32,128,128]{2,1,0:T(8,128)(2,1)} custom-call(bf16[32,128,128]{2,1,0:T(8,128)(2,1)} %bitcast.18), custom_call_target="tpu_custom_call" | custom-call | bytes 2097152 | tf_op jit(solution)/shard_map/pallas_call | solution.py:284
  117.8 0.1 multiply_subtract_fusion.taper_ref
  117.8 0.5 fusion.15
  118.3 1.0 fusion.9
  119.4 5.0 %subtract_convert_fusion = (bf16[32,64,1024]{2,1,0:T(8,128)(2,1)}, bf16[32,64,1024]{2,1,0:T(8,128)(2,1)}) fusion(f32[64,1024]{1,0:T(8,128)S(1)} %get-tuple-element.9, f32[32,1024]{1,0:T(8,128)S(1)} %get-tuple-element.11, f32[64,1024]{1,0:T(8,128)S(1)} %get-tuple-element.10, f32[32,1024]{1,0:T(8,128)S(1)} %get-tuple-element.12), kind=kLoop, calls=%fused_computation.3 | loop fusion | flops 18874368 | bytes 9175040 | tf_op jit(solution)/shard_map/convert.3
  124.4 0.0 copy-start
  124.4 8.2 %pad_maximum_fusion.table_ref.table_hbm = bf16[2048,2048]{1,0:T(8,128)(2,1)} fusion(bf16[2048,1024]{1,0:T(8,128)(2,1)} %bitcast.16, bf16[2048,1024]{1,0:T(8,128)(2,1)} %bitcast.15), kind=kLoop, calls=%fused_computation.1 | loop fusion | flops 16777216 | bytes 16777216 | tf_op jit(solution)/shard_map/concatenate | solution.py:29
  132.6 0.0 copy-done
  132.6 8.3 %shard_map.52.first_hbm = bf16[4,128,1024]{2,1,0:T(8,128)(2,1)S(1)} custom-call(bf16[32,128,128]{2,1,0:T(8,128)(2,1)S(1)} %copy-done, bf16[2048,2048]{1,0:T(8,128)(2,1)} %pad_maximum_fusion.table_ref.table_hbm, f32[16,128]{1,0:T(8,128)S(1)} %multiply_subtract_fusion.taper_ref), custom_call_target="tpu_custom_call" | custom-call | flops 2147483648 | bytes 10485760 | tf_op jit(solution)/shard_map/pallas_call | solution.py:206
  140.9 0.0 copy-start.1
  140.9 1.1 copy-done.1
  142.0 27.5 %all-to-all-done = bf16[512,16,128]{2,1,0:T(8,128)(2,1)S(1)} async-done(((bf16[512,16,128]{2,1,0:T(8,128)(2,1)}), bf16[512,16,128]{2,1,0:T(8,128)(2,1)S(1)}, u32[]{:S(2)}, u32[]{:S(2)}) %all-to-all-start) | async-done | bytes 2097184 | tf_op jit(solution)/shard_map/all_to_all | solution.py:336
  169.5 10.4 %shard_map.53 = bf16[128,2048]{1,0:T(8,128)(2,1)} custom-call(s32[128,1]{1,0:T(8,128)S(1)} %get-tuple-element.6.ids_ref, bf16[16,32,16,128]{3,2,1,0:T(8,128)(2,1)S(1)} %bitcast.14, bf16[4,128,1024]{2,1,0:T(8,128)(2,1)} %copy-done.1, bf16[2048,2048]{1,0:T(8,128)(2,1)} %pad_maximum_fusion.table_ref.table_hbm, f32[16,128]{1,0:T(8,128)S(1)} %multiply_subtract_fusion.taper_ref), custom_call_target="tpu_custom_call" | custom-call | flops 2147483648 | bytes 10485760 | tf_op jit(solution)/shard_map/pallas_call | solution.py:224
  (2 shorter events, 0.0 us)
Async XLA Ops:
  0.0 69.7 %copy-start.2 = (s32[128]{0:T(128)S(1)}, s32[128]{0:T(128)}, u32[]{:S(2)}) copy-start(s32[128]{0:T(128)} %param.5) | copy-start | bytes 1540
  52.3 117.2 %all-to-all-start = ((bf16[512,16,128]{2,1,0:T(8,128)(2,1)}), bf16[512,16,128]{2,1,0:T(8,128)(2,1)S(1)}, u32[]{:S(2)}, u32[]{:S(2)}) async-start(bf16[512,16,128]{2,1,0:T(8,128)(2,1)} %bitcast.17), calls=%async_computation | async-start | bytes 4194304 | tf_op jit(solution)/shard_map/all_to_all | solution.py:336
  124.4 8.2 %copy-start = (bf16[32,128,128]{2,1,0:T(8,128)(2,1)S(1)}, bf16[32,128,128]{2,1,0:T(8,128)(2,1)}, u32[]{:S(2)}) copy-start(bf16[32,128,128]{2,1,0:T(8,128)(2,1)} %shard_map.51.x_ref) | copy-start | bytes 3145732
  140.9 1.1 copy-start.1

commit v20 on v15

--- a/solution.py
+++ b/solution.py
@@ -70,7 +70,7 @@
     out_ref[...] = jnp.dot(onehot, table_ref[...], preferred_element_type=jnp.float32).astype(out_ref.dtype)
 
 
-def pick_rows(table, ids, block=2048):
+def pick_rows(table, ids, block=4096):
     rows, width = table.shape
     count = ids.shape[0]
     block = min(block, count)

time: 181 us -> 181 us (level)
  no operation moved by 1% of the time
where the time goes in v20:
time: 181 us; the launch traced here: 180 us
  Pallas kernels  91.7 us (51%)
  blocking collectives  22.1 us (12%)
  waiting for transfers between devices  20.3 us (11%)
  other arithmetic  17.5 us (10%)
  starting transfers between devices  17.4 us (10%)
  local copies, waits for them, and re-layouts  10.4 us (6%)
    pallas_call x3, Pallas kernels, exchange(): pl.pallas_call(functools.partial(_exchange_kernel, axis), out_shape=jax.S...  60.5 us
    all_gather x1, blocking collectives, local(): firsts = lax.all_gather(first_station, 'slab', axis=0, tiled=False)  22.1 us
    all_to_all x1, waiting for transfers between devices, local(): lax.all_to_all(served, ('region', 'slab'), split_axis=0, concat_axis=0, t...  20.3 us
    all_to_all x1, starting transfers between devices, local(): lax.all_to_all(served, ('region', 'slab'), split_axis=0, concat_axis=0, t...  17.4 us
    pallas_call x2, Pallas kernels, pick_rows(): pl.pallas_call(_pick_kernel, out_shape=jax.ShapeDtypeStruct((count, width...  12.4 us
    pallas_call x1, Pallas kernels, cross_rows(): pl.pallas_call(_cross_kernel, out_shape=jax.ShapeDtypeStruct((rows, 2 * B...  10.4 us
    pallas_call x1, Pallas kernels, white_rows(): pl.pallas_call(_white_kernel, out_shape=jax.ShapeDtypeStruct((2 * SEG, ro...  8.34 us
    concatenate x1, other arithmetic, dft_table(): return jnp.concatenate([cos_part, -sin_part], axis=1).astype(jnp.bfloat16)  8.22 us
  transfers between devices with their start and end apart: 1, of which 1 were waited for; matrix products, arithmetic and copies ran while one was open for 9% of the time, Pallas kernels for 22%

profile of v20, /device:TPU:1, one launch (start us, length us, event | category | flops | bytes accessed | tf_op | source)
XLA Modules:
  0.0 179.8 jit_solution(7572583248274495121)
XLA Ops:
  0.0 0.7 broadcast_multiply_fusion
  0.7 0.7 fusion.17
  1.4 0.2 reduce_window_sum.11
  1.6 0.8 select_reduce_fusion
  2.4 0.1 copy.24
  2.5 0.1 copy.23
  2.6 0.1 fusion.14
  2.8 1.1 scatter_custom_fusion
  3.9 0.7 broadcast_in_dim.5.x_ref
  4.6 17.4 %shard_map.46 = s32[32,8,128]{2,1,0:T(8,128)} custom-call(s32[32,8,128]{2,1,0:T(8,128)} %broadcast_in_dim.5.x_ref), custom_call_target="tpu_custom_call" | custom-call | bytes 131072 | tf_op jit(solution)/shard_map/pallas_call | solution.py:284
  22.0 0.9 slice.7
  22.9 0.1 copy.25
  23.0 0.1 copy.26
  23.1 0.1 reshape.115
  23.3 0.0 copy-start.2
  23.3 0.6 pad.9.x_ref
  23.9 17.1 %shard_map.47 = s32[16,8,128]{2,1,0:T(8,128)} custom-call(s32[16,8,128]{2,1,0:T(8,128)} %pad.9.x_ref), custom_call_target="tpu_custom_call" | custom-call | bytes 65536 | tf_op jit(solution)/shard_map/pallas_call | solution.py:284
  41.1 0.8 slice.8
  41.9 2.6 %copy.27.ids_ref = s32[8192,1]{1,0:T(8,128)} copy(s32[8192,1]{0,1:T(1,128)S(1)} %bitcast.20) | data formatting | bytes 65536 | tf_op jit(solution)/shard_map/reshape;reshape | solution.py:89
  44.5 7.4 %shard_map.48 = bf16[8192,128]{1,0:T(8,128)(2,1)} custom-call(s32[8192,1]{1,0:T(8,128)} %copy.27.ids_ref, bf16[1024,128]{1,0:T(8,128)(2,1)} %table_ref.3), custom_call_target="tpu_custom_call" | custom-call | flops 2147483648 | bytes 2359296 | tf_op jit(solution)/shard_map/pallas_call | solution.py:77
  51.9 17.4 %all-to-all-start = ((bf16[512,16,128]{2,1,0:T(8,128)(2,1)}), bf16[512,16,128]{2,1,0:T(8,128)(2,1)S(1)}, u32[]{:S(2)}, u32[]{:S(2)}) async-start(bf16[512,16,128]{2,1,0:T(8,128)(2,1)} %bitcast.17), calls=%async_computation | async-start | bytes 4194304 | tf_op jit(solution)/shard_map/all_to_all | solution.py:334
  69.4 0.0 copy-done.2
  69.4 22.1 %all-gather.1 = s32[32,1,128]{2,1,0:T(1,128)S(1)} all-gather(s32[1,1,128]{2,1,0:T(1,128)S(1)} %bitcast.26), channel_id=2, replica_groups=mesh['region'=16,'slab'=32] {'slab'}, dimensions={0}, use_global_device_ids=true | all-gather | bytes 16896 | tf_op jit(solution)/shard_map/all_gather | solution.py:325
  91.4 2.0 %copy.28.ids_ref = s32[4096,1]{1,0:T(8,128)} copy(s32[4096,1]{0,1:T(1,128)S(1)} %bitcast.21) | data formatting | bytes 32768 | tf_op jit(solution)/shard_map/reshape;reshape | solution.py:89
  93.4 5.0 %shard_map.49 = bf16[4096,128]{1,0:T(8,128)(2,1)} custom-call(s32[4096,1]{1,0:T(8,128)} %copy.28.ids_ref, bf16[1024,128]{1,0:T(8,128)(2,1)} %table_ref.3), custom_call_target="tpu_custom_call" | custom-call | flops 1073741824 | bytes 1310720 | tf_op jit(solution)/shard_map/pallas_call | solution.py:77
  98.4 26.0 %shard_map.50.x_ref = bf16[32,128,128]{2,1,0:T(8,128)(2,1)} custom-call(bf16[32,128,128]{2,1,0:T(8,128)(2,1)} %bitcast.18), custom_call_target="tpu_custom_call" | custom-call | bytes 2097152 | tf_op jit(solution)/shard_map/pallas_call | solution.py:284
  124.4 0.1 multiply_subtract_fusion.taper_ref
  124.5 0.5 fusion.15
  125.0 1.0 fusion.9
  126.0 5.2 %subtract_convert_fusion = (bf16[32,64,1024]{2,1,0:T(8,128)(2,1)}, bf16[32,64,1024]{2,1,0:T(8,128)(2,1)}) fusion(f32[64,1024]{1,0:T(8,128)S(1)} %get-tuple-element.9, f32[32,1024]{1,0:T(8,128)S(1)} %get-tuple-element.11, f32[64,1024]{1,0:T(8,128)S(1)} %get-tuple-element.10, f32[32,1024]{1,0:T(8,128)S(1)} %get-tuple-element.12), kind=kLoop, calls=%fused_computation.3 | loop fusion | flops 18874368 | bytes 9175040 | tf_op jit(solution)/shard_map/convert.3
  131.2 0.0 copy-start
  131.2 8.2 %pad_maximum_fusion.table_ref.table_hbm = bf16[2048,2048]{1,0:T(8,128)(2,1)} fusion(bf16[2048,1024]{1,0:T(8,128)(2,1)} %bitcast.16, bf16[2048,1024]{1,0:T(8,128)(2,1)} %bitcast.15), kind=kLoop, calls=%fused_computation.1 | loop fusion | flops 16777216 | bytes 16777216 | tf_op jit(solution)/shard_map/concatenate | solution.py:29
  139.5 0.0 copy-done
  139.5 8.3 %shard_map.51.first_hbm = bf16[4,128,1024]{2,1,0:T(8,128)(2,1)S(1)} custom-call(bf16[32,128,128]{2,1,0:T(8,128)(2,1)S(1)} %copy-done, bf16[2048,2048]{1,0:T(8,128)(2,1)} %pad_maximum_fusion.table_ref.table_hbm, f32[16,128]{1,0:T(8,128)S(1)} %multiply_subtract_fusion.taper_ref), custom_call_target="tpu_custom_call" | custom-call | flops 2147483648 | bytes 10485760 | tf_op jit(solution)/shard_map/pallas_call | solution.py:206
  147.8 0.0 copy-start.1
  147.8 1.1 copy-done.1
  148.9 20.3 %all-to-all-done = bf16[512,16,128]{2,1,0:T(8,128)(2,1)S(1)} async-done(((bf16[512,16,128]{2,1,0:T(8,128)(2,1)}), bf16[512,16,128]{2,1,0:T(8,128)(2,1)S(1)}, u32[]{:S(2)}, u32[]{:S(2)}) %all-to-all-start) | async-done | bytes 2097184 | tf_op jit(solution)/shard_map/all_to_all | solution.py:334
  169.2 10.4 %shard_map.52 = bf16[128,2048]{1,0:T(8,128)(2,1)} custom-call(s32[128,1]{1,0:T(8,128)S(1)} %get-tuple-element.6.ids_ref, bf16[16,32,16,128]{3,2,1,0:T(8,128)(2,1)S(1)} %bitcast.14, bf16[4,128,1024]{2,1,0:T(8,128)(2,1)} %copy-done.1, bf16[2048,2048]{1,0:T(8,128)(2,1)} %pad_maximum_fusion.table_ref.table_hbm, f32[16,128]{1,0:T(8,128)S(1)} %multiply_subtract_fusion.taper_ref), custom_call_target="tpu_custom_call" | custom-call | flops 2147483648 | bytes 10485760 | tf_op jit(solution)/shard_map/pallas_call | solution.py:224
  (1 shorter events, 0.0 us)
Async XLA Ops:
  23.3 46.1 %copy-start.2 = (s32[128]{0:T(128)S(1)}, s32[128]{0:T(128)}, u32[]{:S(2)}) copy-start(s32[128]{0:T(128)} %param.5) | copy-start | bytes 1540
  51.9 117.2 %all-to-all-start = ((bf16[512,16,128]{2,1,0:T(8,128)(2,1)}), bf16[512,16,128]{2,1,0:T(8,128)(2,1)S(1)}, u32[]{:S(2)}, u32[]{:S(2)}) async-start(bf16[512,16,128]{2,1,0:T(8,128)(2,1)} %bitcast.17), calls=%async_computation | async-start | bytes 4194304 | tf_op jit(solution)/shard_map/all_to_all | solution.py:334
  131.2 8.2 %copy-start = (bf16[32,128,128]{2,1,0:T(8,128)(2,1)S(1)}, bf16[32,128,128]{2,1,0:T(8,128)(2,1)}, u32[]{:S(2)}) copy-start(bf16[32,128,128]{2,1,0:T(8,128)(2,1)} %shard_map.50.x_ref) | copy-start | bytes 3145732
  147.8 1.1 copy-start.1
